TPU v7x, 32 devices: a whole 2x2x4 slice. The times are simulated.
32 devices in a mesh: dp: 8 (over y, x, core), mp: 4 (over z).
Axes of the slice: x: 2, y: 2, z: 4, core: 2. Of those that a mesh axis runs over, the one named last changes fastest.
Arguments:
- tokens: bfloat16 [32, 512, 768], P('dp'), may hold values from -6 to 6
- doc_lengths: int32 [32, 4], P('dp'), may hold values from 1 to 256, 512 in all within a row
- w_query: bfloat16 [768, 768], P(None, 'mp'), may hold values from -0.21875 to 0.21875
- b_query: bfloat16 [768], P('mp'), may hold values from -3 to 3
- w_key: bfloat16 [768, 768], P(None, 'mp'), may hold values from -0.21875 to 0.21875
- w_value: bfloat16 [768, 768], P(None, 'mp'), may hold values from -0.21875 to 0.21875
- b_value: bfloat16 [768], P('mp'), may hold values from -3 to 3
- w_output: bfloat16 [768, 768], P('mp'), may hold values from -0.875 to 0.875
- b_output: bfloat16 [768], replicated, may hold values from -3 to 3
- gain_attn: bfloat16 [768], replicated, may hold values from 0.5 to 1.5
- shift_attn: bfloat16 [768], replicated, may hold values from -2 to 2
- w_expand: bfloat16 [768, 3072], P(None, 'mp'), may hold values from -0.21875 to 0.21875
- b_expand: bfloat16 [3072], P('mp'), may hold values from -3 to 3
- w_reduce: bfloat16 [3072, 768], P('mp'), may hold values from -0.21875 to 0.21875
- b_reduce: bfloat16 [768], replicated, may hold values from -2 to 2
- gain_ffn: bfloat16 [768], replicated, may hold values from 0.5 to 1.5
- shift_ffn: bfloat16 [768], replicated, may hold values from -2 to 2
- cotangent: bfloat16 [32, 512, 768], P('dp'), may hold values from -6 to 6
Outputs:
- output: bfloat16 [32, 512, 768], P('dp')
- grad_tokens: bfloat16 [32, 512, 768], P('dp')
- grad_w_query: float32 [768, 768], P(None, 'mp')
- grad_b_query: float32 [768], P('mp')
- grad_w_key: float32 [768, 768], P(None, 'mp')
- grad_w_value: float32 [768, 768], P(None, 'mp')
- grad_b_value: float32 [768], P('mp')
- grad_w_output: float32 [768, 768], P('mp')
- grad_b_output: float32 [768], replicated
- grad_gain_attn: float32 [768], replicated
- grad_shift_attn: float32 [768], replicated
- grad_w_expand: float32 [768, 3072], P(None, 'mp')
- grad_b_expand: float32 [3072], P('mp')
- grad_w_reduce: float32 [3072, 768], P('mp')
- grad_b_reduce: float32 [768], replicated
- grad_gain_ffn: float32 [768], replicated
- grad_shift_ffn: float32 [768], replicated
Inputs may be any that keep to these rules, and one draw needn't show every extreme that they name: `doc_lengths`: the 4 lengths of a row sum to 512, and the largest of every row is 256.
All inputs are finite; a program needn't handle non-finite values.
Results may differ from a plain program's by a relative error of at most 0.014.
Values sent between devices are 32-bit elements; how exact they have to be, the bound alone decides.
No kernel may reach another device: no remote copies, remote signals or barrier semaphores. Data moves between devices by JAX's collectives and lax.ppermute only.
A program may use at most 128 MiB of HBM per device.

v0:
```python
import jax
import jax.numpy as jnp
from jax import lax
from jax.experimental import pallas as pl
from jax.experimental.pallas import tpu as pltpu
from jax.sharding import PartitionSpec as P

HD = 64
GROUP = 8
EXTRA = 16
MASK = -float(2**30)
EPS = 1e-12
F32 = jnp.float32
BF16 = jnp.bfloat16
LIMIT = 60 << 20


def dot(left, right, left_dim, right_dim):
    return lax.dot_general(
        left, right, (((left_dim,), (right_dim,)), ((), ())), preferred_element_type=F32
    )


def params():
    return pltpu.CompilerParams(vmem_limit_bytes=LIMIT)


def cost(flops, moved):
    return pl.CostEstimate(flops=int(flops), bytes_accessed=int(moved), transcendentals=0)


def whole(shape):
    zeros = (0,) * len(shape)
    return pl.BlockSpec(shape, lambda *_: zeros, pipeline_mode=pl.Buffered(1))


def split3(row):
    high = row.astype(BF16).astype(F32)
    rest = row - high
    mid = rest.astype(BF16).astype(F32)
    return high, mid, rest - mid


def rows_of(height, first, parts, width):
    place = lax.broadcasted_iota(jnp.int32, (height, width), 0)
    out = jnp.zeros((height, width), F32)
    for i, part in enumerate(parts):
        out = jnp.where(place == first + i, part, out)
    return out


def put(out_ref, start, values, step):
    rows = pl.ds(pl.multiple_of(start, step), values.shape[0])
    out_ref[rows, :] = values.astype(out_ref.dtype)


def peer_shard(place_ref, shards, k):
    return lax.rem(place_ref[GROUP] + shards - k, shards)


def own_block(*shape):
    return pl.BlockSpec(shape, lambda i, p: (p[GROUP],) + (0,) * (len(shape) - 2) + (i,))


def peer_block(peers, first, *shape):
    middle = (0,) * (len(shape) - 2)
    return pl.BlockSpec(
        shape, lambda k, i, p: (lax.rem(p[GROUP] + peers - first - k, peers),) + middle + (i,)
    )


ANY = pl.BlockSpec(memory_space=pl.ANY)


def shift_matrix(amount, length, forward):
    row = lax.broadcasted_iota(jnp.int32, (length, length), 0)
    column = lax.broadcasted_iota(jnp.int32, (length, length), 1)
    apart = column - row if forward else row - column
    return jnp.where((apart == amount) | (apart == amount - length), 1.0, 0.0).astype(BF16)


def shift_kernel(place_ref, first_ref, second_ref, first_out, second_out):
    length = first_ref.shape[0]
    amount = place_ref[GROUP + 1 + pl.program_id(0)]
    matrix = shift_matrix(amount, length, True)
    first_out[...] = dot(matrix, first_ref[...], 1, 0).astype(BF16)
    second_out[...] = dot(matrix, second_ref[...], 1, 0).astype(BF16)


def shift(place, length, first, second):
    tokens, width = first.shape
    by_row = lambda: pl.BlockSpec((length, width), lambda i, *_: (i, 0))
    return pl.pallas_call(
        shift_kernel,
        grid_spec=pltpu.PrefetchScalarGridSpec(
            num_scalar_prefetch=1,
            grid=(tokens // length,),
            in_specs=[by_row(), by_row()],
            out_specs=[by_row(), by_row()],
        ),
        out_shape=[jax.ShapeDtypeStruct((tokens, width), BF16)] * 2,
        compiler_params=params(),
        cost_estimate=cost(4 * tokens * length * width, 12e6),
        name="shift",
    )(place, first, second)


def unshift_kernel(place_ref, in_ref, out_ref):
    length = in_ref.shape[0]
    matrix = shift_matrix(place_ref[GROUP + 1 + pl.program_id(0)], length, False)
    out_ref[...] = dot(matrix, in_ref[...], 1, 0).astype(BF16)


def unshift(place, length, shifted):
    tokens, width = shifted.shape
    by_row = lambda: pl.BlockSpec((length, width), lambda i, *_: (i, 0))
    return pl.pallas_call(
        unshift_kernel,
        grid_spec=pltpu.PrefetchScalarGridSpec(
            num_scalar_prefetch=1,
            grid=(tokens // length,),
            in_specs=[by_row()],
            out_specs=by_row(),
        ),
        out_shape=jax.ShapeDtypeStruct((tokens, width), BF16),
        compiler_params=params(),
        cost_estimate=cost(2 * tokens * length * width, 6e6),
        name="unshift",
    )(place, shifted)


def tiles(heads, block):
    return [(h, slice(i * block, (i + 1) * block)) for h in range(heads) for i in range(2)]


def attend_rows(x_ref, bias_ref, qf_ref, kf_ref, w_scr, qkv_ref, ctx_ref, aug_ref):
    heads = ctx_ref.shape[0]
    length = x_ref.shape[0]
    block = length // 2
    span = 3 * HD
    proj = dot(w_scr[...], x_ref[...], 1, 1)
    scale = HD ** (-0.5)
    column = bias_ref[...].T[:, 0:1]
    for h in range(heads):
        part = proj[h * span : (h + 1) * span]
        queries = part[:HD] + column[h * HD : (h + 1) * HD]
        values = part[2 * HD :] + column[(heads + h) * HD : (heads + h + 1) * HD]
        qkv_ref[h, :HD, :] = (queries * scale).astype(BF16)
        qkv_ref[h, HD : 2 * HD, :] = part[HD : 2 * HD].astype(BF16)
        qkv_ref[h, 2 * HD :, :] = values.astype(BF16)
    ones_rows = rows_of(EXTRA, 0, (jnp.ones((1, block), F32),), block).astype(BF16)
    items = tiles(heads, block)
    scores = []
    for h, at in items:
        queries = jnp.concatenate([qkv_ref[h, :HD, at], qf_ref[:, at]], axis=0)
        keys = jnp.concatenate([qkv_ref[h, HD : 2 * HD, at], kf_ref[:, at]], axis=0)
        scores.append(dot(keys, queries, 0, 0))
    highest = [jnp.max(part, axis=0, keepdims=True) for part in scores]
    weight = [jnp.exp(part - top).astype(BF16) for part, top in zip(scores, highest)]
    context = []
    for (h, at), part in zip(items, weight):
        values = jnp.concatenate([qkv_ref[h, 2 * HD :, at], ones_rows], axis=0)
        context.append(dot(values, part, 1, 0))
    for (h, at), part, top in zip(items, context, highest):
        total = part[HD : HD + 1]
        ctx_ref[h, :, at] = (part[:HD] * (1.0 / total)).astype(BF16)
        log_total = top + jnp.log(total)
        extra = rows_of(EXTRA, 4, split3(-log_total), block)
        aug_ref[h, :, at] = (extra + qf_ref[:, at].astype(F32)).astype(BF16)


def attend_own_kernel(place_ref, x_ref, bias_ref, qf_ref, kf_ref, own_ref, *refs):
    w_ref, wo_ref, qkv_ref, ctx_ref, aug_ref = refs
    height = w_ref.shape[0]

    @pl.when(pl.program_id(0) == 0)
    def _():
        w_ref[...] = own_ref[:height, :]
        wo_ref[...] = own_ref[height:, :]

    attend_rows(x_ref, bias_ref, qf_ref, kf_ref, w_ref, qkv_ref, ctx_ref, aug_ref)


def attend_own(length, peers, place, inputs, bias, qf, kf, own):
    heads = own.shape[0] // (4 * HD)
    tokens, width = inputs.shape
    every = peers * heads
    shapes = [(every * 3 * HD, width), (every * HD, width)]
    shapes += [(every, n, tokens) for n in (3 * HD, HD, EXTRA)]
    by_row = pl.BlockSpec((EXTRA, length), lambda i, *_: (0, i))
    return pl.pallas_call(
        attend_own_kernel,
        grid_spec=pltpu.PrefetchScalarGridSpec(
            num_scalar_prefetch=1,
            grid=(tokens // length,),
            in_specs=[
                pl.BlockSpec((length, width), lambda i, *_: (i, 0)),
                whole(bias.shape),
                by_row,
                by_row,
                whole(own.shape),
            ],
            out_specs=[
                pl.BlockSpec((heads * 3 * HD, width), lambda i, p: (p[GROUP], 0)),
                pl.BlockSpec((heads * HD, width), lambda i, p: (p[GROUP], 0)),
                *[own_block(heads, n, length) for n in (3 * HD, HD, EXTRA)],
            ],
        ),
        out_shape=[jax.ShapeDtypeStruct(shape, BF16) for shape in shapes],
        compiler_params=params(),
        cost_estimate=cost(heads * tokens * (6 * HD * width + 16 * 64 * length), 12e6),
        name="attend_own",
    )(place, inputs, bias, qf, kf, own)


def attend_peers_kernel(spots, place_ref, x_ref, bias_ref, qf_ref, kf_ref, *refs):
    count = len(spots)
    parts = refs[:count]
    w_ref, wo_ref, qkv_ref, ctx_ref, aug_ref, w_scr = refs[count + 5 :]
    height = w_ref.shape[0]

    @pl.when(pl.program_id(1) == 0)
    def _():
        size = w_scr.shape[0] // GROUP
        for ref, (index, offset) in zip(parts, spots):
            put(w_scr, place_ref[index] * size + offset, ref[0], 16)
        w_ref[...] = w_scr[:height, :]
        wo_ref[...] = w_scr[height:, :]

    attend_rows(x_ref, bias_ref.at[0], qf_ref, kf_ref, w_ref, qkv_ref, ctx_ref, aug_ref)


def attend_peers(length, peers, place, inputs, bias, qf, kf, pieces, arrays):
    heads = arrays[2].shape[0] // peers
    tokens, width = inputs.shape
    spots = [(index, offset) for _, index, offset in pieces]
    parts = [array for array, _, _ in pieces]
    by_row = pl.BlockSpec((EXTRA, length), lambda k, i, *_: (0, i))
    return pl.pallas_call(
        lambda *refs: attend_peers_kernel(spots, *refs),
        grid_spec=pltpu.PrefetchScalarGridSpec(
            num_scalar_prefetch=1,
            grid=(peers - 1, tokens // length),
            in_specs=[
                pl.BlockSpec((length, width), lambda k, i, *_: (i, 0)),
                pl.BlockSpec((1,) + bias.shape[1:], lambda k, i, *_: (k, 0, 0)),
                by_row,
                by_row,
                *[
                    pl.BlockSpec((1,) + a.shape[1:], lambda k, i, *_: (k, 0, 0)) for a in parts
                ],
                *[ANY] * 5,
            ],
            out_specs=[
                *[
                    pl.BlockSpec(
                        (heads * n, width),
                        lambda k, i, p: (lax.rem(p[GROUP] + peers - 1 - k, peers), 0),
                    )
                    for n in (3 * HD, HD)
                ],
                *[peer_block(peers, 1, heads, n, length) for n in (3 * HD, HD, EXTRA)],
            ],
            scratch_shapes=[pltpu.VMEM((heads * 4 * HD, width), BF16)],
        ),
        out_shape=[jax.ShapeDtypeStruct(a.shape, a.dtype) for a in arrays],
        input_output_aliases={5 + len(parts) + i: i for i in range(5)},
        compiler_params=params(),
        cost_estimate=cost(
            (peers - 1) * heads * tokens * (6 * HD * width + 16 * 64 * length), 30e6
        ),
        name="attend_peers",
    )(place, inputs, bias, qf, kf, *parts, *arrays)


def attend_back_rows(qkv_ref, ctx_ref, aug_ref, grad_ref, kf_ref, out_ref):
    heads, _, length = ctx_ref.shape
    block = length // 2
    scale = HD ** (-0.5)
    one = jnp.ones((1, block), F32)
    ones_rows = rows_of(EXTRA, 0, (one, one, one), block).astype(BF16)
    items = tiles(heads, block)
    scores, spreads = [], []
    for h, at in items:
        scores.append(
            dot(
                jnp.concatenate([qkv_ref[h, HD : 2 * HD, at], kf_ref[:, at]], axis=0),
                jnp.concatenate([qkv_ref[h, :HD, at], aug_ref[h, :, at]], axis=0),
                0,
                0,
            )
        )
    for h, at in items:
        grad = grad_ref[h, :, at]
        inner = jnp.sum(grad.astype(F32) * ctx_ref[h, :, at].astype(F32), axis=0, keepdims=True)
        grad_extra = rows_of(EXTRA, 0, split3(-inner), block).astype(BF16)
        spreads.append(
            dot(
                jnp.concatenate([qkv_ref[h, 2 * HD :, at], ones_rows], axis=0),
                jnp.concatenate([grad, grad_extra], axis=0),
                0,
                0,
            )
        )
    probs = [jnp.exp(part) for part in scores]
    slopes = [(part * spread).astype(BF16) for part, spread in zip(probs, spreads)]
    probs = [part.astype(BF16) for part in probs]
    for (h, at), part in zip(items, probs):
        out_ref[h, 2 * HD :, at] = dot(grad_ref[h, :, at], part, 1, 1).astype(BF16)
    for (h, at), part in zip(items, slopes):
        out_ref[h, HD : 2 * HD, at] = dot(qkv_ref[h, :HD, at], part, 1, 1).astype(BF16)
    for (h, at), part in zip(items, slopes):
        grad = dot(qkv_ref[h, HD : 2 * HD, at], part, 1, 0)
        out_ref[h, :HD, at] = (grad * scale).astype(BF16)


def attend_back_own_kernel(place_ref, qkv_ref, ctx_ref, aug_ref, grad_ref, kf_ref, *refs):
    x_ref, dwo_ref, small_ref, early_ref, out_ref, mine_ref, send_ref, grad_scr, sum_scr = refs
    heads = ctx_ref.shape[0]
    height = heads * HD
    step = pl.program_id(0)

    @pl.when(step == 0)
    def _():
        grad_scr[...] = jnp.zeros_like(grad_scr)
        sum_scr[...] = jnp.zeros_like(sum_scr)

    attend_back_rows(qkv_ref, ctx_ref, aug_ref, grad_ref, kf_ref, out_ref)
    ones = jnp.ones((8, x_ref.shape[0]), BF16)
    row = lax.broadcasted_iota(jnp.int32, (8, 3 * HD), 0)
    sums = jnp.zeros((8, 3 * HD), F32)
    for h in range(heads):
        grad = dot(out_ref[h], x_ref[...], 1, 0)
        for i in range(3):
            grad_scr[i * height + h * HD : i * height + (h + 1) * HD, :] += grad[
                i * HD : (i + 1) * HD
            ]
        sums = jnp.where(row == 3 + h, dot(ones, out_ref[h], 1, 1), sums)
    sum_scr[:, : 3 * HD] += sums

    @pl.when(step == pl.num_programs(0) - 1)
    def _():
        size, size_two = 3 * height // GROUP, height // GROUP
        top = size + size_two
        for rel in range(4):
            for source, ref in enumerate((mine_ref, send_ref)):
                owner = place_ref[2 * rel + source]
                ref[rel, :size, :] = grad_scr[pl.ds(pl.multiple_of(owner * size, 8), size), :]
                start = pl.multiple_of(owner * size_two, 8)
                ref[rel, size:top, :] = dwo_ref[pl.ds(start, size_two), :]
                ref[rel, top : top + 8, :] = jnp.where(
                    owner == 0, small_ref[...] + sum_scr[...], 0.0
                )
                ref[rel, top + 8 :, :] = jnp.where(owner == 0, early_ref[...], 0.0)


def attend_back_own(length, place, qkv, ctx, aug, grad, kf, inputs, dwo, small, early):
    height, width = dwo.shape
    heads = height // HD
    tokens = inputs.shape[0]
    share = 4 * height // GROUP + 16
    return pl.pallas_call(
        attend_back_own_kernel,
        grid_spec=pltpu.PrefetchScalarGridSpec(
            num_scalar_prefetch=1,
            grid=(tokens // length,),
            in_specs=[
                own_block(heads, 3 * HD, length),
                own_block(heads, HD, length),
                own_block(heads, EXTRA, length),
                own_block(heads, HD, length),
                pl.BlockSpec((EXTRA, length), lambda i, *_: (0, i)),
                pl.BlockSpec((length, width), lambda i, *_: (i, 0)),
                whole(dwo.shape),
                whole(small.shape),
                whole(early.shape),
            ],
            out_specs=[
                own_block(heads, 3 * HD, length),
                whole((4, share, width)),
                whole((4, share, width)),
            ],
            scratch_shapes=[pltpu.VMEM((3 * height, width), F32), pltpu.VMEM((8, width), F32)],
        ),
        out_shape=[jax.ShapeDtypeStruct(qkv.shape, BF16)]
        + [jax.ShapeDtypeStruct((4, share, width), F32)] * 2,
        compiler_params=params(),
        cost_estimate=cost(heads * tokens * (20 * 64 * length + 6 * HD * width), 12e6),
        name="attend_back_own",
    )(place, qkv, ctx, aug, grad, kf, inputs, dwo, small, early)


def attend_back_kernel(place_ref, qkv_ref, ctx_ref, aug_ref, grad_ref, kf_ref, old_ref, out_ref):
    attend_back_rows(qkv_ref, ctx_ref, aug_ref, grad_ref, kf_ref, out_ref)


def attend_back(length, peers, first, count, place, qkv, ctx, aug, grad, kf, out):
    every, _, tokens = qkv.shape
    heads = every // peers
    by_peer = lambda n: peer_block(peers, first, heads, n, length)
    return pl.pallas_call(
        attend_back_kernel,
        grid_spec=pltpu.PrefetchScalarGridSpec(
            num_scalar_prefetch=1,
            grid=(count, tokens // length),
            in_specs=[
                by_peer(3 * HD),
                by_peer(HD),
                by_peer(EXTRA),
                by_peer(HD),
                pl.BlockSpec((EXTRA, length), lambda k, i, *_: (0, i)),
                ANY,
            ],
            out_specs=by_peer(3 * HD),
        ),
        out_shape=jax.ShapeDtypeStruct(out.shape, BF16),
        input_output_aliases={6: 0},
        compiler_params=params(),
        cost_estimate=cost(count * heads * tokens * 20 * 64 * length, 12e6),
        name="attend_back",
    )(place, qkv, ctx, aug, grad, kf, out)


def norm_forward(hidden):
    center = hidden - jnp.mean(hidden, axis=-1, keepdims=True)
    inverse = lax.rsqrt(jnp.mean(center * center, axis=-1, keepdims=True) + EPS)
    return center * inverse, inverse


def norm_backward(grad, gain, norm, inverse):
    scaled = grad * gain
    first = jnp.mean(scaled, axis=-1, keepdims=True)
    second = jnp.mean(scaled * norm, axis=-1, keepdims=True)
    return (scaled - first - norm * second) * inverse


def column_sum(values):
    return jnp.sum(values, axis=0, keepdims=True)


def flat(values):
    return values.reshape(-1, values.shape[-1])


def attended_kernel(x_ref, ctx_ref, wo_ref, vec_ref, sum_ref, low_ref):
    b_output, gain_one, shift_one = vec_ref[0:1], vec_ref[1:2], vec_ref[2:3]
    half = x_ref.shape[0] // 2
    halves = [slice(0, half), slice(half, 2 * half)]
    attended = [dot(flat(ctx_ref[:, :, at]), wo_ref[...], 0, 0) for at in halves]
    for at, part in zip(halves, attended):
        residual = x_ref[at, :].astype(F32) + (part + b_output)
        sum_ref[at, :] = residual
        norm_one, _ = norm_forward(residual)
        low_ref[at, :] = (norm_one * gain_one + shift_one).astype(BF16)


def add_attended(inputs, ctx, w_output, vectors):
    tokens, width = inputs.shape
    every = ctx.shape[0]
    block = 512
    by_token = lambda: pl.BlockSpec((block, width), lambda i: (i, 0))
    return pl.pallas_call(
        attended_kernel,
        grid=(tokens // block,),
        in_specs=[
            by_token(),
            pl.BlockSpec((every, HD, block), lambda i: (0, 0, i)),
            whole(w_output.shape),
            whole(vectors.shape),
        ],
        out_specs=[by_token(), by_token()],
        out_shape=[
            jax.ShapeDtypeStruct((tokens, width), F32),
            jax.ShapeDtypeStruct((tokens, width), BF16),
        ],
        compiler_params=params(),
        cost_estimate=cost(2 * tokens * width * every * HD, 17e6),
        name="add_attended",
    )(inputs, ctx, w_output, vectors)


def fill(place_ref, own_ref, parts, spots, out_ref):
    shards, height, _ = out_ref.shape
    out_ref[place_ref[GROUP]] = own_ref[...]
    for k in range(1, shards):
        shard = peer_shard(place_ref, shards, k)
        for ref, (index, offset) in zip(parts, spots):
            start = place_ref[index] * (height // GROUP) + offset
            put(out_ref.at[shard], start, ref[k - 1], 16)


def expand_kernel(spots, place_ref, low_ref, bias_ref, own_ref, *refs):
    parts, (act_ref, slope_ref, full_ref, we_ref, sem) = refs[: len(spots)], refs[len(spots) :]
    shards = we_ref.shape[0]
    kept = pltpu.make_async_copy(we_ref, full_ref, sem)

    @pl.when(pl.program_id(0) == 0)
    def _():
        fill(place_ref, own_ref, parts, spots, we_ref)
        kept.start()

    @pl.when(pl.program_id(0) == pl.num_programs(0) - 1)
    def _():
        kept.wait()

    half = low_ref.shape[0] // 2
    halves = [slice(0, half), slice(half, 2 * half)]
    def shard(s, carry):
        bias = bias_ref[peer_shard(place_ref, shards, s), 1:2]
        products = [dot(low_ref[at, :], we_ref[s], 1, 0) for at in halves]
        for at, product in zip(halves, products):
            hidden = product + bias
            square = hidden * hidden
            bent = jnp.tanh(hidden * (0.7978845608028654 + 0.035677408136300125 * square))
            gate = 0.5 + 0.5 * bent
            active = hidden * gate
            act_ref[s, at, :] = active.astype(BF16)
            slope = gate + (active * (1.0 - gate)) * (
                1.5957691216057308 + 0.21406444881780075 * square
            )
            slope_ref[s, at, :] = slope.astype(BF16)
        return carry

    lax.fori_loop(0, shards, shard, 0)


def expand(place, low, biases, own, pieces, shards):
    tokens, width = low.shape
    hidden = own.shape[1]
    block = 512
    spots = [(index, offset) for _, index, offset in pieces]
    parts = [array for array, _, _ in pieces]
    full = (shards, width, hidden)
    by_shard = lambda: pl.BlockSpec((shards, block, hidden), lambda i, *_: (0, i, 0))
    return pl.pallas_call(
        lambda *refs: expand_kernel(spots, *refs),
        grid_spec=pltpu.PrefetchScalarGridSpec(
            num_scalar_prefetch=1,
            grid=(tokens // block,),
            in_specs=[
                pl.BlockSpec((block, width), lambda i, *_: (i, 0)),
                whole(biases.shape),
                whole(own.shape),
                *[whole(a.shape) for a in parts],
            ],
            out_specs=[by_shard(), by_shard(), ANY],
            scratch_shapes=[pltpu.VMEM(full, BF16), pltpu.SemaphoreType.DMA],
        ),
        out_shape=[
            jax.ShapeDtypeStruct((shards, tokens, hidden), BF16),
            jax.ShapeDtypeStruct((shards, tokens, hidden), BF16),
            jax.ShapeDtypeStruct(full, BF16),
        ],
        compiler_params=params(),
        cost_estimate=cost(2 * tokens * width * shards * hidden, 40e6),
        name="expand",
    )(place, low, biases, own, *parts)


def reduce_kernel(spots, place_ref, sum_ref, cot_ref, act_ref, slope_ref, vec_ref, *refs):
    own_ref, refs = refs[0], refs[1:]
    piece_refs, refs = refs[: len(spots)], refs[len(spots) :]
    out_ref, g2_ref, full_ref, mine_ref, send_ref, small_scr = refs[:6]
    dwe_scr, dwr_scr, wr_ref, sems = refs[6:]
    kept = pltpu.make_async_copy(wr_ref, full_ref, sems.at[0])
    step = pl.program_id(0)
    shards = act_ref.shape[0]
    me = place_ref[GROUP]

    @pl.when(step == 0)
    def _():
        fill(place_ref, own_ref, piece_refs, spots, wr_ref)
        kept.start()
        for scr in (dwe_scr, dwr_scr, small_scr):
            scr[...] = jnp.zeros_like(scr)

    gain_one, shift_one = vec_ref[1:2], vec_ref[2:3]
    b_reduce, gain_two, shift_two = vec_ref[3:4], vec_ref[4:5], vec_ref[5:6]
    half = sum_ref.shape[0] // 2
    halves = [slice(0, half), slice(half, 2 * half)]
    mixed = []
    for at in halves:
        part = dot(act_ref[0, at, :], wr_ref[0], 1, 0)
        for s in range(1, shards):
            part = part + dot(act_ref[s, at, :], wr_ref[s], 1, 0)
        mixed.append(part)
    small = [jnp.zeros((1, sum_ref.shape[1]), F32)] * 4
    low, normed_low, active = [], [], []
    for at, part in zip(halves, mixed):
        norm_one, _ = norm_forward(sum_ref[at, :])
        normed = norm_one * gain_one + shift_one
        normed_low.append(normed.astype(BF16))
        norm_two, inverse_two = norm_forward(normed + (part + b_reduce))
        out_ref[at, :] = (norm_two * gain_two + shift_two).astype(BF16)
        cot = cot_ref[at, :].astype(F32)
        grad_two = norm_backward(cot, gain_two, norm_two, inverse_two)
        g2_ref[at, :] = grad_two
        low.append(grad_two.astype(BF16))
        active.append(dot(low[-1], own_ref[...], 1, 1))
        small[0] = small[0] + column_sum(grad_two)
        small[1] = small[1] + column_sum(cot * norm_two)
        small[2] = small[2] + column_sum(cot)
    dwr_scr[...] += dot(act_ref[me], jnp.concatenate(low, axis=0), 0, 0)
    own = []
    for at, part in zip(halves, active):
        own.append((part * slope_ref[0, at, :].astype(F32)).astype(BF16))
        small[3] = small[3] + column_sum(own[-1].astype(F32))
    dwe_scr[...] += dot(
        jnp.concatenate(normed_low, axis=0), jnp.concatenate(own, axis=0), 0, 0
    )
    for n, part in enumerate(small):
        small_scr[n : n + 1] += part

    @pl.when(step == pl.num_programs(0) - 1)
    def _():
        copies = [kept]
        for plane in range(4):
            for ref, core in ((send_ref, place_ref[1]), (mine_ref, place_ref[0])):
                owner = 2 * plane + lax.rem(core, 2)
                top = 0
                for scr in (dwe_scr, dwr_scr):
                    size = scr.shape[0] // GROUP
                    start = pl.multiple_of(owner * size, 8)
                    copy = pltpu.make_async_copy(
                        scr.at[pl.ds(start, size), :],
                        ref.at[plane, top : top + size, :],
                        sems.at[len(copies)],
                    )
                    copy.start()
                    copies.append(copy)
                    top += size
        for copy in copies:
            copy.wait()


def reduce(place, residual, cot, act, slope, vectors, own, pieces):
    tokens, width = residual.shape
    shards, _, hidden = act.shape
    block = 512
    share = (width + hidden) // GROUP
    spots = [(index, offset) for _, index, offset in pieces]
    arrays = [array for array, _, _ in pieces]
    by_token = lambda: pl.BlockSpec((block, width), lambda i, *_: (i, 0))
    return pl.pallas_call(
        lambda *refs: reduce_kernel(spots, *refs),
        grid_spec=pltpu.PrefetchScalarGridSpec(
            num_scalar_prefetch=1,
            grid=(tokens // block,),
            in_specs=[
                by_token(),
                by_token(),
                pl.BlockSpec((shards, block, hidden), lambda i, *_: (0, i, 0)),
                pl.BlockSpec((1, block, hidden), lambda i, p: (p[GROUP], i, 0)),
                whole(vectors.shape),
                whole(own.shape),
                *[whole(a.shape) for a in arrays],
            ],
            out_specs=[
                by_token(),
                by_token(),
                ANY,
                ANY,
                ANY,
                whole((8, width)),
            ],
            scratch_shapes=[
                pltpu.VMEM((width, hidden), F32),
                pltpu.VMEM((hidden, width), F32),
                pltpu.VMEM((shards, hidden, width), BF16),
                pltpu.SemaphoreType.DMA((17,)),
            ],
        ),
        out_shape=[
            jax.ShapeDtypeStruct((tokens, width), BF16),
            jax.ShapeDtypeStruct((tokens, width), F32),
            jax.ShapeDtypeStruct((shards, hidden, width), BF16),
            jax.ShapeDtypeStruct((4, share, width), F32),
            jax.ShapeDtypeStruct((4, share, width), F32),
            jax.ShapeDtypeStruct((8, width), F32),
        ],
        compiler_params=params(),
        cost_estimate=cost(tokens * width * hidden * (2 * shards + 6), 40e6),
        name="reduce",
    )(place, residual, cot, act, slope, vectors, own, *arrays)


def return_kernel(place_ref, sum_ref, g2_ref, slope_ref, ctx_ref, we_ref, wr_ref, w_ref, *refs):
    vec_ref, g1_ref, dctx_ref, dwo_ref, small_ref = refs
    shards = we_ref.shape[0]

    @pl.when(pl.program_id(0) == 0)
    def _():
        dwo_ref[...] = jnp.zeros_like(dwo_ref)
        small_ref[...] = jnp.zeros_like(small_ref)

    half = sum_ref.shape[0] // 2
    halves = [slice(0, half), slice(half, 2 * half)]
    gain_one = vec_ref[1:2]
    low = [g2_ref[at, :].astype(BF16) for at in halves]
    items = [(s, i) for s in range(shards) for i in range(2)]
    total = [g2_ref[at, :] for at in halves]
    ahead = dot(low[0], wr_ref[0], 1, 1)
    for n, (s, i) in enumerate(items):
        grad_active = ahead
        if n + 1 < len(items):
            s_next, i_next = items[n + 1]
            ahead = dot(low[i_next], wr_ref[s_next], 1, 1)
        grad_hidden = (grad_active * slope_ref[s, halves[i], :].astype(F32)).astype(BF16)
        total[i] = total[i] + dot(grad_hidden, we_ref[s], 1, 1)
    small = [jnp.zeros((1, sum_ref.shape[1]), F32)] * 3
    one = []
    for at, grad_normed in zip(halves, total):
        norm_one, inverse_one = norm_forward(sum_ref[at, :])
        grad_one = norm_backward(grad_normed, gain_one, norm_one, inverse_one)
        g1_ref[at, :] = grad_one
        one.append(grad_one.astype(BF16))
        small[0] = small[0] + column_sum(grad_one)
        small[1] = small[1] + column_sum(grad_normed * norm_one)
        small[2] = small[2] + column_sum(grad_normed)
    one = jnp.concatenate(one, axis=0)
    dctx = dot(w_ref[...], one, 1, 1)
    dwo_ref[...] += dot(flat(ctx_ref[...]), one, 1, 0)
    dctx_ref[...] = dctx.astype(BF16).reshape(dctx_ref.shape)
    for n, part in enumerate(small):
        small_ref[n : n + 1] += part


def back_to_context(place, residual, grad_two, slope, ctx, w_expand, w_reduce, weights, vectors):
    tokens, width = residual.shape
    shards, _, hidden = w_expand.shape
    every = ctx.shape[0]
    heads = every // shards
    block = 512
    by_token = lambda: pl.BlockSpec((block, width), lambda i, *_: (i, 0))
    return pl.pallas_call(
        return_kernel,
        grid_spec=pltpu.PrefetchScalarGridSpec(
            num_scalar_prefetch=1,
            grid=(tokens // block,),
            in_specs=[
                by_token(),
                by_token(),
                pl.BlockSpec((shards, block, hidden), lambda i, *_: (0, i, 0)),
                own_block(heads, HD, block),
                whole(w_expand.shape),
                whole(w_reduce.shape),
                whole(weights.shape),
                whole(vectors.shape),
            ],
            out_specs=[
                by_token(),
                pl.BlockSpec((every, HD, block), lambda i, *_: (0, 0, i)),
                whole((heads * HD, width)),
                whole((8, width)),
            ],
        ),
        out_shape=[
            jax.ShapeDtypeStruct((tokens, width), F32),
            jax.ShapeDtypeStruct(ctx.shape, BF16),
            jax.ShapeDtypeStruct((heads * HD, width), F32),
            jax.ShapeDtypeStruct((8, width), F32),
        ],
        compiler_params=params(),
        cost_estimate=cost(tokens * width * (4 * shards * hidden + 2 * every * HD), 40e6),
        name="back_to_context",
    )(place, residual, grad_two, slope, ctx, w_expand, w_reduce, weights, vectors)


def spread_kernel(spots, place_ref, *refs):
    parts, outs = refs[: len(spots)], refs[len(spots) :]
    for ref, (index, offset) in zip(parts, spots):
        start = 0
        for i, out_ref in enumerate(outs):
            size = out_ref.shape[0] // GROUP
            if offset <= i * size < offset + ref.shape[1]:
                put(out_ref, place_ref[index] * size, ref[0, start : start + size, :], 8)
                start += size


def spread(place, pieces, sizes):
    spots = [(index, offset) for _, index, offset in pieces]
    parts = [array for array, _, _ in pieces]
    width = parts[0].shape[2]
    shapes = [(GROUP * size, width) for size in sizes]
    return pl.pallas_call(
        lambda *refs: spread_kernel(spots, *refs),
        grid_spec=pltpu.PrefetchScalarGridSpec(
            num_scalar_prefetch=1,
            grid=(1,),
            in_specs=[whole(a.shape) for a in parts],
            out_specs=[whole(s) for s in shapes],
        ),
        out_shape=[jax.ShapeDtypeStruct(s, F32) for s in shapes],
        compiler_params=params(),
        cost_estimate=cost(0, 10e6),
        name="spread",
    )(place, *parts)


def spread_late_kernel(heads, place_ref, *refs):
    parts = refs[:GROUP]
    dq_ref, dk_ref, dv_ref, dwo_ref, small_ref, grad_scr = refs[GROUP:]
    height = heads * HD
    size, size_two = 3 * height // GROUP, height // GROUP
    top = size + size_two
    for i, ref in enumerate(parts):
        owner = place_ref[i]
        put(grad_scr, owner * size, ref[:size, :], 8)
        put(dwo_ref, owner * size_two, ref[size:top, :], 8)

        @pl.when(owner == 0)
        def _():
            small_ref[...] = ref[top:, :]

    for i, out_ref in enumerate((dq_ref, dk_ref, dv_ref)):
        out_ref[...] = grad_scr[i * height : (i + 1) * height, :]


def spread_late(place, parts, heads):
    share, width = parts[0].shape
    height = heads * HD
    shapes = [(height, width)] * 4 + [(16, width)]
    return pl.pallas_call(
        lambda *refs: spread_late_kernel(heads, *refs),
        grid_spec=pltpu.PrefetchScalarGridSpec(
            num_scalar_prefetch=1,
            grid=(1,),
            in_specs=[whole(a.shape) for a in parts],
            out_specs=[whole(s) for s in shapes],
            scratch_shapes=[pltpu.VMEM((3 * height, width), F32)],
        ),
        out_shape=[jax.ShapeDtypeStruct(s, F32) for s in shapes],
        compiler_params=params(),
        cost_estimate=cost(0, 8 * parts[0].size * 8),
        name="spread_late",
    )(place, *parts)


def input_grads_kernel(place_ref, g1_ref, grad_ref, w_ref, out_ref):
    amount = place_ref[GROUP + 1 + pl.program_id(0)]
    matrix = shift_matrix(amount, g1_ref.shape[0], False)
    total = g1_ref[...] + dot(flat(grad_ref[...]), w_ref[...], 0, 0)
    out_ref[...] = dot(matrix, total.astype(BF16), 1, 0).astype(BF16)


def input_grads(place, length, grad_one, grads, weights):
    tokens, width = grad_one.shape
    every = grads.shape[0]
    by_row = lambda: pl.BlockSpec((length, width), lambda i, *_: (i, 0))
    return pl.pallas_call(
        input_grads_kernel,
        grid_spec=pltpu.PrefetchScalarGridSpec(
            num_scalar_prefetch=1,
            grid=(tokens // length,),
            in_specs=[
                by_row(),
                pl.BlockSpec((every, 3 * HD, length), lambda i, *_: (0, 0, i)),
                whole(weights.shape),
            ],
            out_specs=by_row(),
        ),
        out_shape=jax.ShapeDtypeStruct((tokens, width), BF16),
        compiler_params=params(),
        cost_estimate=cost(2 * tokens * width * (every * 3 * HD + length), 20e6),
        name="input_grads",
    )(place, grad_one, grads, weights)


def after(values, *others):
    return lax.optimization_barrier((values, others))[0]


def solution(mesh):
    peers = mesh.shape["mp"]
    lanes = mesh.shape["dp"]
    rotations = [[(i, (i + k) % peers) for i in range(peers)] for k in range(1, peers)]

    def flip(values, bits):
        return lax.ppermute(values, "dp", [(i, i ^ bits) for i in range(lanes)])

    def from_peers(piece):
        return jnp.stack([lax.ppermute(piece, "mp", perm) for perm in rotations])

    def swapped(piece, *ready):
        copies = jnp.broadcast_to(piece[None], (peers,) + piece.shape)
        got = lax.all_to_all(after(copies, *ready), "mp", 0, 0, tiled=True)
        me = lax.axis_index("mp")
        return jnp.concatenate(
            [
                lax.dynamic_slice_in_dim(got, lax.rem(me + peers - k, peers), 1, 0)
                for k in range(1, peers)
            ]
        )

    def both(near):
        return flip(near, 2), flip(near, 4)

    def corner(by_x, by_y, cut):
        return flip(by_y[:, :cut], 2), flip(by_x[:, cut:], 4)

    def listed(near, by_x, by_y, first, second, cut):
        places = ((near, 0, 0), (by_x, 1, 0), (by_y, 2, 0), (first, 3, 0), (second, 3, cut))
        return with_core(places)

    def with_core(places):
        out = []
        for array, rel, offset in places:
            out.append((array, 2 * rel, offset))
            out.append((flip(array, 1), 2 * rel + 1, offset))
        return out

    planes = [[g + c + i for i in (0, 2, 4, 6)] for g in range(0, lanes, GROUP) for c in (0, 1)]

    def swap_plane(values):
        return lax.all_to_all(values, "dp", 0, 0, tiled=True, axis_index_groups=planes)

    def sum_groups(total):
        step = GROUP
        while step < lanes:
            total = total + flip(total, step)
            step *= 2
        return total

    def partial_sums(mine, got, *ready):
        got = after(got, *ready)
        return [mine[rel] + got[rel] for rel in range(4)]

    def exchange(parts):
        return [flip(parts[rel], 2 * rel) for rel in (1, 2, 3)]

    def total_of(first, rest, *ready):
        rest = after(rest, *ready)
        return sum_groups(first + rest[0] + rest[1] + rest[2])

    def finish(arrays, *ready):
        out = []
        for array in after(arrays, *ready):
            out += [array, flip(array, 1)]
        return out

    def local(
        tokens,
        doc_lengths,
        w_query,
        b_query,
        w_key,
        w_value,
        b_value,
        w_output,
        b_output,
        gain_attn,
        shift_attn,
        w_expand,
        b_expand,
        w_reduce,
        b_reduce,
        gain_ffn,
        shift_ffn,
        cotangent,
    ):
        row_count, length, width = tokens.shape
        heads = w_query.shape[1] // HD
        hidden = w_expand.shape[1]
        count = row_count * length
        inside = lax.axis_index("dp") % GROUP
        me = lax.axis_index("mp")
        ends = jnp.cumsum(doc_lengths, axis=-1)
        longest = jnp.max(doc_lengths, axis=-1, keepdims=True)
        offset = jnp.max(jnp.where(doc_lengths == longest, ends - doc_lengths, 0), axis=-1)
        place = jnp.stack([inside ^ i for i in range(GROUP)] + [me])
        place = jnp.concatenate([place, offset]).astype(jnp.int32)

        by_head = lambda w: w.T.reshape(heads, HD, width)
        own_heads = jnp.concatenate([by_head(w_query), by_head(w_key), by_head(w_value)], axis=1)
        own_heads = jnp.concatenate([own_heads.reshape(3 * heads * HD, width), w_output])
        blank = jnp.zeros((width - 2 * heads * HD,), BF16)
        own_bias = jnp.stack(
            [jnp.concatenate([b_query, b_value, blank]), b_expand]
            + [jnp.zeros((width,), BF16)] * 6
        ).astype(F32)

        def piece_of(array, bits=0):
            size = array.shape[0] // GROUP
            return lax.dynamic_slice_in_dim(array, (inside ^ bits) * size, size, 0).astype(F32)

        piece = piece_of(own_heads)
        near = from_peers(jnp.concatenate([piece, own_bias]))

        position = (jnp.arange(length, dtype=jnp.int32)[None] + offset[:, None]) % length
        segment = jnp.sum((position[:, :, None] >= ends[:, None, :]).astype(jnp.int32), axis=-1)
        segment = segment.reshape(1, count)
        docs = doc_lengths.shape[1]
        label = jnp.arange(EXTRA, dtype=jnp.int32)[:, None]
        is_doc = label < docs
        qf = jnp.where(is_doc & (segment == label), 1.0, 0.0).astype(BF16)
        kf = jnp.where(
            is_doc,
            jnp.where(segment == label, 0.0, MASK),
            jnp.where(label < docs + 3, 1.0, 0.0),
        ).astype(BF16)
        inputs, cot = shift(
            place, length, tokens.reshape(count, width), cotangent.reshape(count, width)
        )
        own = attend_own(
            length, peers, place, inputs, own_bias, qf, kf, own_heads
        )

        near = after(near, own)
        biases = near[:, -own_bias.shape[0] :]
        all_biases = jnp.concatenate([own_bias[None], biases])
        near = near[:, : -own_bias.shape[0]]
        cut = piece.shape[0] // 2
        near_expand = swapped(piece_of(w_expand), near)
        sides = both(near)
        corners = corner(*sides, cut)
        pieces = listed(near, *sides, *corners, cut)
        near_reduce = swapped(piece_of(w_reduce), near_expand)
        sides_expand = both(after(near_expand, corners))
        weights, all_output, qkv, ctx, aug = attend_peers(
            length, peers, place, inputs, after(biases, near_expand), qf, kf, pieces, own
        )

        sides_expand = after(sides_expand, ctx)
        cut = width // GROUP // 2
        corners = corner(*sides_expand, cut)
        vectors = jnp.stack(
            [b_output, gain_attn, shift_attn, b_reduce, gain_ffn, shift_ffn]
            + [jnp.zeros((width,), BF16)] * 2
        ).astype(F32)
        residual, low = add_attended(inputs, ctx, all_output, after(vectors, sides_expand))
        near_reduce, corners = after((near_reduce, corners), low)
        pieces = listed(near_expand, *sides_expand, *corners, cut)
        sides_reduce = both(near_reduce)
        diagonal = swapped(piece_of(w_reduce, 6), near_reduce)
        act, slope, all_expand = expand(
            place, low, after(all_biases, near_reduce), w_expand, pieces, peers
        )
        far_reduce = after((*sides_reduce, diagonal), act)
        pieces = with_core([(array, rel, 0) for rel, array in enumerate([near_reduce, *far_reduce])])
        shifted, grad_two, all_reduce, mine, send, small_one = reduce(
            place, residual, cot, act, slope, vectors, w_reduce, pieces
        )
        got = flip(send, 1)
        output = unshift(place, length, shifted)
        chip = mine + after(got, output)
        early = swap_plane(chip)
        grad_one, dctx, dwo, small = back_to_context(
            place,
            residual,
            grad_two,
            slope,
            ctx,
            all_expand,
            all_reduce,
            all_output,
            after(vectors, chip),
        )
        cut = width // GROUP
        early = sum_groups(jnp.sum(after(early, grad_one), axis=0))[None]
        sides = both(early)
        dqkv, mine, send = attend_back_own(
            length, place, qkv, ctx, aug, dctx, after(kf, early), inputs, dwo, small, small_one
        )
        got = flip(after(send, sides), 1)
        dqkv = attend_back(
            length, peers, 1, 1, place, qkv, ctx, aug, dctx, after(kf, sides), dqkv
        )
        corners = corner(*sides, cut)
        beside = [flip(array, 1) for array in (early, *sides)]
        parts = partial_sums(mine, got, dqkv)
        rest = exchange(parts)
        corners, beside, kept = after((corners, beside, kf), parts)
        dqkv = attend_back(length, peers, 2, peers - 2, place, qkv, ctx, aug, dctx, kept, dqkv)
        total = total_of(parts[0], rest, dqkv)
        second = [total] + exchange([None] + [total] * 3)
        beside += [flip(array, 1) for array in corners]
        pieces = []
        spots = ((0, 0), (2, 0), (4, 0), (6, 0), (6, cut))
        for near, far, (index, top) in zip((early, *sides, *corners), beside, spots):
            pieces += [(near, index, top), (far, index + 1, top)]
        grad_one = after(grad_one, total, beside)
        grad_tokens = input_grads(place, length, grad_one, dqkv, weights)
        second = finish(second, grad_tokens)
        dwe, dwr = spread(place, pieces, [width // GROUP, hidden // GROUP])
        dq, dk, dv, dwo, small_two = spread_late(place, second, heads)
        sums = lambda i: small_two[3 : 3 + heads, i * HD : (i + 1) * HD].reshape(heads * HD)
        shape = (row_count, length, width)
        return (
            output.reshape(shape),
            grad_tokens.reshape(shape),
            dq.T,
            sums(0),
            dk.T,
            dv.T,
            sums(2),
            dwo,
            small_two[0],
            small_two[1],
            small_two[2],
            dwe,
            small_two[11],
            dwr,
            small_two[8],
            small_two[9],
            small_two[10],
        )

    rows, split = P("dp", None, None), P(None, "mp")
    return jax.shard_map(
        local,
        mesh=mesh,
        in_specs=(
            rows,
            P("dp", None),
            split,
            P("mp"),
            split,
            split,
            P("mp"),
            P("mp", None),
            P(),
            P(),
            P(),
            split,
            P("mp"),
            P("mp", None),
            P(),
            P(),
            P(),
            rows,
        ),
        out_specs=(
            rows,
            rows,
            split,
            P("mp"),
            split,
            split,
            P("mp"),
            P("mp", None),
            P(),
            P(),
            P(),
            split,
            P("mp"),
            P("mp", None),
            P(),
            P(),
            P(),
        ),
        check_vma=False,
    )
```

profile of v0, /device:TPU:0, one launch (start us, length us, event | category | flops | bytes accessed | tf_op | source)
XLA Modules:
  0.0 344.2 jit_solution(13539654764523819944)
XLA Ops:
  3.7 5.1 %collective-permute-start.2 = (f32[104,768]{1,0:T(8,128)S(1)}, f32[104,768]{1,0:T(8,128)S(1)}, u32[]{:S(2)}, u32[]{:S(2)}) collective-permute-start(f32[104,768]{1,0:T(8,128)S(1)} %pad_maximum_fusion.6), channel_id=1, source_target_pairs={{0,3},{1,0},{2,1},{3,2},{4,7},{5,4},{6,5},{7,6},{8,11},{9,8},{10,9... | collective-permute-start | bytes 958472 | tf_op jit(solution)/shard_map/ppermute | solution.py:882
  14.7 7.7 %shift.1 = (bf16[2048,768]{1,0:T(8,128)(2,1)}, bf16[2048,768]{1,0:T(8,128)(2,1)}) custom-call(s32[13]{0:T(128)} %concatenate.34.place_ref.refs_0_, bf16[2048,768]{1,0:T(8,128)(2,1)} %bitcast.56, bf16[2048,768]{1,0:T(8,128)(2,1)} %bitcast.57), custom_call_target="tpu_custom_call" | custom-call | flops 3221225472 | bytes 12000000 | tf_op jit(solution)/shard_map/shift/pallas_call | solution.py:93
  22.4 8.6 %attend_own.1 = (bf16[2304,768]{1,0:T(8,128)(2,1)}, bf16[768,768]{1,0:T(8,128)(2,1)}, bf16[12,192,2048]{2,1,0:T(8,128)(2,1)}, bf16[12,64,2048]{2,1,0:T(8,128)(2,1)}, bf16[12,16,2048]{2,1,0:T(8,128)(2,1)}) custom-call(s32[13]{0:T(128)} %concatenate.34.place_ref.refs_0_, bf16[2048,768]{1,0:T(8,128)(2,1)} %get-tuple-element.91.x_ref.refs_1_.refs_0_, ...), custom_call_target="tpu_custom_call" | custom-call | flops 5033164800 | bytes 12000000 | tf_op jit(solution)/shard_map/attend_own/pallas_call | solution.py:191
  31.0 5.0 %collective-permute-done.1 = f32[104,768]{1,0:T(8,128)S(1)} collective-permute-done((f32[104,768]{1,0:T(8,128)S(1)}, f32[104,768]{1,0:T(8,128)S(1)}, u32[]{:S(2)}, u32[]{:S(2)}) %collective-permute-start.1) | collective-permute-done | bytes 319520 | tf_op jit(solution)/shard_map/ppermute | solution.py:882
  38.2 4.1 %all-to-all-start = ((f32[4,96,768]{2,1,0:T(8,128)}), f32[4,96,768]{2,1,0:T(8,128)S(1)}, u32[]{:S(2)}, u32[]{:S(2)}) async-start(f32[4,96,768]{2,1,0:T(8,128)} %broadcast_in_dim.77), calls=%async_computation | async-start | bytes 2359296 | tf_op jit(solution)/shard_map/all_to_all | solution.py:886
  46.2 16.9 %collective-permute-done.6.refs_9_ = f32[3,96,768]{2,1,0:T(8,128)} collective-permute-done((f32[3,96,768]{2,1,0:T(8,128)}, f32[3,96,768]{2,1,0:T(8,128)}, u32[]{:S(2)}, u32[]{:S(2)}) %collective-permute-start.6) | collective-permute-done | bytes 884768 | tf_op jit(solution)/shard_map/ppermute | solution.py:879
  69.4 5.6 %collective-permute-done.8.refs_11_ = f32[3,48,768]{2,1,0:T(8,128)S(1)} collective-permute-done((f32[3,48,768]{2,1,0:T(8,128)S(1)}, f32[3,48,768]{2,1,0:T(8,128)S(1)}, u32[]{:S(2)}, u32[]{:S(2)}) %collective-permute-start.8) | collective-permute-done | bytes 442400 | tf_op jit(solution)/shard_map/ppermute | solution.py:879
  75.0 5.2 %collective-permute-done.10.refs_13_ = f32[3,48,768]{2,1,0:T(8,128)} collective-permute-done((f32[3,48,768]{2,1,0:T(8,128)S(1)}, f32[3,48,768]{2,1,0:T(8,128)}, u32[]{:S(2)}, u32[]{:S(2)}) %collective-permute-start.10) | collective-permute-done | bytes 442400 | tf_op jit(solution)/shard_map/ppermute | solution.py:879
  82.4 4.8 %all-to-all-start.1 = ((f32[4,96,768]{2,1,0:T(8,128)}), f32[4,96,768]{2,1,0:T(8,128)S(1)}, u32[]{:S(2)}, u32[]{:S(2)}) async-start(f32[4,96,768]{2,1,0:T(8,128)} %broadcast_in_dim.78), calls=%async_computation.1 | async-start | bytes 2359296 | tf_op jit(solution)/shard_map/all_to_all | solution.py:886
  90.7 22.9 %attend_peers.1 = (bf16[2304,768]{1,0:T(8,128)(2,1)}, bf16[768,768]{1,0:T(8,128)(2,1)}, bf16[12,192,2048]{2,1,0:T(8,128)(2,1)}, bf16[12,64,2048]{2,1,0:T(8,128)(2,1)}, bf16[12,16,2048]{2,1,0:T(8,128)(2,1)}) custom-call(s32[13]{0:T(128)} %concatenate.34.place_ref.refs_0_, ...), custom_call_target="tpu_custom_call", output_to_operand_aliasing={{0}: (15, {}), {1}: (16, {}), {2}: (17, {}), {3}: (18, {}),... | custom-call | flops 15099494400 | bytes 30000000 | tf_op jit(solution)/shard_map/attend_peers/pallas_call | solution.py:239
  119.2 8.7 %add_attended.1 = (f32[2048,768]{1,0:T(8,128)}, bf16[2048,768]{1,0:T(8,128)(2,1)}) custom-call(bf16[2048,768]{1,0:T(8,128)(2,1)} %get-tuple-element.91.x_ref.refs_1_.refs_0_, bf16[12,64,2048]{2,1,0:T(8,128)(2,1)} %get-tuple-element.100.ctx_ref, bf16[768,768]{1,0:T(8,128)(2,1)} %get-tuple-element.101.wo_ref.w_ref, ...), custom_call_target="tpu_custom_call" | custom-call | flops 2415919104 | bytes 17000000 | tf_op jit(solution)/shard_map/add_attended/pallas_call | solution.py:462
  132.0 4.9 %all-to-all-start.2 = ((f32[4,96,768]{2,1,0:T(8,128)}), f32[4,96,768]{2,1,0:T(8,128)S(1)}, u32[]{:S(2)}, u32[]{:S(2)}) async-start(f32[4,96,768]{2,1,0:T(8,128)} %broadcast_in_dim.79), calls=%async_computation.2 | async-start | bytes 2359296 | tf_op jit(solution)/shard_map/all_to_all | solution.py:886
  140.2 26.7 %expand.1 = (bf16[4,2048,768]{2,1,0:T(8,128)(2,1)}, bf16[4,2048,768]{2,1,0:T(8,128)(2,1)}, bf16[4,768,768]{2,1,0:T(8,128)(2,1)}) custom-call(s32[13]{0:T(128)} %concatenate.34.place_ref.refs_0_, bf16[2048,768]{1,0:T(8,128)(2,1)} %get-tuple-element.108.refs_1_, f32[4,8,768]{2,1,0:T(8,128)} %pad_maximum_fusion.7.refs_2_, bf16[768,768]{1,0:T(8,128)(2,1)} %refs_3_.1, ...), custom_call_target="tpu_custom_call" | custom-call | flops 9663676416 | bytes 40000000 | tf_op jit(solution)/shard_map/expand/pallas_call | solution.py:535
  173.2 36.5 %reduce.15 = (bf16[2048,768]{1,0:T(8,128)(2,1)}, f32[2048,768]{1,0:T(8,128)}, bf16[4,768,768]{2,1,0:T(8,128)(2,1)}, f32[4,192,768]{2,1,0:T(8,128)}, f32[4,192,768]{2,1,0:T(8,128)}, /*index=5*/f32[8,768]{1,0:T(8,128)}) custom-call(s32[13]{0:T(128)} %concatenate.34.place_ref.refs_0_, f32[2048,768]{1,0:T(8,128)} %get-tuple-element.106.refs_1_.sum_ref, ...), custom_call_target="tpu_custom_call" | custom-call | flops 16911433728 | bytes 40000000 | tf_op jit(solution)/shard_map/reduce/pallas_call | solution.py:644
  210.0 6.2 %unshift.1 = bf16[2048,768]{1,0:T(8,128)(2,1)} custom-call(s32[13]{0:T(128)} %concatenate.34.place_ref.refs_0_, bf16[2048,768]{1,0:T(8,128)(2,1)} %get-tuple-element.120.in_ref), custom_call_target="tpu_custom_call" | custom-call | flops 1610612736 | bytes 6000000 | tf_op jit(solution)/shard_map/unshift/pallas_call | solution.py:117
  216.2 3.4 add.118
  219.5 3.9 %all-to-all-start.3 = ((f32[4,192,768]{2,1,0:T(8,128)}), f32[4,192,768]{2,1,0:T(8,128)S(1)}, u32[]{:S(2)}, u32[]{:S(2)}) async-start(f32[4,192,768]{2,1,0:T(8,128)} %add.118), calls=%async_computation.3 | async-start | bytes 4718592 | tf_op jit(solution)/shard_map/all_to_all | solution.py:915
  223.4 33.6 %back_to_context.1 = (f32[2048,768]{1,0:T(8,128)}, bf16[12,64,2048]{2,1,0:T(8,128)(2,1)}, f32[192,768]{1,0:T(8,128)}, f32[8,768]{1,0:T(8,128)}) custom-call(s32[13]{0:T(128)} %concatenate.34.place_ref.refs_0_, f32[2048,768]{1,0:T(8,128)} %get-tuple-element.106.refs_1_.sum_ref, f32[2048,768]{1,0:T(8,128)} %get-tuple-element.121.g2_ref, ...), custom_call_target="tpu_custom_call" | custom-call | flops 21743271936 | bytes 40000000 | tf_op jit(solution)/shard_map/back_to_context/pallas_call | solution.py:735
  260.8 11.8 %attend_back_own.1 = (bf16[12,192,2048]{2,1,0:T(8,128)(2,1)}, f32[4,112,768]{2,1,0:T(8,128)}, f32[4,112,768]{2,1,0:T(8,128)}) custom-call(s32[13]{0:T(128)} %concatenate.34.place_ref.refs_0_, bf16[12,192,2048]{2,1,0:T(8,128)(2,1)} %get-tuple-element.129.qkv_ref, bf16[12,64,2048]{2,1,0:T(8,128)(2,1)} %get-tuple-element.100.ctx_ref, ...), custom_call_target="tpu_custom_call" | custom-call | flops 5838471168 | bytes 12000000 | tf_op jit(solution)/shard_map/attend_back_own/pallas_call | solution.py:362
  280.6 8.0 %attend_back.2.old_ref = bf16[12,192,2048]{2,1,0:T(8,128)(2,1)} custom-call(s32[13]{0:T(128)} %concatenate.34.place_ref.refs_0_, bf16[12,192,2048]{2,1,0:T(8,128)(2,1)} %get-tuple-element.129.qkv_ref, bf16[12,64,2048]{2,1,0:T(8,128)(2,1)} %get-tuple-element.100.ctx_ref, ...), custom_call_target="tpu_custom_call", output_to_operand_aliasing={{}: (6, {})} | custom-call | flops 4026531840 | bytes 12000000 | tf_op jit(solution)/shard_map/attend_back/pallas_call | solution.py:401
  293.6 13.1 %attend_back.3.grad_ref = bf16[12,192,2048]{2,1,0:T(8,128)(2,1)} custom-call(s32[13]{0:T(128)} %concatenate.34.place_ref.refs_0_, bf16[12,192,2048]{2,1,0:T(8,128)(2,1)} %get-tuple-element.129.qkv_ref, bf16[12,64,2048]{2,1,0:T(8,128)(2,1)} %get-tuple-element.100.ctx_ref, ...), custom_call_target="tpu_custom_call", output_to_operand_aliasing={{}: (6, {})} | custom-call | flops 8053063680 | bytes 12000000 | tf_op jit(solution)/shard_map/attend_back/pallas_call | solution.py:401
  311.8 16.5 %input_grads.1 = bf16[2048,768]{1,0:T(8,128)(2,1)} custom-call(s32[13]{0:T(128)} %concatenate.34.place_ref.refs_0_, f32[2048,768]{1,0:T(8,128)} %get-tuple-element.152.g1_ref, bf16[12,192,2048]{2,1,0:T(8,128)(2,1)} %attend_back.3.grad_ref, bf16[2304,768]{1,0:T(8,128)(2,1)} %get-tuple-element.153.w_ref), custom_call_target="tpu_custom_call" | custom-call | flops 8858370048 | bytes 20000000 | tf_op jit(solution)/shard_map/input_grads/pallas_call | solution.py:850
  329.5 5.4 %spread.1 = (f32[768,768]{1,0:T(8,128)}, f32[768,768]{1,0:T(8,128)}) custom-call(s32[13]{0:T(128)} %concatenate.34.place_ref.refs_0_, f32[1,192,768]{2,1,0:T(8,128)} %bitcast.46, f32[1,192,768]{2,1,0:T(8,128)} %collective-permute-done.36.refs_2_, f32[1,192,768]{2,1,0:T(8,128)} %collective-permute-done.28.refs_3_, ...), custom_call_target="tpu_custom_call" | custom-call | bytes 10000000 | tf_op jit(solution)/shard_map/spread/pallas_call | solution.py:785
  336.7 4.0 %spread_late.1 = (f32[192,768]{1,0:T(8,128)}, f32[192,768]{1,0:T(8,128)}, f32[192,768]{1,0:T(8,128)}, f32[192,768]{1,0:T(8,128)}, f32[16,768]{1,0:T(8,128)}) custom-call(s32[13]{0:T(128)} %concatenate.34.place_ref.refs_0_, f32[112,768]{1,0:T(8,128)} %copy-done.2, f32[112,768]{1,0:T(8,128)} %copy-done.10, f32[112,768]{1,0:T(8,128)} %copy-done.9, ...), custom_call_target="tpu_custom_call" | custom-call | bytes 5505024 | tf_op jit(solution)/shard_map/spread_late/pallas_call | solution.py:823
  (222 shorter events, 74.5 us)
Async XLA Ops:
  3.7 27.3 %collective-permute-start.2 = (f32[104,768]{1,0:T(8,128)S(1)}, f32[104,768]{1,0:T(8,128)S(1)}, u32[]{:S(2)}, u32[]{:S(2)}) collective-permute-start(f32[104,768]{1,0:T(8,128)S(1)} %pad_maximum_fusion.6), channel_id=1, source_target_pairs={{0,3},{1,0},{2,1},{3,2},{4,7},{5,4},{6,5},{7,6},{8,11},{9,8},{10,9... | collective-permute-start | bytes 958472 | tf_op jit(solution)/shard_map/ppermute | solution.py:882
  8.8 27.2 %collective-permute-start.1 = (f32[104,768]{1,0:T(8,128)S(1)}, f32[104,768]{1,0:T(8,128)S(1)}, u32[]{:S(2)}, u32[]{:S(2)}) collective-permute-start(f32[104,768]{1,0:T(8,128)S(1)} %pad_maximum_fusion.6), channel_id=1, source_target_pairs={{0,2},{1,3},{2,0},{3,1},{4,6},{5,7},{6,4},{7,5},{8,10},{9,11},{10,... | collective-permute-start | bytes 958472 | tf_op jit(solution)/shard_map/ppermute | solution.py:882
  8.8 27.2 %collective-permute-start = (f32[104,768]{1,0:T(8,128)S(1)}, f32[104,768]{1,0:T(8,128)S(1)}, u32[]{:S(2)}, u32[]{:S(2)}) collective-permute-start(f32[104,768]{1,0:T(8,128)S(1)} %pad_maximum_fusion.6), channel_id=1, source_target_pairs={{0,1},{1,2},{2,3},{3,0},{4,5},{5,6},{6,7},{7,4},{8,9},{9,10},{10,1... | collective-permute-start | bytes 958472 | tf_op jit(solution)/shard_map/ppermute | solution.py:882
  38.2 42.0 %all-to-all-start = ((f32[4,96,768]{2,1,0:T(8,128)}), f32[4,96,768]{2,1,0:T(8,128)S(1)}, u32[]{:S(2)}, u32[]{:S(2)}) async-start(f32[4,96,768]{2,1,0:T(8,128)} %broadcast_in_dim.77), calls=%async_computation | async-start | bytes 2359296 | tf_op jit(solution)/shard_map/all_to_all | solution.py:886
  42.2 20.8 %collective-permute-start.6 = (f32[3,96,768]{2,1,0:T(8,128)}, f32[3,96,768]{2,1,0:T(8,128)}, u32[]{:S(2)}, u32[]{:S(2)}) collective-permute-start(f32[3,96,768]{2,1,0:T(8,128)} %slice.76.refs_5_), channel_id=1, source_target_pairs={{0,16},{4,20},{8,24},{12,28},{16,0},{20,4},{24,8},{28,12},{1,17},{... | collective-permute-start | bytes 2654216 | tf_op jit(solution)/shard_map/ppermute | solution.py:879
  43.8 22.6 %collective-permute-start.4 = (f32[3,96,768]{2,1,0:T(8,128)}, f32[3,96,768]{2,1,0:T(8,128)}, u32[]{:S(2)}, u32[]{:S(2)}) collective-permute-start(f32[3,96,768]{2,1,0:T(8,128)} %slice.76.refs_5_), channel_id=1, source_target_pairs={{0,8},{4,12},{8,0},{12,4},{16,24},{20,28},{24,16},{28,20},{1,9},{5... | collective-permute-start | bytes 2654216 | tf_op jit(solution)/shard_map/ppermute | solution.py:879
  46.2 42.4 %collective-permute-start.3 = (f32[3,96,768]{2,1,0:T(8,128)}, f32[3,96,768]{2,1,0:T(8,128)}, u32[]{:S(2)}, u32[]{:S(2)}) collective-permute-start(f32[3,96,768]{2,1,0:T(8,128)} %slice.76.refs_5_), channel_id=1, source_target_pairs={{0,4},{4,0},{8,12},{12,8},{16,20},{20,16},{24,28},{28,24},{1,5},{5... | collective-permute-start | bytes 2654216 | tf_op jit(solution)/shard_map/ppermute | solution.py:879
  66.4 24.2 %collective-permute-start.7 = (f32[3,96,768]{2,1,0:T(8,128)}, f32[3,96,768]{2,1,0:T(8,128)}, u32[]{:S(2)}, u32[]{:S(2)}) collective-permute-start(f32[3,96,768]{2,1,0:T(8,128)} %collective-permute-done.6.refs_9_), channel_id=1, source_target_pairs={{0,4},{4,0},{8,12},{12,8},{16,20},{20,16},{24,28},{28,24},{1,5},{5... | collective-permute-start | bytes 2654216 | tf_op jit(solution)/shard_map/ppermute | solution.py:879
  69.2 21.5 %collective-permute-start.5 = (f32[3,96,768]{2,1,0:T(8,128)}, f32[3,96,768]{2,1,0:T(8,128)}, u32[]{:S(2)}, u32[]{:S(2)}) collective-permute-start(f32[3,96,768]{2,1,0:T(8,128)} %collective-permute-done.4.refs_7_), channel_id=1, source_target_pairs={{0,4},{4,0},{8,12},{12,8},{16,20},{20,16},{24,28},{28,24},{1,5},{5... | collective-permute-start | bytes 2654216 | tf_op jit(solution)/shard_map/ppermute | solution.py:879
  82.4 45.5 %all-to-all-start.1 = ((f32[4,96,768]{2,1,0:T(8,128)}), f32[4,96,768]{2,1,0:T(8,128)S(1)}, u32[]{:S(2)}, u32[]{:S(2)}) async-start(f32[4,96,768]{2,1,0:T(8,128)} %broadcast_in_dim.78), calls=%async_computation.1 | async-start | bytes 2359296 | tf_op jit(solution)/shard_map/all_to_all | solution.py:886
  88.6 49.6 %collective-permute-start.16 = (f32[3,96,768]{2,1,0:T(8,128)}, f32[3,96,768]{2,1,0:T(8,128)}, u32[]{:S(2)}, u32[]{:S(2)}) collective-permute-start(f32[3,96,768]{2,1,0:T(8,128)} %pad_maximum_fusion.3.refs_4_), channel_id=1, source_target_pairs={{0,4},{4,0},{8,12},{12,8},{16,20},{20,16},{24,28},{28,24},{1,5},{5... | collective-permute-start | bytes 2654216 | tf_op jit(solution)/shard_map/ppermute | solution.py:879
  88.8 24.7 %collective-permute-start.13 = (f32[3,96,768]{2,1,0:T(8,128)}, f32[3,96,768]{2,1,0:T(8,128)}, u32[]{:S(2)}, u32[]{:S(2)}) collective-permute-start(f32[3,96,768]{2,1,0:T(8,128)} %pad_maximum_fusion.3.refs_4_), channel_id=1, source_target_pairs={{0,16},{4,20},{8,24},{12,28},{16,0},{20,4},{24,8},{28,12},{1,17},{... | collective-permute-start | bytes 2654216 | tf_op jit(solution)/shard_map/ppermute | solution.py:879
  90.6 23.0 %collective-permute-start.12 = (f32[3,96,768]{2,1,0:T(8,128)}, f32[3,96,768]{2,1,0:T(8,128)}, u32[]{:S(2)}, u32[]{:S(2)}) collective-permute-start(f32[3,96,768]{2,1,0:T(8,128)} %pad_maximum_fusion.3.refs_4_), channel_id=1, source_target_pairs={{0,8},{4,12},{8,0},{12,4},{16,24},{20,28},{24,16},{28,20},{1,9},{5... | collective-permute-start | bytes 2654216 | tf_op jit(solution)/shard_map/ppermute | solution.py:879
  114.6 23.9 %collective-permute-start.17 = (f32[3,96,768]{2,1,0:T(8,128)}, f32[3,96,768]{2,1,0:T(8,128)}, u32[]{:S(2)}, u32[]{:S(2)}) collective-permute-start(f32[3,96,768]{2,1,0:T(8,128)} %collective-permute-done.12.refs_6_), channel_id=1, source_target_pairs={{0,4},{4,0},{8,12},{12,8},{16,20},{20,16},{24,28},{28,24},{1,5},{5... | collective-permute-start | bytes 2654216 | tf_op jit(solution)/shard_map/ppermute | solution.py:879
  116.5 22.5 %collective-permute-start.18 = (f32[3,96,768]{2,1,0:T(8,128)}, f32[3,96,768]{2,1,0:T(8,128)}, u32[]{:S(2)}, u32[]{:S(2)}) collective-permute-start(f32[3,96,768]{2,1,0:T(8,128)} %collective-permute-done.13.refs_8_), channel_id=1, source_target_pairs={{0,4},{4,0},{8,12},{12,8},{16,20},{20,16},{24,28},{28,24},{1,5},{5... | collective-permute-start | bytes 2654216 | tf_op jit(solution)/shard_map/ppermute | solution.py:879
  132.0 35.1 %all-to-all-start.2 = ((f32[4,96,768]{2,1,0:T(8,128)}), f32[4,96,768]{2,1,0:T(8,128)S(1)}, u32[]{:S(2)}, u32[]{:S(2)}) async-start(f32[4,96,768]{2,1,0:T(8,128)} %broadcast_in_dim.79), calls=%async_computation.2 | async-start | bytes 2359296 | tf_op jit(solution)/shard_map/all_to_all | solution.py:886
  138.2 29.0 %collective-permute-start.23 = (f32[3,96,768]{2,1,0:T(8,128)S(1)}, f32[3,96,768]{2,1,0:T(8,128)S(1)}, u32[]{:S(2)}, u32[]{:S(2)}) collective-permute-start(f32[3,96,768]{2,1,0:T(8,128)S(1)} %pad_maximum_fusion.4.refs_7_), channel_id=1, source_target_pairs={{0,16},{4,20},{8,24},{12,28},{16,0},{20,4},{24,8},{28,12},{1,17},{... | collective-permute-start | bytes 2654216 | tf_op jit(solution)/shard_map/ppermute | solution.py:879
  138.5 28.7 %collective-permute-start.22 = (f32[3,96,768]{2,1,0:T(8,128)S(1)}, f32[3,96,768]{2,1,0:T(8,128)}, u32[]{:S(2)}, u32[]{:S(2)}) collective-permute-start(f32[3,96,768]{2,1,0:T(8,128)S(1)} %pad_maximum_fusion.4.refs_7_), channel_id=1, source_target_pairs={{0,8},{4,12},{8,0},{12,4},{16,24},{20,28},{24,16},{28,20},{1,9},{5... | collective-permute-start | bytes 2654216 | tf_op jit(solution)/shard_map/ppermute | solution.py:879
  139.0 28.9 %collective-permute-start.21 = (f32[3,96,768]{2,1,0:T(8,128)S(1)}, f32[3,96,768]{2,1,0:T(8,128)}, u32[]{:S(2)}, u32[]{:S(2)}) collective-permute-start(f32[3,96,768]{2,1,0:T(8,128)S(1)} %pad_maximum_fusion.4.refs_7_), channel_id=1, source_target_pairs={{0,4},{4,0},{8,12},{12,8},{16,20},{20,16},{24,28},{28,24},{1,5},{5... | collective-permute-start | bytes 2654216 | tf_op jit(solution)/shard_map/ppermute | solution.py:879
  219.5 37.5 %all-to-all-start.3 = ((f32[4,192,768]{2,1,0:T(8,128)}), f32[4,192,768]{2,1,0:T(8,128)S(1)}, u32[]{:S(2)}, u32[]{:S(2)}) async-start(f32[4,192,768]{2,1,0:T(8,128)} %add.118), calls=%async_computation.3 | async-start | bytes 4718592 | tf_op jit(solution)/shard_map/all_to_all | solution.py:915
  293.1 18.6 %collective-permute-start.39 = (f32[1,96,768]{2,1,0:T(8,128)}, f32[1,96,768]{2,1,0:T(8,128)S(1)}, u32[]{:S(2)}, u32[]{:S(2)}) collective-permute-start(f32[1,96,768]{2,1,0:T(8,128)} %collective-permute-done.34.refs_7_), channel_id=1, source_target_pairs={{0,4},{4,0},{8,12},{12,8},{16,20},{20,16},{24,28},{28,24},{1,5},{5... | collective-permute-start | bytes 884744 | tf_op jit(solution)/shard_map/ppermute | solution.py:879
  293.1 18.6 %collective-permute-start.40 = (f32[1,96,768]{2,1,0:T(8,128)}, f32[1,96,768]{2,1,0:T(8,128)S(1)}, u32[]{:S(2)}, u32[]{:S(2)}) collective-permute-start(f32[1,96,768]{2,1,0:T(8,128)} %collective-permute-done.35.refs_9_), channel_id=1, source_target_pairs={{0,4},{4,0},{8,12},{12,8},{16,20},{20,16},{24,28},{28,24},{1,5},{5... | collective-permute-start | bytes 884744 | tf_op jit(solution)/shard_map/ppermute | solution.py:879
  308.2 20.1 %collective-permute-start.43 = (f32[112,768]{1,0:T(8,128)S(1)}, f32[112,768]{1,0:T(8,128)S(1)}, u32[]{:S(2)}, u32[]{:S(2)}) collective-permute-start(f32[112,768]{1,0:T(8,128)S(1)} %add_add_fusion.refs_1_), channel_id=1, source_target_pairs={{0,24},{4,28},{8,16},{12,20},{16,8},{20,12},{24,0},{28,4},{1,25},{... | collective-permute-start | bytes 1032200 | tf_op jit(solution)/shard_map/ppermute | solution.py:879
  309.7 18.6 %collective-permute-start.42 = (f32[112,768]{1,0:T(8,128)S(1)}, f32[112,768]{1,0:T(8,128)S(1)}, u32[]{:S(2)}, u32[]{:S(2)}) collective-permute-start(f32[112,768]{1,0:T(8,128)S(1)} %add_add_fusion.refs_1_), channel_id=1, source_target_pairs={{0,16},{4,20},{8,24},{12,28},{16,0},{20,4},{24,8},{28,12},{1,17},{... | collective-permute-start | bytes 1032200 | tf_op jit(solution)/shard_map/ppermute | solution.py:879
  (60 other events, 554.7 us)
where the time goes:
time: 346 us; the launch traced here: 344 us
  Pallas kernels  210 us (61%)
  starting transfers between devices  54.3 us (16%)
  waiting for transfers between devices  43.5 us (13%)
  local copies, waits for them, and re-layouts  21.9 us (6%)
  other arithmetic  13.6 us (4%)
    ppermute x45, waiting for transfers between devices, flip(): return lax.ppermute(values, 'dp', [(i, i ^ bits) for i in range(lanes)])  38.5 us
    pallas_call x1, Pallas kernels, reduce(): pl.pallas_call(lambda *refs: reduce_kernel(spots, *refs), grid_spec=pltpu...  36.5 us
    pallas_call x1, Pallas kernels, back_to_context(): pl.pallas_call(return_kernel, grid_spec=pltpu.PrefetchScalarGridSpec(num_...  33.6 us
    ppermute x45, starting transfers between devices, flip(): return lax.ppermute(values, 'dp', [(i, i ^ bits) for i in range(lanes)])  30.5 us
    pallas_call x1, Pallas kernels, expand(): pl.pallas_call(lambda *refs: expand_kernel(spots, *refs), grid_spec=pltpu...  26.7 us
    pallas_call x1, Pallas kernels, attend_peers(): pl.pallas_call(lambda *refs: attend_peers_kernel(spots, *refs), grid_spec...  22.9 us
    pallas_call x2, Pallas kernels, attend_back(): pl.pallas_call(attend_back_kernel, grid_spec=pltpu.PrefetchScalarGridSpec...  21.1 us
    pallas_call x1, Pallas kernels, input_grads(): pl.pallas_call(input_grads_kernel, grid_spec=pltpu.PrefetchScalarGridSpec...  16.5 us
  transfers between devices with their start and end apart: 52, of which 14 were waited for; matrix products, arithmetic and copies ran while one was open for 6% of the time, Pallas kernels for 49%

commit v1 on v0

--- a/solution.py
+++ b/solution.py
@@ -170,23 +170,20 @@
 
 
 def attend_own_kernel(place_ref, x_ref, bias_ref, qf_ref, kf_ref, own_ref, *refs):
-    w_ref, wo_ref, qkv_ref, ctx_ref, aug_ref = refs
-    height = w_ref.shape[0]
+    w_ref, qkv_ref, ctx_ref, aug_ref = refs
 
     @pl.when(pl.program_id(0) == 0)
     def _():
-        w_ref[...] = own_ref[:height, :]
-        wo_ref[...] = own_ref[height:, :]
+        w_ref[...] = own_ref[...]
 
     attend_rows(x_ref, bias_ref, qf_ref, kf_ref, w_ref, qkv_ref, ctx_ref, aug_ref)
 
 
 def attend_own(length, peers, place, inputs, bias, qf, kf, own):
-    heads = own.shape[0] // (4 * HD)
+    heads = own.shape[0] // (3 * HD)
     tokens, width = inputs.shape
     every = peers * heads
-    shapes = [(every * 3 * HD, width), (every * HD, width)]
-    shapes += [(every, n, tokens) for n in (3 * HD, HD, EXTRA)]
+    shapes = [(every * 3 * HD, width)] + [(every, n, tokens) for n in (3 * HD, HD, EXTRA)]
     by_row = pl.BlockSpec((EXTRA, length), lambda i, *_: (0, i))
     return pl.pallas_call(
         attend_own_kernel,
@@ -202,7 +199,6 @@
             ],
             out_specs=[
                 pl.BlockSpec((heads * 3 * HD, width), lambda i, p: (p[GROUP], 0)),
-                pl.BlockSpec((heads * HD, width), lambda i, p: (p[GROUP], 0)),
                 *[own_block(heads, n, length) for n in (3 * HD, HD, EXTRA)],
             ],
         ),
@@ -216,22 +212,20 @@
 def attend_peers_kernel(spots, place_ref, x_ref, bias_ref, qf_ref, kf_ref, *refs):
     count = len(spots)
     parts = refs[:count]
-    w_ref, wo_ref, qkv_ref, ctx_ref, aug_ref, w_scr = refs[count + 5 :]
-    height = w_ref.shape[0]
+    w_ref, qkv_ref, ctx_ref, aug_ref, wide_scr = refs[count + 4 :]
 
     @pl.when(pl.program_id(1) == 0)
     def _():
-        size = w_scr.shape[0] // GROUP
+        size = w_ref.shape[0] // GROUP
         for ref, (index, offset) in zip(parts, spots):
-            put(w_scr, place_ref[index] * size + offset, ref[0], 16)
-        w_ref[...] = w_scr[:height, :]
-        wo_ref[...] = w_scr[height:, :]
+            put(wide_scr, place_ref[index] * size + offset, ref[0], 8)
+        w_ref[...] = wide_scr[...].astype(BF16)
 
     attend_rows(x_ref, bias_ref.at[0], qf_ref, kf_ref, w_ref, qkv_ref, ctx_ref, aug_ref)
 
 
 def attend_peers(length, peers, place, inputs, bias, qf, kf, pieces, arrays):
-    heads = arrays[2].shape[0] // peers
+    heads = arrays[1].shape[0] // peers
     tokens, width = inputs.shape
     spots = [(index, offset) for _, index, offset in pieces]
     parts = [array for array, _, _ in pieces]
@@ -249,22 +243,19 @@
                 *[
                     pl.BlockSpec((1,) + a.shape[1:], lambda k, i, *_: (k, 0, 0)) for a in parts
                 ],
-                *[ANY] * 5,
+                *[ANY] * 4,
             ],
             out_specs=[
-                *[
-                    pl.BlockSpec(
-                        (heads * n, width),
-                        lambda k, i, p: (lax.rem(p[GROUP] + peers - 1 - k, peers), 0),
-                    )
-                    for n in (3 * HD, HD)
-                ],
+                pl.BlockSpec(
+                    (heads * 3 * HD, width),
+                    lambda k, i, p: (lax.rem(p[GROUP] + peers - 1 - k, peers), 0),
+                ),
                 *[peer_block(peers, 1, heads, n, length) for n in (3 * HD, HD, EXTRA)],
             ],
-            scratch_shapes=[pltpu.VMEM((heads * 4 * HD, width), BF16)],
+            scratch_shapes=[pltpu.VMEM((heads * 3 * HD, width), F32)],
         ),
         out_shape=[jax.ShapeDtypeStruct(a.shape, a.dtype) for a in arrays],
-        input_output_aliases={5 + len(parts) + i: i for i in range(5)},
+        input_output_aliases={5 + len(parts) + i: i for i in range(4)},
         compiler_params=params(),
         cost_estimate=cost(
             (peers - 1) * heads * tokens * (6 * HD * width + 16 * 64 * length), 30e6
@@ -442,7 +433,44 @@
     return values.reshape(-1, values.shape[-1])
 
 
-def attended_kernel(x_ref, ctx_ref, wo_ref, vec_ref, sum_ref, low_ref):
+def fill(place_ref, own_ref, parts, spots, out_ref):
+    shards, height, _ = out_ref.shape
+    out_ref[place_ref[GROUP]] = own_ref[...]
+    for k in range(1, shards):
+        shard = peer_shard(place_ref, shards, k)
+        for ref, (index, offset) in zip(parts, spots):
+            start = place_ref[index] * (height // GROUP) + offset
+            put(out_ref.at[shard], start, ref[k - 1], 16)
+
+
+def expand_kernel(spots, place_ref, x_ref, ctx_ref, bias_ref, vec_ref, own_ref, own_wo_ref, *refs):
+    parts, refs = refs[: len(spots)], refs[len(spots) :]
+    sum_ref, act_ref, slope_ref, full_ref, wo_ref, we_ref, wide_scr, low_scr, sem = refs
+    shards, width, _ = we_ref.shape
+    size, size_two = width // GROUP, wo_ref.shape[0] // (shards * GROUP)
+    kept = pltpu.make_async_copy(we_ref, full_ref, sem)
+
+    @pl.when(pl.program_id(0) == 0)
+    def _():
+        me = place_ref[GROUP]
+        we_ref[me] = own_ref[...]
+        put(wide_scr, me * size_two * GROUP, own_wo_ref[...], 8)
+        for k in range(1, shards):
+            shard = peer_shard(place_ref, shards, k)
+            for ref, (index, offset) in zip(parts, spots):
+                part = ref[k - 1]
+                count = min(part.shape[0], size - offset)
+                put(we_ref.at[shard], place_ref[index] * size + offset, part[:count], 16)
+                if count < part.shape[0]:
+                    start = (shard * GROUP + place_ref[index]) * size_two
+                    put(wide_scr, start, part[count:], 8)
+        wo_ref[...] = wide_scr[...].astype(BF16)
+        kept.start()
+
+    @pl.when(pl.program_id(0) == pl.num_programs(0) - 1)
+    def _():
+        kept.wait()
+
     b_output, gain_one, shift_one = vec_ref[0:1], vec_ref[1:2], vec_ref[2:3]
     half = x_ref.shape[0] // 2
     halves = [slice(0, half), slice(half, 2 * half)]
@@ -451,63 +479,11 @@
         residual = x_ref[at, :].astype(F32) + (part + b_output)
         sum_ref[at, :] = residual
         norm_one, _ = norm_forward(residual)
-        low_ref[at, :] = (norm_one * gain_one + shift_one).astype(BF16)
-
-
-def add_attended(inputs, ctx, w_output, vectors):
-    tokens, width = inputs.shape
-    every = ctx.shape[0]
-    block = 512
-    by_token = lambda: pl.BlockSpec((block, width), lambda i: (i, 0))
-    return pl.pallas_call(
-        attended_kernel,
-        grid=(tokens // block,),
-        in_specs=[
-            by_token(),
-            pl.BlockSpec((every, HD, block), lambda i: (0, 0, i)),
-            whole(w_output.shape),
-            whole(vectors.shape),
-        ],
-        out_specs=[by_token(), by_token()],
-        out_shape=[
-            jax.ShapeDtypeStruct((tokens, width), F32),
-            jax.ShapeDtypeStruct((tokens, width), BF16),
-        ],
-        compiler_params=params(),
-        cost_estimate=cost(2 * tokens * width * every * HD, 17e6),
-        name="add_attended",
-    )(inputs, ctx, w_output, vectors)
-
-
-def fill(place_ref, own_ref, parts, spots, out_ref):
-    shards, height, _ = out_ref.shape
-    out_ref[place_ref[GROUP]] = own_ref[...]
-    for k in range(1, shards):
-        shard = peer_shard(place_ref, shards, k)
-        for ref, (index, offset) in zip(parts, spots):
-            start = place_ref[index] * (height // GROUP) + offset
-            put(out_ref.at[shard], start, ref[k - 1], 16)
-
-
-def expand_kernel(spots, place_ref, low_ref, bias_ref, own_ref, *refs):
-    parts, (act_ref, slope_ref, full_ref, we_ref, sem) = refs[: len(spots)], refs[len(spots) :]
-    shards = we_ref.shape[0]
-    kept = pltpu.make_async_copy(we_ref, full_ref, sem)
-
-    @pl.when(pl.program_id(0) == 0)
-    def _():
-        fill(place_ref, own_ref, parts, spots, we_ref)
-        kept.start()
-
-    @pl.when(pl.program_id(0) == pl.num_programs(0) - 1)
-    def _():
-        kept.wait()
-
-    half = low_ref.shape[0] // 2
-    halves = [slice(0, half), slice(half, 2 * half)]
-    def shard(s, carry):
+        low_scr[at, :] = (norm_one * gain_one + shift_one).astype(BF16)
+
+    def shard_step(s, carry):
         bias = bias_ref[peer_shard(place_ref, shards, s), 1:2]
-        products = [dot(low_ref[at, :], we_ref[s], 1, 0) for at in halves]
+        products = [dot(low_scr[at, :], we_ref[s], 1, 0) for at in halves]
         for at, product in zip(halves, products):
             hidden = product + bias
             square = hidden * hidden
@@ -521,16 +497,18 @@
             slope_ref[s, at, :] = slope.astype(BF16)
         return carry
 
-    lax.fori_loop(0, shards, shard, 0)
-
-
-def expand(place, low, biases, own, pieces, shards):
-    tokens, width = low.shape
+    lax.fori_loop(0, shards, shard_step, 0)
+
+
+def expand(place, inputs, ctx, biases, vectors, own, own_wo, pieces, shards):
+    tokens, width = inputs.shape
     hidden = own.shape[1]
+    every = ctx.shape[0]
     block = 512
     spots = [(index, offset) for _, index, offset in pieces]
     parts = [array for array, _, _ in pieces]
     full = (shards, width, hidden)
+    by_token = lambda: pl.BlockSpec((block, width), lambda i, *_: (i, 0))
     by_shard = lambda: pl.BlockSpec((shards, block, hidden), lambda i, *_: (0, i, 0))
     return pl.pallas_call(
         lambda *refs: expand_kernel(spots, *refs),
@@ -538,23 +516,33 @@
             num_scalar_prefetch=1,
             grid=(tokens // block,),
             in_specs=[
-                pl.BlockSpec((block, width), lambda i, *_: (i, 0)),
+                by_token(),
+                pl.BlockSpec((every, HD, block), lambda i, *_: (0, 0, i)),
                 whole(biases.shape),
+                whole(vectors.shape),
                 whole(own.shape),
+                whole(own_wo.shape),
                 *[whole(a.shape) for a in parts],
             ],
-            out_specs=[by_shard(), by_shard(), ANY],
-            scratch_shapes=[pltpu.VMEM(full, BF16), pltpu.SemaphoreType.DMA],
+            out_specs=[by_token(), by_shard(), by_shard(), ANY, whole((every * HD, width))],
+            scratch_shapes=[
+                pltpu.VMEM(full, BF16),
+                pltpu.VMEM((every * HD, width), F32),
+                pltpu.VMEM((block, width), BF16),
+                pltpu.SemaphoreType.DMA,
+            ],
         ),
         out_shape=[
+            jax.ShapeDtypeStruct((tokens, width), F32),
             jax.ShapeDtypeStruct((shards, tokens, hidden), BF16),
             jax.ShapeDtypeStruct((shards, tokens, hidden), BF16),
             jax.ShapeDtypeStruct(full, BF16),
+            jax.ShapeDtypeStruct((every * HD, width), BF16),
         ],
         compiler_params=params(),
-        cost_estimate=cost(2 * tokens * width * shards * hidden, 40e6),
+        cost_estimate=cost(2 * tokens * width * (shards * hidden + every * HD), 40e6),
         name="expand",
-    )(place, low, biases, own, *parts)
+    )(place, inputs, ctx, biases, vectors, own, own_wo, *parts)
 
 
 def reduce_kernel(spots, place_ref, sum_ref, cot_ref, act_ref, slope_ref, vec_ref, *refs):
@@ -578,36 +566,50 @@
     b_reduce, gain_two, shift_two = vec_ref[3:4], vec_ref[4:5], vec_ref[5:6]
     half = sum_ref.shape[0] // 2
     halves = [slice(0, half), slice(half, 2 * half)]
-    mixed = []
-    for at in halves:
-        part = dot(act_ref[0, at, :], wr_ref[0], 1, 0)
-        for s in range(1, shards):
-            part = part + dot(act_ref[s, at, :], wr_ref[s], 1, 0)
-        mixed.append(part)
-    small = [jnp.zeros((1, sum_ref.shape[1]), F32)] * 4
-    low, normed_low, active = [], [], []
-    for at, part in zip(halves, mixed):
+    quarter = half // 4
+    width = sum_ref.shape[1]
+    small = [jnp.zeros((1, width), F32)] * 4
+
+    def norm_part(start, mixed):
+        at = slice(start, start + quarter)
         norm_one, _ = norm_forward(sum_ref[at, :])
         normed = norm_one * gain_one + shift_one
-        normed_low.append(normed.astype(BF16))
-        norm_two, inverse_two = norm_forward(normed + (part + b_reduce))
+        norm_two, inverse_two = norm_forward(normed + (mixed + b_reduce))
         out_ref[at, :] = (norm_two * gain_two + shift_two).astype(BF16)
         cot = cot_ref[at, :].astype(F32)
         grad_two = norm_backward(cot, gain_two, norm_two, inverse_two)
         g2_ref[at, :] = grad_two
-        low.append(grad_two.astype(BF16))
-        active.append(dot(low[-1], own_ref[...], 1, 1))
         small[0] = small[0] + column_sum(grad_two)
         small[1] = small[1] + column_sum(cot * norm_two)
         small[2] = small[2] + column_sum(cot)
-    dwr_scr[...] += dot(act_ref[me], jnp.concatenate(low, axis=0), 0, 0)
-    own = []
-    for at, part in zip(halves, active):
-        own.append((part * slope_ref[0, at, :].astype(F32)).astype(BF16))
-        small[3] = small[3] + column_sum(own[-1].astype(F32))
-    dwe_scr[...] += dot(
-        jnp.concatenate(normed_low, axis=0), jnp.concatenate(own, axis=0), 0, 0
-    )
+        return grad_two.astype(BF16), normed.astype(BF16)
+
+    first, second = halves
+    mixed = dot(act_ref[0, first, :], wr_ref[0], 1, 0)
+    for s in range(1, shards):
+        mixed = mixed + dot(act_ref[s, first, :], wr_ref[s], 1, 0)
+    later = None
+    parts = []
+    for s in range(shards):
+        product = dot(act_ref[s, second, :], wr_ref[s], 1, 0)
+        later = product if later is None else later + product
+        parts.append(norm_part(s * quarter, mixed[s * quarter : (s + 1) * quarter]))
+    low_a = jnp.concatenate([part[0] for part in parts], axis=0)
+    normed_a = jnp.concatenate([part[1] for part in parts], axis=0)
+    active_a = dot(low_a, own_ref[...], 1, 1)
+    parts = [norm_part(half + s * quarter, later[s * quarter : (s + 1) * quarter]) for s in (0, 1)]
+    dwr_scr[...] += dot(act_ref[me, first, :], low_a, 0, 0)
+    parts += [norm_part(half + s * quarter, later[s * quarter : (s + 1) * quarter]) for s in (2, 3)]
+    own_a = (active_a * slope_ref[0, first, :].astype(F32)).astype(BF16)
+    low_b = jnp.concatenate([part[0] for part in parts], axis=0)
+    normed_b = jnp.concatenate([part[1] for part in parts], axis=0)
+    active_b = dot(low_b, own_ref[...], 1, 1)
+    small[3] = small[3] + column_sum(own_a.astype(F32))
+    dwe_scr[...] += dot(normed_a, own_a, 0, 0)
+    own_b = (active_b * slope_ref[0, second, :].astype(F32)).astype(BF16)
+    dwr_scr[...] += dot(act_ref[me, second, :], low_b, 0, 0)
+    small[3] = small[3] + column_sum(own_b.astype(F32))
+    dwe_scr[...] += dot(normed_b, own_b, 0, 0)
     for n, part in enumerate(small):
         small_scr[n : n + 1] += part
 
@@ -972,7 +974,7 @@
 
         by_head = lambda w: w.T.reshape(heads, HD, width)
         own_heads = jnp.concatenate([by_head(w_query), by_head(w_key), by_head(w_value)], axis=1)
-        own_heads = jnp.concatenate([own_heads.reshape(3 * heads * HD, width), w_output])
+        own_heads = own_heads.reshape(3 * heads * HD, width)
         blank = jnp.zeros((width - 2 * heads * HD,), BF16)
         own_bias = jnp.stack(
             [jnp.concatenate([b_query, b_value, blank]), b_expand]
@@ -1009,31 +1011,39 @@
         biases = near[:, -own_bias.shape[0] :]
         all_biases = jnp.concatenate([own_bias[None], biases])
         near = near[:, : -own_bias.shape[0]]
-        cut = piece.shape[0] // 2
-        near_expand = swapped(piece_of(w_expand), near)
+        cut = piece.shape[0] // 16 * 8
+        share = jnp.concatenate([piece_of(w_expand), piece_of(w_output)])
+        near_expand = swapped(share, near)
         sides = both(near)
         corners = corner(*sides, cut)
         pieces = listed(near, *sides, *corners, cut)
-        near_reduce = swapped(piece_of(w_reduce), near_expand)
         sides_expand = both(after(near_expand, corners))
-        weights, all_output, qkv, ctx, aug = attend_peers(
+        near_reduce = swapped(piece_of(w_reduce), near_expand, [array for array, _, _ in pieces])
+        weights, qkv, ctx, aug = attend_peers(
             length, peers, place, inputs, after(biases, near_expand), qf, kf, pieces, own
         )
 
         sides_expand = after(sides_expand, ctx)
-        cut = width // GROUP // 2
+        cut = share.shape[0] // 2 // 16 * 16 + 16
         corners = corner(*sides_expand, cut)
         vectors = jnp.stack(
             [b_output, gain_attn, shift_attn, b_reduce, gain_ffn, shift_ffn]
             + [jnp.zeros((width,), BF16)] * 2
         ).astype(F32)
-        residual, low = add_attended(inputs, ctx, all_output, after(vectors, sides_expand))
-        near_reduce, corners = after((near_reduce, corners), low)
         pieces = listed(near_expand, *sides_expand, *corners, cut)
+        near_reduce = after(near_reduce, sides_expand)
+        diagonal = swapped(piece_of(w_reduce, 6), near_reduce)
         sides_reduce = both(near_reduce)
-        diagonal = swapped(piece_of(w_reduce, 6), near_reduce)
-        act, slope, all_expand = expand(
-            place, low, after(all_biases, near_reduce), w_expand, pieces, peers
+        residual, act, slope, all_expand, all_output = expand(
+            place,
+            inputs,
+            ctx,
+            after(all_biases, near_reduce),
+            vectors,
+            w_expand,
+            w_output,
+            pieces,
+            peers,
         )
         far_reduce = after((*sides_reduce, diagonal), act)
         pieces = with_core([(array, rel, 0) for rel, array in enumerate([near_reduce, *far_reduce])])

time: 346 us -> 337 us (0.974)
  Pallas kernels: 210 us -> 206 us
    pallas_call x1 -> x0, Pallas kernels: 8.65 us -> none  [add_attended(): pl.pallas_call(attended_kernel, grid=(tokens // block,), in_specs=[by_tok...]
    pallas_call x1, Pallas kernels: 26.7 us -> 33.2 us  [expand(): pl.pallas_call(lambda *refs: expand_kernel(spots, *refs), grid_spec=pltpu...]
    ppermute x3, waiting for transfers between devices: 5.02 us -> 0.01 us  [from_peers(): return jnp.stack([lax.ppermute(piece, 'mp', perm) for perm in rotations])]
    all_to_all x3, waiting for transfers between devices: 0.01 us -> 4.69 us  [swapped(): got = lax.all_to_all(after(copies, *ready), 'mp', 0, 0, tiled=True)]
  transfers between devices with their start and end apart: 52 -> 52, of which waited for: 14 -> 15; matrix products, arithmetic and copies ran while one was open for 6% -> 6% of each run, Pallas kernels for 49% -> 50%
where the time goes in v1:
time: 337 us; the launch traced here: 335 us
  Pallas kernels  206 us (61%)
  starting transfers between devices  52.1 us (15%)
  waiting for transfers between devices  42.2 us (13%)
  local copies, waits for them, and re-layouts  21.6 us (6%)
  other arithmetic  12.5 us (4%)
    ppermute x45, waiting for transfers between devices, flip(): return lax.ppermute(values, 'dp', [(i, i ^ bits) for i in range(lanes)])  37.5 us
    pallas_call x1, Pallas kernels, reduce(): pl.pallas_call(lambda *refs: reduce_kernel(spots, *refs), grid_spec=pltpu...  35.5 us
    pallas_call x1, Pallas kernels, back_to_context(): pl.pallas_call(return_kernel, grid_spec=pltpu.PrefetchScalarGridSpec(num_...  33.6 us
    pallas_call x1, Pallas kernels, expand(): pl.pallas_call(lambda *refs: expand_kernel(spots, *refs), grid_spec=pltpu...  33.2 us
    ppermute x45, starting transfers between devices, flip(): return lax.ppermute(values, 'dp', [(i, i ^ bits) for i in range(lanes)])  29.7 us
    pallas_call x1, Pallas kernels, attend_peers(): pl.pallas_call(lambda *refs: attend_peers_kernel(spots, *refs), grid_spec...  22.4 us
    pallas_call x2, Pallas kernels, attend_back(): pl.pallas_call(attend_back_kernel, grid_spec=pltpu.PrefetchScalarGridSpec...  21 us
    pallas_call x1, Pallas kernels, input_grads(): pl.pallas_call(input_grads_kernel, grid_spec=pltpu.PrefetchScalarGridSpec...  16.5 us
  transfers between devices with their start and end apart: 52, of which 15 were waited for; matrix products, arithmetic and copies ran while one was open for 6% of the time, Pallas kernels for 50%

profile of v1, /device:TPU:0, one launch (start us, length us, event | category | flops | bytes accessed | tf_op | source)
XLA Modules:
  0.0 335.5 jit_solution(5563397678824163918)
XLA Ops:
  3.6 5.1 %collective-permute-start.2 = (f32[80,768]{1,0:T(8,128)S(1)}, f32[80,768]{1,0:T(8,128)S(1)}, u32[]{:S(2)}, u32[]{:S(2)}) collective-permute-start(f32[80,768]{1,0:T(8,128)S(1)} %pad_maximum_fusion.5), channel_id=1, source_target_pairs={{0,3},{1,0},{2,1},{3,2},{4,7},{5,4},{6,5},{7,6},{8,11},{9,8},{10,9... | collective-permute-start | bytes 737288 | tf_op jit(solution)/shard_map/ppermute | solution.py:884
  13.2 7.7 %shift.1 = (bf16[2048,768]{1,0:T(8,128)(2,1)}, bf16[2048,768]{1,0:T(8,128)(2,1)}) custom-call(s32[13]{0:T(128)} %concatenate.37.place_ref.refs_0_, bf16[2048,768]{1,0:T(8,128)(2,1)} %bitcast.56, bf16[2048,768]{1,0:T(8,128)(2,1)} %bitcast.57), custom_call_target="tpu_custom_call" | custom-call | flops 3221225472 | bytes 12000000 | tf_op jit(solution)/shard_map/shift/pallas_call | solution.py:93
  20.9 8.4 %attend_own.1 = (bf16[2304,768]{1,0:T(8,128)(2,1)}, bf16[12,192,2048]{2,1,0:T(8,128)(2,1)}, bf16[12,64,2048]{2,1,0:T(8,128)(2,1)}, bf16[12,16,2048]{2,1,0:T(8,128)(2,1)}) custom-call(s32[13]{0:T(128)} %concatenate.37.place_ref.refs_0_, bf16[2048,768]{1,0:T(8,128)(2,1)} %get-tuple-element.86.x_ref.refs_1_.refs_0_, f32[8,768]{1,0:T(8,128)} %copy-done.18, ...), custom_call_target="tpu_custom_call" | custom-call | flops 5033164800 | bytes 12000000 | tf_op jit(solution)/shard_map/attend_own/pallas_call | solution.py:188
  31.9 4.1 %all-to-all-start = ((f32[4,120,768]{2,1,0:T(8,128)}), f32[4,120,768]{2,1,0:T(8,128)S(1)}, u32[]{:S(2)}, u32[]{:S(2)}) async-start(f32[4,120,768]{2,1,0:T(8,128)} %broadcast_in_dim.77), calls=%async_computation | async-start | bytes 2949120 | tf_op jit(solution)/shard_map/all_to_all | solution.py:888
  39.0 12.9 %collective-permute-done.4.refs_7_ = f32[3,72,768]{2,1,0:T(8,128)} collective-permute-done((f32[3,72,768]{2,1,0:T(8,128)S(1)}, f32[3,72,768]{2,1,0:T(8,128)}, u32[]{:S(2)}, u32[]{:S(2)}) %collective-permute-start.4) | collective-permute-done | bytes 663584 | tf_op jit(solution)/shard_map/ppermute | solution.py:881
  57.6 4.0 %collective-permute-done.10.refs_13_ = f32[3,40,768]{2,1,0:T(8,128)} collective-permute-done((f32[3,40,768]{2,1,0:T(8,128)S(1)}, f32[3,40,768]{2,1,0:T(8,128)}, u32[]{:S(2)}, u32[]{:S(2)}) %collective-permute-start.10) | collective-permute-done | bytes 368672 | tf_op jit(solution)/shard_map/ppermute | solution.py:881
  61.7 3.9 %collective-permute-done.8.refs_11_ = f32[3,32,768]{2,1,0:T(8,128)} collective-permute-done((f32[3,32,768]{2,1,0:T(8,128)S(1)}, f32[3,32,768]{2,1,0:T(8,128)}, u32[]{:S(2)}, u32[]{:S(2)}) %collective-permute-start.8) | collective-permute-done | bytes 294944 | tf_op jit(solution)/shard_map/ppermute | solution.py:881
  65.6 4.7 %all-to-all-done = f32[4,120,768]{2,1,0:T(8,128)S(1)} async-done(((f32[4,120,768]{2,1,0:T(8,128)}), f32[4,120,768]{2,1,0:T(8,128)S(1)}, u32[]{:S(2)}, u32[]{:S(2)}) %all-to-all-start) | async-done | bytes 1474592 | tf_op jit(solution)/shard_map/all_to_all | solution.py:888
  72.6 3.5 %all-to-all-start.1 = ((f32[4,96,768]{2,1,0:T(8,128)}), f32[4,96,768]{2,1,0:T(8,128)S(1)}, u32[]{:S(2)}, u32[]{:S(2)}) async-start(f32[4,96,768]{2,1,0:T(8,128)} %broadcast_in_dim.78), calls=%async_computation.1 | async-start | bytes 2359296 | tf_op jit(solution)/shard_map/all_to_all | solution.py:888
  79.8 22.4 %attend_peers.1 = (bf16[2304,768]{1,0:T(8,128)(2,1)}, bf16[12,192,2048]{2,1,0:T(8,128)(2,1)}, bf16[12,64,2048]{2,1,0:T(8,128)(2,1)}, bf16[12,16,2048]{2,1,0:T(8,128)(2,1)}) custom-call(s32[13]{0:T(128)} %concatenate.37.place_ref.refs_0_, ...), custom_call_target="tpu_custom_call", output_to_operand_aliasing={{0}: (15, {}), {1}: (16, {}), {2}: (17, {}), {3}: (18, {})} | custom-call | flops 15099494400 | bytes 30000000 | tf_op jit(solution)/shard_map/attend_peers/pallas_call | solution.py:233
  110.6 4.8 %all-to-all-start.2 = ((f32[4,96,768]{2,1,0:T(8,128)}), f32[4,96,768]{2,1,0:T(8,128)S(1)}, u32[]{:S(2)}, u32[]{:S(2)}) async-start(f32[4,96,768]{2,1,0:T(8,128)} %broadcast_in_dim.79), calls=%async_computation.2 | async-start | bytes 2359296 | tf_op jit(solution)/shard_map/all_to_all | solution.py:888
  118.1 5.1 %collective-permute-done.19.refs_15_ = f32[3,56,768]{2,1,0:T(8,128)} collective-permute-done((f32[3,56,768]{2,1,0:T(8,128)}, f32[3,56,768]{2,1,0:T(8,128)}, u32[]{:S(2)}, u32[]{:S(2)}) %collective-permute-start.19) | collective-permute-done | bytes 516128 | tf_op jit(solution)/shard_map/ppermute | solution.py:881
  126.1 33.2 %expand.1 = (f32[2048,768]{1,0:T(8,128)}, bf16[4,2048,768]{2,1,0:T(8,128)(2,1)}, bf16[4,2048,768]{2,1,0:T(8,128)(2,1)}, bf16[4,768,768]{2,1,0:T(8,128)(2,1)}, bf16[768,768]{1,0:T(8,128)(2,1)}) custom-call(s32[13]{0:T(128)} %concatenate.37.place_ref.refs_0_, bf16[2048,768]{1,0:T(8,128)(2,1)} %get-tuple-element.86.x_ref.refs_1_.refs_0_, ...), custom_call_target="tpu_custom_call" | custom-call | flops 12079595520 | bytes 40000000 | tf_op jit(solution)/shard_map/expand/pallas_call | solution.py:513
  165.6 35.5 %reduce.15 = (bf16[2048,768]{1,0:T(8,128)(2,1)}, f32[2048,768]{1,0:T(8,128)}, bf16[4,768,768]{2,1,0:T(8,128)(2,1)}, f32[4,192,768]{2,1,0:T(8,128)}, f32[4,192,768]{2,1,0:T(8,128)}, /*index=5*/f32[8,768]{1,0:T(8,128)}) custom-call(s32[13]{0:T(128)} %concatenate.37.place_ref.refs_0_, f32[2048,768]{1,0:T(8,128)} %get-tuple-element.101.refs_1_.sum_ref, ...), custom_call_target="tpu_custom_call" | custom-call | flops 16911433728 | bytes 40000000 | tf_op jit(solution)/shard_map/reduce/pallas_call | solution.py:646
  201.4 6.2 %unshift.1 = bf16[2048,768]{1,0:T(8,128)(2,1)} custom-call(s32[13]{0:T(128)} %concatenate.37.place_ref.refs_0_, bf16[2048,768]{1,0:T(8,128)(2,1)} %get-tuple-element.109.in_ref), custom_call_target="tpu_custom_call" | custom-call | flops 1610612736 | bytes 6000000 | tf_op jit(solution)/shard_map/unshift/pallas_call | solution.py:117
  207.7 3.4 %add.125 = f32[4,192,768]{2,1,0:T(8,128)} add(f32[4,192,768]{2,1,0:T(8,128)S(1)} %copy-done, f32[4,192,768]{2,1,0:T(8,128)} %collective-permute-done.27) | non-fusion elementwise | flops 589824 | bytes 7077888 | tf_op jit(solution)/shard_map/add | solution.py:1055
  211.0 3.9 %all-to-all-start.3 = ((f32[4,192,768]{2,1,0:T(8,128)}), f32[4,192,768]{2,1,0:T(8,128)S(1)}, u32[]{:S(2)}, u32[]{:S(2)}) async-start(f32[4,192,768]{2,1,0:T(8,128)} %add.125), calls=%async_computation.3 | async-start | bytes 4718592 | tf_op jit(solution)/shard_map/all_to_all | solution.py:917
  214.9 33.6 %back_to_context.1 = (f32[2048,768]{1,0:T(8,128)}, bf16[12,64,2048]{2,1,0:T(8,128)(2,1)}, f32[192,768]{1,0:T(8,128)}, f32[8,768]{1,0:T(8,128)}) custom-call(s32[13]{0:T(128)} %concatenate.37.place_ref.refs_0_, f32[2048,768]{1,0:T(8,128)} %get-tuple-element.101.refs_1_.sum_ref, f32[2048,768]{1,0:T(8,128)} %get-tuple-element.110.g2_ref, ...), custom_call_target="tpu_custom_call" | custom-call | flops 21743271936 | bytes 40000000 | tf_op jit(solution)/shard_map/back_to_context/pallas_call | solution.py:737
  252.1 11.8 %attend_back_own.1 = (bf16[12,192,2048]{2,1,0:T(8,128)(2,1)}, f32[4,112,768]{2,1,0:T(8,128)}, f32[4,112,768]{2,1,0:T(8,128)}) custom-call(s32[13]{0:T(128)} %concatenate.37.place_ref.refs_0_, bf16[12,192,2048]{2,1,0:T(8,128)(2,1)} %get-tuple-element.119.qkv_ref, bf16[12,64,2048]{2,1,0:T(8,128)(2,1)} %get-tuple-element.94.refs_2_.ctx_ref, ...), custom_call_target="tpu_custom_call" | custom-call | flops 5838471168 | bytes 12000000 | tf_op jit(solution)/shard_map/attend_back_own/pallas_call | solution.py:353
  271.9 8.0 %attend_back.2.old_ref = bf16[12,192,2048]{2,1,0:T(8,128)(2,1)} custom-call(s32[13]{0:T(128)} %concatenate.37.place_ref.refs_0_, bf16[12,192,2048]{2,1,0:T(8,128)(2,1)} %get-tuple-element.119.qkv_ref, bf16[12,64,2048]{2,1,0:T(8,128)(2,1)} %get-tuple-element.94.refs_2_.ctx_ref, ...), custom_call_target="tpu_custom_call", output_to_operand_aliasing={{}: (6, {})} | custom-call | flops 4026531840 | bytes 12000000 | tf_op jit(solution)/shard_map/attend_back/pallas_call | solution.py:392
  284.9 13.1 %attend_back.3.grad_ref = bf16[12,192,2048]{2,1,0:T(8,128)(2,1)} custom-call(s32[13]{0:T(128)} %concatenate.37.place_ref.refs_0_, bf16[12,192,2048]{2,1,0:T(8,128)(2,1)} %get-tuple-element.119.qkv_ref, bf16[12,64,2048]{2,1,0:T(8,128)(2,1)} %get-tuple-element.94.refs_2_.ctx_ref, ...), custom_call_target="tpu_custom_call", output_to_operand_aliasing={{}: (6, {})} | custom-call | flops 8053063680 | bytes 12000000 | tf_op jit(solution)/shard_map/attend_back/pallas_call | solution.py:392
  303.1 16.5 %input_grads.1 = bf16[2048,768]{1,0:T(8,128)(2,1)} custom-call(s32[13]{0:T(128)} %concatenate.37.place_ref.refs_0_, f32[2048,768]{1,0:T(8,128)} %get-tuple-element.142.g1_ref, bf16[12,192,2048]{2,1,0:T(8,128)(2,1)} %attend_back.3.grad_ref, bf16[2304,768]{1,0:T(8,128)(2,1)} %get-tuple-element.143.w_ref), custom_call_target="tpu_custom_call" | custom-call | flops 8858370048 | bytes 20000000 | tf_op jit(solution)/shard_map/input_grads/pallas_call | solution.py:852
  320.8 5.4 %spread.1 = (f32[768,768]{1,0:T(8,128)}, f32[768,768]{1,0:T(8,128)}) custom-call(s32[13]{0:T(128)} %concatenate.37.place_ref.refs_0_, f32[1,192,768]{2,1,0:T(8,128)} %bitcast.44, f32[1,192,768]{2,1,0:T(8,128)} %collective-permute-done.36.refs_2_, f32[1,192,768]{2,1,0:T(8,128)} %collective-permute-done.28.refs_3_, ...), custom_call_target="tpu_custom_call" | custom-call | bytes 10000000 | tf_op jit(solution)/shard_map/spread/pallas_call | solution.py:787
  327.9 4.0 %spread_late.1 = (f32[192,768]{1,0:T(8,128)}, f32[192,768]{1,0:T(8,128)}, f32[192,768]{1,0:T(8,128)}, f32[192,768]{1,0:T(8,128)}, f32[16,768]{1,0:T(8,128)}) custom-call(s32[13]{0:T(128)} %concatenate.37.place_ref.refs_0_, f32[112,768]{1,0:T(8,128)} %copy-done.2, f32[112,768]{1,0:T(8,128)} %copy-done.11, f32[112,768]{1,0:T(8,128)} %copy-done.10, ...), custom_call_target="tpu_custom_call" | custom-call | bytes 5505024 | tf_op jit(solution)/shard_map/spread_late/pallas_call | solution.py:825
  (222 shorter events, 73.0 us)
Async XLA Ops:
  3.6 26.9 %collective-permute-start.2 = (f32[80,768]{1,0:T(8,128)S(1)}, f32[80,768]{1,0:T(8,128)S(1)}, u32[]{:S(2)}, u32[]{:S(2)}) collective-permute-start(f32[80,768]{1,0:T(8,128)S(1)} %pad_maximum_fusion.5), channel_id=1, source_target_pairs={{0,3},{1,0},{2,1},{3,2},{4,7},{5,4},{6,5},{7,6},{8,11},{9,8},{10,9... | collective-permute-start | bytes 737288 | tf_op jit(solution)/shard_map/ppermute | solution.py:884
  8.7 21.8 %collective-permute-start.1 = (f32[80,768]{1,0:T(8,128)S(1)}, f32[80,768]{1,0:T(8,128)S(1)}, u32[]{:S(2)}, u32[]{:S(2)}) collective-permute-start(f32[80,768]{1,0:T(8,128)S(1)} %pad_maximum_fusion.5), channel_id=1, source_target_pairs={{0,2},{1,3},{2,0},{3,1},{4,6},{5,7},{6,4},{7,5},{8,10},{9,11},{10,... | collective-permute-start | bytes 737288 | tf_op jit(solution)/shard_map/ppermute | solution.py:884
  8.7 21.8 %collective-permute-start = (f32[80,768]{1,0:T(8,128)S(1)}, f32[80,768]{1,0:T(8,128)S(1)}, u32[]{:S(2)}, u32[]{:S(2)}) collective-permute-start(f32[80,768]{1,0:T(8,128)S(1)} %pad_maximum_fusion.5), channel_id=1, source_target_pairs={{0,1},{1,2},{2,3},{3,0},{4,5},{5,6},{6,7},{7,4},{8,9},{9,10},{10,1... | collective-permute-start | bytes 737288 | tf_op jit(solution)/shard_map/ppermute | solution.py:884
  31.9 38.4 %all-to-all-start = ((f32[4,120,768]{2,1,0:T(8,128)}), f32[4,120,768]{2,1,0:T(8,128)S(1)}, u32[]{:S(2)}, u32[]{:S(2)}) async-start(f32[4,120,768]{2,1,0:T(8,128)} %broadcast_in_dim.77), calls=%async_computation | async-start | bytes 2949120 | tf_op jit(solution)/shard_map/all_to_all | solution.py:888
  37.5 17.0 %collective-permute-start.6 = (f32[3,72,768]{2,1,0:T(8,128)S(1)}, f32[3,72,768]{2,1,0:T(8,128)}, u32[]{:S(2)}, u32[]{:S(2)}) collective-permute-start(f32[3,72,768]{2,1,0:T(8,128)S(1)} %slice.76.refs_5_), channel_id=1, source_target_pairs={{0,16},{4,20},{8,24},{12,28},{16,0},{20,4},{24,8},{28,12},{1,17},{... | collective-permute-start | bytes 1990664 | tf_op jit(solution)/shard_map/ppermute | solution.py:881
  54.5 17.0 %collective-permute-start.3 = (f32[3,72,768]{2,1,0:T(8,128)S(1)}, f32[3,72,768]{2,1,0:T(8,128)}, u32[]{:S(2)}, u32[]{:S(2)}) collective-permute-start(f32[3,72,768]{2,1,0:T(8,128)S(1)} %slice.76.refs_5_), channel_id=1, source_target_pairs={{0,4},{4,0},{8,12},{12,8},{16,20},{20,16},{24,28},{28,24},{1,5},{5... | collective-permute-start | bytes 1990664 | tf_op jit(solution)/shard_map/ppermute | solution.py:881
  54.5 17.0 %collective-permute-start.7 = (f32[3,72,768]{2,1,0:T(8,128)}, f32[3,72,768]{2,1,0:T(8,128)}, u32[]{:S(2)}, u32[]{:S(2)}) collective-permute-start(f32[3,72,768]{2,1,0:T(8,128)} %collective-permute-done.6.refs_9_), channel_id=1, source_target_pairs={{0,4},{4,0},{8,12},{12,8},{16,20},{20,16},{24,28},{28,24},{1,5},{5... | collective-permute-start | bytes 1990664 | tf_op jit(solution)/shard_map/ppermute | solution.py:881
  72.6 36.6 %all-to-all-start.1 = ((f32[4,96,768]{2,1,0:T(8,128)}), f32[4,96,768]{2,1,0:T(8,128)S(1)}, u32[]{:S(2)}, u32[]{:S(2)}) async-start(f32[4,96,768]{2,1,0:T(8,128)} %broadcast_in_dim.78), calls=%async_computation.1 | async-start | bytes 2359296 | tf_op jit(solution)/shard_map/all_to_all | solution.py:888
  76.8 25.7 %collective-permute-start.13 = (f32[3,120,768]{2,1,0:T(8,128)}, f32[3,120,768]{2,1,0:T(8,128)}, u32[]{:S(2)}, u32[]{:S(2)}) collective-permute-start(f32[3,120,768]{2,1,0:T(8,128)} %pad_maximum_fusion.refs_7_), channel_id=1, source_target_pairs={{0,16},{4,20},{8,24},{12,28},{16,0},{20,4},{24,8},{28,12},{1,17},{... | collective-permute-start | bytes 3317768 | tf_op jit(solution)/shard_map/ppermute | solution.py:881
  78.3 25.4 %collective-permute-start.12 = (f32[3,120,768]{2,1,0:T(8,128)}, f32[3,120,768]{2,1,0:T(8,128)}, u32[]{:S(2)}, u32[]{:S(2)}) collective-permute-start(f32[3,120,768]{2,1,0:T(8,128)} %pad_maximum_fusion.refs_7_), channel_id=1, source_target_pairs={{0,8},{4,12},{8,0},{12,4},{16,24},{20,28},{24,16},{28,20},{1,9},{5... | collective-permute-start | bytes 3317768 | tf_op jit(solution)/shard_map/ppermute | solution.py:881
  106.4 18.5 %collective-permute-start.14 = (f32[3,120,768]{2,1,0:T(8,128)}, f32[3,120,768]{2,1,0:T(8,128)}, u32[]{:S(2)}, u32[]{:S(2)}) collective-permute-start(f32[3,120,768]{2,1,0:T(8,128)} %pad_maximum_fusion.refs_7_), channel_id=1, source_target_pairs={{0,4},{4,0},{8,12},{12,8},{16,20},{20,16},{24,28},{28,24},{1,5},{5... | collective-permute-start | bytes 3317768 | tf_op jit(solution)/shard_map/ppermute | solution.py:881
  106.4 19.5 %collective-permute-start.15 = (f32[3,120,768]{2,1,0:T(8,128)}, f32[3,120,768]{2,1,0:T(8,128)}, u32[]{:S(2)}, u32[]{:S(2)}) collective-permute-start(f32[3,120,768]{2,1,0:T(8,128)} %collective-permute-done.12.refs_9_), channel_id=1, source_target_pairs={{0,4},{4,0},{8,12},{12,8},{16,20},{20,16},{24,28},{28,24},{1,5},{5... | collective-permute-start | bytes 3317768 | tf_op jit(solution)/shard_map/ppermute | solution.py:881
  106.9 19.0 %collective-permute-start.16 = (f32[3,120,768]{2,1,0:T(8,128)}, f32[3,120,768]{2,1,0:T(8,128)}, u32[]{:S(2)}, u32[]{:S(2)}) collective-permute-start(f32[3,120,768]{2,1,0:T(8,128)} %collective-permute-done.13.refs_11_), channel_id=1, source_target_pairs={{0,4},{4,0},{8,12},{12,8},{16,20},{20,16},{24,28},{28,24},{1,5},{5... | collective-permute-start | bytes 3317768 | tf_op jit(solution)/shard_map/ppermute | solution.py:881
  110.6 48.8 %all-to-all-start.2 = ((f32[4,96,768]{2,1,0:T(8,128)}), f32[4,96,768]{2,1,0:T(8,128)S(1)}, u32[]{:S(2)}, u32[]{:S(2)}) async-start(f32[4,96,768]{2,1,0:T(8,128)} %broadcast_in_dim.79), calls=%async_computation.2 | async-start | bytes 2359296 | tf_op jit(solution)/shard_map/all_to_all | solution.py:888
  124.8 34.7 %collective-permute-start.23 = (f32[3,96,768]{2,1,0:T(8,128)S(1)}, f32[3,96,768]{2,1,0:T(8,128)S(1)}, u32[]{:S(2)}, u32[]{:S(2)}) collective-permute-start(f32[3,96,768]{2,1,0:T(8,128)S(1)} %pad_maximum_fusion.2.refs_7_), channel_id=1, source_target_pairs={{0,16},{4,20},{8,24},{12,28},{16,0},{20,4},{24,8},{28,12},{1,17},{... | collective-permute-start | bytes 2654216 | tf_op jit(solution)/shard_map/ppermute | solution.py:881
  125.3 34.2 %collective-permute-start.22 = (f32[3,96,768]{2,1,0:T(8,128)S(1)}, f32[3,96,768]{2,1,0:T(8,128)}, u32[]{:S(2)}, u32[]{:S(2)}) collective-permute-start(f32[3,96,768]{2,1,0:T(8,128)S(1)} %pad_maximum_fusion.2.refs_7_), channel_id=1, source_target_pairs={{0,8},{4,12},{8,0},{12,4},{16,24},{20,28},{24,16},{28,20},{1,9},{5... | collective-permute-start | bytes 2654216 | tf_op jit(solution)/shard_map/ppermute | solution.py:881
  125.9 34.6 %collective-permute-start.21 = (f32[3,96,768]{2,1,0:T(8,128)S(1)}, f32[3,96,768]{2,1,0:T(8,128)}, u32[]{:S(2)}, u32[]{:S(2)}) collective-permute-start(f32[3,96,768]{2,1,0:T(8,128)S(1)} %pad_maximum_fusion.2.refs_7_), channel_id=1, source_target_pairs={{0,4},{4,0},{8,12},{12,8},{16,20},{20,16},{24,28},{28,24},{1,5},{5... | collective-permute-start | bytes 2654216 | tf_op jit(solution)/shard_map/ppermute | solution.py:881
  211.0 37.5 %all-to-all-start.3 = ((f32[4,192,768]{2,1,0:T(8,128)}), f32[4,192,768]{2,1,0:T(8,128)S(1)}, u32[]{:S(2)}, u32[]{:S(2)}) async-start(f32[4,192,768]{2,1,0:T(8,128)} %add.125), calls=%async_computation.3 | async-start | bytes 4718592 | tf_op jit(solution)/shard_map/all_to_all | solution.py:917
  280.9 17.1 %collective-permute-start.33 = (f32[112,768]{1,0:T(8,128)}, f32[112,768]{1,0:T(8,128)S(1)}, u32[]{:S(2)}, u32[]{:S(2)}) collective-permute-start(f32[112,768]{1,0:T(8,128)} %get-tuple-element.163), channel_id=1, source_target_pairs={{0,24},{4,28},{8,16},{12,20},{16,8},{20,12},{24,0},{28,4},{1,25},{... | collective-permute-start | bytes 1032200 | tf_op jit(solution)/shard_map/ppermute | solution.py:881
  284.4 18.7 %collective-permute-start.39 = (f32[1,96,768]{2,1,0:T(8,128)}, f32[1,96,768]{2,1,0:T(8,128)S(1)}, u32[]{:S(2)}, u32[]{:S(2)}) collective-permute-start(f32[1,96,768]{2,1,0:T(8,128)} %collective-permute-done.34.refs_7_), channel_id=1, source_target_pairs={{0,4},{4,0},{8,12},{12,8},{16,20},{20,16},{24,28},{28,24},{1,5},{5... | collective-permute-start | bytes 884744 | tf_op jit(solution)/shard_map/ppermute | solution.py:881
  284.4 18.7 %collective-permute-start.40 = (f32[1,96,768]{2,1,0:T(8,128)}, f32[1,96,768]{2,1,0:T(8,128)S(1)}, u32[]{:S(2)}, u32[]{:S(2)}) collective-permute-start(f32[1,96,768]{2,1,0:T(8,128)} %collective-permute-done.35.refs_9_), channel_id=1, source_target_pairs={{0,4},{4,0},{8,12},{12,8},{16,20},{20,16},{24,28},{28,24},{1,5},{5... | collective-permute-start | bytes 884744 | tf_op jit(solution)/shard_map/ppermute | solution.py:881
  299.5 20.1 %collective-permute-start.43 = (f32[112,768]{1,0:T(8,128)S(1)}, f32[112,768]{1,0:T(8,128)S(1)}, u32[]{:S(2)}, u32[]{:S(2)}) collective-permute-start(f32[112,768]{1,0:T(8,128)S(1)} %add_add_fusion.refs_1_), channel_id=1, source_target_pairs={{0,24},{4,28},{8,16},{12,20},{16,8},{20,12},{24,0},{28,4},{1,25},{... | collective-permute-start | bytes 1032200 | tf_op jit(solution)/shard_map/ppermute | solution.py:881
  301.0 18.6 %collective-permute-start.42 = (f32[112,768]{1,0:T(8,128)S(1)}, f32[112,768]{1,0:T(8,128)S(1)}, u32[]{:S(2)}, u32[]{:S(2)}) collective-permute-start(f32[112,768]{1,0:T(8,128)S(1)} %add_add_fusion.refs_1_), channel_id=1, source_target_pairs={{0,16},{4,20},{8,24},{12,28},{16,0},{20,4},{24,8},{28,12},{1,17},{... | collective-permute-start | bytes 1032200 | tf_op jit(solution)/shard_map/ppermute | solution.py:881
  301.6 18.0 %collective-permute-start.41 = (f32[112,768]{1,0:T(8,128)S(1)}, f32[112,768]{1,0:T(8,128)S(1)}, u32[]{:S(2)}, u32[]{:S(2)}) collective-permute-start(f32[112,768]{1,0:T(8,128)S(1)} %add_add_fusion.refs_1_), channel_id=1, source_target_pairs={{0,8},{4,12},{8,0},{12,4},{16,24},{20,28},{24,16},{28,20},{1,9},{5... | collective-permute-start | bytes 1032200 | tf_op jit(solution)/shard_map/ppermute | solution.py:881
  (60 other events, 605.2 us)

commit v2 on v1

--- a/solution.py
+++ b/solution.py
@@ -497,7 +497,7 @@
             slope_ref[s, at, :] = slope.astype(BF16)
         return carry
 
-    lax.fori_loop(0, shards, shard_step, 0)
+    lax.fori_loop(0, shards, shard_step, 0, unroll=2)
 
 
 def expand(place, inputs, ctx, biases, vectors, own, own_wo, pieces, shards):
@@ -616,16 +616,16 @@
     @pl.when(step == pl.num_programs(0) - 1)
     def _():
         copies = [kept]
-        for plane in range(4):
-            for ref, core in ((send_ref, place_ref[1]), (mine_ref, place_ref[0])):
-                owner = 2 * plane + lax.rem(core, 2)
+        for rel in range(4):
+            for source, ref in ((1, send_ref), (0, mine_ref)):
+                owner = place_ref[2 * rel + source]
                 top = 0
                 for scr in (dwe_scr, dwr_scr):
                     size = scr.shape[0] // GROUP
                     start = pl.multiple_of(owner * size, 8)
                     copy = pltpu.make_async_copy(
                         scr.at[pl.ds(start, size), :],
-                        ref.at[plane, top : top + size, :],
+                        ref.at[rel, top : top + size, :],
                         sems.at[len(copies)],
                     )
                     copy.start()
@@ -910,11 +910,6 @@
             out.append((array, 2 * rel, offset))
             out.append((flip(array, 1), 2 * rel + 1, offset))
         return out
-
-    planes = [[g + c + i for i in (0, 2, 4, 6)] for g in range(0, lanes, GROUP) for c in (0, 1)]
-
-    def swap_plane(values):
-        return lax.all_to_all(values, "dp", 0, 0, tiled=True, axis_index_groups=planes)
 
     def sum_groups(total):
         step = GROUP
@@ -1052,8 +1047,8 @@
         )
         got = flip(send, 1)
         output = unshift(place, length, shifted)
-        chip = mine + after(got, output)
-        early = swap_plane(chip)
+        chip = partial_sums(mine, got, output)
+        early = exchange(chip)
         grad_one, dctx, dwo, small = back_to_context(
             place,
             residual,
@@ -1065,8 +1060,7 @@
             all_output,
             after(vectors, chip),
         )
-        cut = width // GROUP
-        early = sum_groups(jnp.sum(after(early, grad_one), axis=0))[None]
+        early = total_of(chip[0], early, grad_one)[None]
         sides = both(early)
         dqkv, mine, send = attend_back_own(
             length, place, qkv, ctx, aug, dctx, after(kf, early), inputs, dwo, small, small_one
@@ -1075,19 +1069,18 @@
         dqkv = attend_back(
             length, peers, 1, 1, place, qkv, ctx, aug, dctx, after(kf, sides), dqkv
         )
-        corners = corner(*sides, cut)
+        across = flip(after(early, sides), 6)
         beside = [flip(array, 1) for array in (early, *sides)]
         parts = partial_sums(mine, got, dqkv)
         rest = exchange(parts)
-        corners, beside, kept = after((corners, beside, kf), parts)
+        across, beside, kept = after((across, beside, kf), parts)
         dqkv = attend_back(length, peers, 2, peers - 2, place, qkv, ctx, aug, dctx, kept, dqkv)
         total = total_of(parts[0], rest, dqkv)
         second = [total] + exchange([None] + [total] * 3)
-        beside += [flip(array, 1) for array in corners]
+        beside.append(flip(across, 1))
         pieces = []
-        spots = ((0, 0), (2, 0), (4, 0), (6, 0), (6, cut))
-        for near, far, (index, top) in zip((early, *sides, *corners), beside, spots):
-            pieces += [(near, index, top), (far, index + 1, top)]
+        for rel, (near, far) in enumerate(zip((early, *sides, across), beside)):
+            pieces += [(near, 2 * rel, 0), (far, 2 * rel + 1, 0)]
         grad_one = after(grad_one, total, beside)
         grad_tokens = input_grads(place, length, grad_one, dqkv, weights)
         second = finish(second, grad_tokens)

time: 337 us -> 331 us (0.982)
    all_to_all x1 -> x0, starting transfers between devices: 3.85 us -> none  [swap_plane(): lax.all_to_all(values, 'dp', 0, 0, tiled=True, axis_index_groups=planes)]
    slice x6 -> x4, local copies, waits for them, and re-layouts: 8.33 us -> 4.95 us  [corner(): return (flip(by_y[:, :cut], 2), flip(by_x[:, cut:], 4))]
    ppermute x45 -> x46, starting transfers between devices: 29.7 us -> 31.7 us  [flip(): return lax.ppermute(values, 'dp', [(i, i ^ bits) for i in range(lanes)])]
    ppermute x45 -> x46, waiting for transfers between devices: 37.5 us -> 39.1 us  [flip(): return lax.ppermute(values, 'dp', [(i, i ^ bits) for i in range(lanes)])]
  transfers between devices with their start and end apart: 52 -> 52, of which waited for: 15 -> 14; matrix products, arithmetic and copies ran while one was open for 6% -> 5% of each run, Pallas kernels for 50% -> 50%
where the time goes in v2:
time: 331 us; the launch traced here: 330 us
  Pallas kernels  204 us (62%)
  starting transfers between devices  50.2 us (15%)
  waiting for transfers between devices  43.8 us (13%)
  local copies, waits for them, and re-layouts  18.3 us (6%)
  other arithmetic  11.8 us (4%)
    ppermute x46, waiting for transfers between devices, flip(): return lax.ppermute(values, 'dp', [(i, i ^ bits) for i in range(lanes)])  39.1 us
    pallas_call x1, Pallas kernels, reduce(): pl.pallas_call(lambda *refs: reduce_kernel(spots, *refs), grid_spec=pltpu...  35.5 us
    pallas_call x1, Pallas kernels, back_to_context(): pl.pallas_call(return_kernel, grid_spec=pltpu.PrefetchScalarGridSpec(num_...  33.6 us
    pallas_call x1, Pallas kernels, expand(): pl.pallas_call(lambda *refs: expand_kernel(spots, *refs), grid_spec=pltpu...  31.9 us
    ppermute x46, starting transfers between devices, flip(): return lax.ppermute(values, 'dp', [(i, i ^ bits) for i in range(lanes)])  31.7 us
    pallas_call x1, Pallas kernels, attend_peers(): pl.pallas_call(lambda *refs: attend_peers_kernel(spots, *refs), grid_spec...  22.3 us
    pallas_call x2, Pallas kernels, attend_back(): pl.pallas_call(attend_back_kernel, grid_spec=pltpu.PrefetchScalarGridSpec...  21 us
    pallas_call x1, Pallas kernels, input_grads(): pl.pallas_call(input_grads_kernel, grid_spec=pltpu.PrefetchScalarGridSpec...  16.2 us
  transfers between devices with their start and end apart: 52, of which 14 were waited for; matrix products, arithmetic and copies ran while one was open for 5% of the time, Pallas kernels for 50%

profile of v2, /device:TPU:0, one launch (start us, length us, event | category | flops | bytes accessed | tf_op | source)
XLA Modules:
  0.0 329.8 jit_solution(5925626076169545665)
XLA Ops:
  3.6 5.1 %collective-permute-start.2 = (f32[80,768]{1,0:T(8,128)S(1)}, f32[80,768]{1,0:T(8,128)S(1)}, u32[]{:S(2)}, u32[]{:S(2)}) collective-permute-start(f32[80,768]{1,0:T(8,128)S(1)} %pad_maximum_fusion.5), channel_id=1, source_target_pairs={{0,3},{1,0},{2,1},{3,2},{4,7},{5,4},{6,5},{7,6},{8,11},{9,8},{10,9... | collective-permute-start | bytes 737288 | tf_op jit(solution)/shard_map/ppermute | solution.py:884
  13.2 7.7 %shift.1 = (bf16[2048,768]{1,0:T(8,128)(2,1)}, bf16[2048,768]{1,0:T(8,128)(2,1)}) custom-call(s32[13]{0:T(128)} %concatenate.37.place_ref.refs_0_, bf16[2048,768]{1,0:T(8,128)(2,1)} %bitcast.61, bf16[2048,768]{1,0:T(8,128)(2,1)} %bitcast.62), custom_call_target="tpu_custom_call" | custom-call | flops 3221225472 | bytes 12000000 | tf_op jit(solution)/shard_map/shift/pallas_call | solution.py:93
  20.9 8.4 %attend_own.1 = (bf16[2304,768]{1,0:T(8,128)(2,1)}, bf16[12,192,2048]{2,1,0:T(8,128)(2,1)}, bf16[12,64,2048]{2,1,0:T(8,128)(2,1)}, bf16[12,16,2048]{2,1,0:T(8,128)(2,1)}) custom-call(s32[13]{0:T(128)} %concatenate.37.place_ref.refs_0_, bf16[2048,768]{1,0:T(8,128)(2,1)} %get-tuple-element.88.x_ref.refs_1_.refs_0_, f32[8,768]{1,0:T(8,128)} %copy-done.17, ...), custom_call_target="tpu_custom_call" | custom-call | flops 5033164800 | bytes 12000000 | tf_op jit(solution)/shard_map/attend_own/pallas_call | solution.py:188
  31.9 4.1 %all-to-all-start = ((f32[4,120,768]{2,1,0:T(8,128)}), f32[4,120,768]{2,1,0:T(8,128)S(1)}, u32[]{:S(2)}, u32[]{:S(2)}) async-start(f32[4,120,768]{2,1,0:T(8,128)} %broadcast_in_dim.77), calls=%async_computation | async-start | bytes 2949120 | tf_op jit(solution)/shard_map/all_to_all | solution.py:888
  39.0 12.9 %collective-permute-done.4.refs_7_ = f32[3,72,768]{2,1,0:T(8,128)} collective-permute-done((f32[3,72,768]{2,1,0:T(8,128)S(1)}, f32[3,72,768]{2,1,0:T(8,128)}, u32[]{:S(2)}, u32[]{:S(2)}) %collective-permute-start.4) | collective-permute-done | bytes 663584 | tf_op jit(solution)/shard_map/ppermute | solution.py:881
  57.6 4.0 %collective-permute-done.10.refs_13_ = f32[3,40,768]{2,1,0:T(8,128)} collective-permute-done((f32[3,40,768]{2,1,0:T(8,128)S(1)}, f32[3,40,768]{2,1,0:T(8,128)}, u32[]{:S(2)}, u32[]{:S(2)}) %collective-permute-start.10) | collective-permute-done | bytes 368672 | tf_op jit(solution)/shard_map/ppermute | solution.py:881
  61.6 3.9 %collective-permute-done.8.refs_11_ = f32[3,32,768]{2,1,0:T(8,128)} collective-permute-done((f32[3,32,768]{2,1,0:T(8,128)S(1)}, f32[3,32,768]{2,1,0:T(8,128)}, u32[]{:S(2)}, u32[]{:S(2)}) %collective-permute-start.8) | collective-permute-done | bytes 294944 | tf_op jit(solution)/shard_map/ppermute | solution.py:881
  65.6 4.7 %all-to-all-done = f32[4,120,768]{2,1,0:T(8,128)S(1)} async-done(((f32[4,120,768]{2,1,0:T(8,128)}), f32[4,120,768]{2,1,0:T(8,128)S(1)}, u32[]{:S(2)}, u32[]{:S(2)}) %all-to-all-start) | async-done | bytes 1474592 | tf_op jit(solution)/shard_map/all_to_all | solution.py:888
  72.6 3.5 %all-to-all-start.1 = ((f32[4,96,768]{2,1,0:T(8,128)}), f32[4,96,768]{2,1,0:T(8,128)S(1)}, u32[]{:S(2)}, u32[]{:S(2)}) async-start(f32[4,96,768]{2,1,0:T(8,128)} %broadcast_in_dim.78), calls=%async_computation.1 | async-start | bytes 2359296 | tf_op jit(solution)/shard_map/all_to_all | solution.py:888
  79.8 22.3 %attend_peers.1 = (bf16[2304,768]{1,0:T(8,128)(2,1)}, bf16[12,192,2048]{2,1,0:T(8,128)(2,1)}, bf16[12,64,2048]{2,1,0:T(8,128)(2,1)}, bf16[12,16,2048]{2,1,0:T(8,128)(2,1)}) custom-call(s32[13]{0:T(128)} %concatenate.37.place_ref.refs_0_, ...), custom_call_target="tpu_custom_call", output_to_operand_aliasing={{0}: (15, {}), {1}: (16, {}), {2}: (17, {}), {3}: (18, {})} | custom-call | flops 15099494400 | bytes 30000000 | tf_op jit(solution)/shard_map/attend_peers/pallas_call | solution.py:233
  110.6 4.8 %all-to-all-start.2 = ((f32[4,96,768]{2,1,0:T(8,128)}), f32[4,96,768]{2,1,0:T(8,128)S(1)}, u32[]{:S(2)}, u32[]{:S(2)}) async-start(f32[4,96,768]{2,1,0:T(8,128)} %broadcast_in_dim.79), calls=%async_computation.2 | async-start | bytes 2359296 | tf_op jit(solution)/shard_map/all_to_all | solution.py:888
  118.1 5.1 %collective-permute-done.19.refs_15_ = f32[3,56,768]{2,1,0:T(8,128)} collective-permute-done((f32[3,56,768]{2,1,0:T(8,128)}, f32[3,56,768]{2,1,0:T(8,128)}, u32[]{:S(2)}, u32[]{:S(2)}) %collective-permute-start.19) | collective-permute-done | bytes 516128 | tf_op jit(solution)/shard_map/ppermute | solution.py:881
  126.1 31.9 %expand.1 = (f32[2048,768]{1,0:T(8,128)}, bf16[4,2048,768]{2,1,0:T(8,128)(2,1)}, bf16[4,2048,768]{2,1,0:T(8,128)(2,1)}, bf16[4,768,768]{2,1,0:T(8,128)(2,1)}, bf16[768,768]{1,0:T(8,128)(2,1)}) custom-call(s32[13]{0:T(128)} %concatenate.37.place_ref.refs_0_, bf16[2048,768]{1,0:T(8,128)(2,1)} %get-tuple-element.88.x_ref.refs_1_.refs_0_, ...), custom_call_target="tpu_custom_call" | custom-call | flops 12079595520 | bytes 40000000 | tf_op jit(solution)/shard_map/expand/pallas_call | solution.py:513
  164.3 35.5 %reduce.15 = (bf16[2048,768]{1,0:T(8,128)(2,1)}, f32[2048,768]{1,0:T(8,128)}, bf16[4,768,768]{2,1,0:T(8,128)(2,1)}, f32[4,192,768]{2,1,0:T(8,128)}, f32[4,192,768]{2,1,0:T(8,128)}, /*index=5*/f32[8,768]{1,0:T(8,128)}) custom-call(s32[13]{0:T(128)} %concatenate.37.place_ref.refs_0_, f32[2048,768]{1,0:T(8,128)} %get-tuple-element.103.refs_1_.sum_ref, ...), custom_call_target="tpu_custom_call" | custom-call | flops 16911433728 | bytes 40000000 | tf_op jit(solution)/shard_map/reduce/pallas_call | solution.py:646
  200.1 6.4 %unshift.1 = bf16[2048,768]{1,0:T(8,128)(2,1)} custom-call(s32[13]{0:T(128)} %concatenate.37.place_ref.refs_0_, bf16[2048,768]{1,0:T(8,128)(2,1)} %get-tuple-element.111.in_ref), custom_call_target="tpu_custom_call" | custom-call | flops 1610612736 | bytes 6000000 | tf_op jit(solution)/shard_map/unshift/pallas_call | solution.py:117
  206.6 2.7 add_bitcast_fusion.1
  212.8 33.6 %back_to_context.1 = (f32[2048,768]{1,0:T(8,128)}, bf16[12,64,2048]{2,1,0:T(8,128)(2,1)}, f32[192,768]{1,0:T(8,128)}, f32[8,768]{1,0:T(8,128)}) custom-call(s32[13]{0:T(128)} %concatenate.37.place_ref.refs_0_, f32[2048,768]{1,0:T(8,128)} %get-tuple-element.103.refs_1_.sum_ref, f32[2048,768]{1,0:T(8,128)} %get-tuple-element.112.g2_ref, ...), custom_call_target="tpu_custom_call" | custom-call | flops 21743271936 | bytes 40000000 | tf_op jit(solution)/shard_map/back_to_context/pallas_call | solution.py:737
  249.6 11.8 %attend_back_own.1 = (bf16[12,192,2048]{2,1,0:T(8,128)(2,1)}, f32[4,112,768]{2,1,0:T(8,128)}, f32[4,112,768]{2,1,0:T(8,128)}) custom-call(s32[13]{0:T(128)} %concatenate.37.place_ref.refs_0_, bf16[12,192,2048]{2,1,0:T(8,128)(2,1)} %get-tuple-element.121.qkv_ref, bf16[12,64,2048]{2,1,0:T(8,128)(2,1)} %get-tuple-element.96.refs_2_.ctx_ref, ...), custom_call_target="tpu_custom_call" | custom-call | flops 5838471168 | bytes 12000000 | tf_op jit(solution)/shard_map/attend_back_own/pallas_call | solution.py:353
  264.9 8.0 %attend_back.2.old_ref = bf16[12,192,2048]{2,1,0:T(8,128)(2,1)} custom-call(s32[13]{0:T(128)} %concatenate.37.place_ref.refs_0_, bf16[12,192,2048]{2,1,0:T(8,128)(2,1)} %get-tuple-element.121.qkv_ref, bf16[12,64,2048]{2,1,0:T(8,128)(2,1)} %get-tuple-element.96.refs_2_.ctx_ref, ...), custom_call_target="tpu_custom_call", output_to_operand_aliasing={{}: (6, {})} | custom-call | flops 4026531840 | bytes 12000000 | tf_op jit(solution)/shard_map/attend_back/pallas_call | solution.py:392
  277.4 3.0 collective-permute-done.37.refs_7_
  280.4 13.1 %attend_back.3.grad_ref = bf16[12,192,2048]{2,1,0:T(8,128)(2,1)} custom-call(s32[13]{0:T(128)} %concatenate.37.place_ref.refs_0_, bf16[12,192,2048]{2,1,0:T(8,128)(2,1)} %get-tuple-element.121.qkv_ref, bf16[12,64,2048]{2,1,0:T(8,128)(2,1)} %get-tuple-element.96.refs_2_.ctx_ref, ...), custom_call_target="tpu_custom_call", output_to_operand_aliasing={{}: (6, {})} | custom-call | flops 8053063680 | bytes 12000000 | tf_op jit(solution)/shard_map/attend_back/pallas_call | solution.py:392
  297.6 16.2 %input_grads.1 = bf16[2048,768]{1,0:T(8,128)(2,1)} custom-call(s32[13]{0:T(128)} %concatenate.37.place_ref.refs_0_, f32[2048,768]{1,0:T(8,128)} %get-tuple-element.146.g1_ref, bf16[12,192,2048]{2,1,0:T(8,128)(2,1)} %attend_back.3.grad_ref, bf16[2304,768]{1,0:T(8,128)(2,1)} %get-tuple-element.147.w_ref), custom_call_target="tpu_custom_call" | custom-call | flops 8858370048 | bytes 20000000 | tf_op jit(solution)/shard_map/input_grads/pallas_call | solution.py:852
  315.0 5.4 %spread.1 = (f32[768,768]{1,0:T(8,128)}, f32[768,768]{1,0:T(8,128)}) custom-call(s32[13]{0:T(128)} %concatenate.37.place_ref.refs_0_, f32[1,192,768]{2,1,0:T(8,128)} %copy-done.1, f32[1,192,768]{2,1,0:T(8,128)} %collective-permute-done.38.refs_2_, f32[1,192,768]{2,1,0:T(8,128)} %collective-permute-done.31.refs_3_, ...), custom_call_target="tpu_custom_call" | custom-call | bytes 10000000 | tf_op jit(solution)/shard_map/spread/pallas_call | solution.py:787
  322.2 4.0 %spread_late.1 = (f32[192,768]{1,0:T(8,128)}, f32[192,768]{1,0:T(8,128)}, f32[192,768]{1,0:T(8,128)}, f32[192,768]{1,0:T(8,128)}, f32[16,768]{1,0:T(8,128)}) custom-call(s32[13]{0:T(128)} %concatenate.37.place_ref.refs_0_, f32[112,768]{1,0:T(8,128)} %copy-done.2, f32[112,768]{1,0:T(8,128)} %copy-done.12, f32[112,768]{1,0:T(8,128)} %copy-done.11, ...), custom_call_target="tpu_custom_call" | custom-call | bytes 5505024 | tf_op jit(solution)/shard_map/spread_late/pallas_call | solution.py:825
  (218 shorter events, 70.2 us)
Async XLA Ops:
  3.6 26.9 %collective-permute-start.2 = (f32[80,768]{1,0:T(8,128)S(1)}, f32[80,768]{1,0:T(8,128)S(1)}, u32[]{:S(2)}, u32[]{:S(2)}) collective-permute-start(f32[80,768]{1,0:T(8,128)S(1)} %pad_maximum_fusion.5), channel_id=1, source_target_pairs={{0,3},{1,0},{2,1},{3,2},{4,7},{5,4},{6,5},{7,6},{8,11},{9,8},{10,9... | collective-permute-start | bytes 737288 | tf_op jit(solution)/shard_map/ppermute | solution.py:884
  8.7 21.8 %collective-permute-start.1 = (f32[80,768]{1,0:T(8,128)S(1)}, f32[80,768]{1,0:T(8,128)S(1)}, u32[]{:S(2)}, u32[]{:S(2)}) collective-permute-start(f32[80,768]{1,0:T(8,128)S(1)} %pad_maximum_fusion.5), channel_id=1, source_target_pairs={{0,2},{1,3},{2,0},{3,1},{4,6},{5,7},{6,4},{7,5},{8,10},{9,11},{10,... | collective-permute-start | bytes 737288 | tf_op jit(solution)/shard_map/ppermute | solution.py:884
  8.7 21.8 %collective-permute-start = (f32[80,768]{1,0:T(8,128)S(1)}, f32[80,768]{1,0:T(8,128)S(1)}, u32[]{:S(2)}, u32[]{:S(2)}) collective-permute-start(f32[80,768]{1,0:T(8,128)S(1)} %pad_maximum_fusion.5), channel_id=1, source_target_pairs={{0,1},{1,2},{2,3},{3,0},{4,5},{5,6},{6,7},{7,4},{8,9},{9,10},{10,1... | collective-permute-start | bytes 737288 | tf_op jit(solution)/shard_map/ppermute | solution.py:884
  31.9 38.4 %all-to-all-start = ((f32[4,120,768]{2,1,0:T(8,128)}), f32[4,120,768]{2,1,0:T(8,128)S(1)}, u32[]{:S(2)}, u32[]{:S(2)}) async-start(f32[4,120,768]{2,1,0:T(8,128)} %broadcast_in_dim.77), calls=%async_computation | async-start | bytes 2949120 | tf_op jit(solution)/shard_map/all_to_all | solution.py:888
  72.6 36.6 %all-to-all-start.1 = ((f32[4,96,768]{2,1,0:T(8,128)}), f32[4,96,768]{2,1,0:T(8,128)S(1)}, u32[]{:S(2)}, u32[]{:S(2)}) async-start(f32[4,96,768]{2,1,0:T(8,128)} %broadcast_in_dim.78), calls=%async_computation.1 | async-start | bytes 2359296 | tf_op jit(solution)/shard_map/all_to_all | solution.py:888
  76.8 25.7 %collective-permute-start.13 = (f32[3,120,768]{2,1,0:T(8,128)}, f32[3,120,768]{2,1,0:T(8,128)}, u32[]{:S(2)}, u32[]{:S(2)}) collective-permute-start(f32[3,120,768]{2,1,0:T(8,128)} %pad_maximum_fusion.refs_7_), channel_id=1, source_target_pairs={{0,16},{4,20},{8,24},{12,28},{16,0},{20,4},{24,8},{28,12},{1,17},{... | collective-permute-start | bytes 3317768 | tf_op jit(solution)/shard_map/ppermute | solution.py:881
  78.3 25.4 %collective-permute-start.12 = (f32[3,120,768]{2,1,0:T(8,128)}, f32[3,120,768]{2,1,0:T(8,128)}, u32[]{:S(2)}, u32[]{:S(2)}) collective-permute-start(f32[3,120,768]{2,1,0:T(8,128)} %pad_maximum_fusion.refs_7_), channel_id=1, source_target_pairs={{0,8},{4,12},{8,0},{12,4},{16,24},{20,28},{24,16},{28,20},{1,9},{5... | collective-permute-start | bytes 3317768 | tf_op jit(solution)/shard_map/ppermute | solution.py:881
  106.3 18.5 %collective-permute-start.14 = (f32[3,120,768]{2,1,0:T(8,128)}, f32[3,120,768]{2,1,0:T(8,128)}, u32[]{:S(2)}, u32[]{:S(2)}) collective-permute-start(f32[3,120,768]{2,1,0:T(8,128)} %pad_maximum_fusion.refs_7_), channel_id=1, source_target_pairs={{0,4},{4,0},{8,12},{12,8},{16,20},{20,16},{24,28},{28,24},{1,5},{5... | collective-permute-start | bytes 3317768 | tf_op jit(solution)/shard_map/ppermute | solution.py:881
  106.4 19.5 %collective-permute-start.15 = (f32[3,120,768]{2,1,0:T(8,128)}, f32[3,120,768]{2,1,0:T(8,128)}, u32[]{:S(2)}, u32[]{:S(2)}) collective-permute-start(f32[3,120,768]{2,1,0:T(8,128)} %collective-permute-done.12.refs_9_), channel_id=1, source_target_pairs={{0,4},{4,0},{8,12},{12,8},{16,20},{20,16},{24,28},{28,24},{1,5},{5... | collective-permute-start | bytes 3317768 | tf_op jit(solution)/shard_map/ppermute | solution.py:881
  106.9 19.0 %collective-permute-start.16 = (f32[3,120,768]{2,1,0:T(8,128)}, f32[3,120,768]{2,1,0:T(8,128)}, u32[]{:S(2)}, u32[]{:S(2)}) collective-permute-start(f32[3,120,768]{2,1,0:T(8,128)} %collective-permute-done.13.refs_11_), channel_id=1, source_target_pairs={{0,4},{4,0},{8,12},{12,8},{16,20},{20,16},{24,28},{28,24},{1,5},{5... | collective-permute-start | bytes 3317768 | tf_op jit(solution)/shard_map/ppermute | solution.py:881
  110.6 47.5 %all-to-all-start.2 = ((f32[4,96,768]{2,1,0:T(8,128)}), f32[4,96,768]{2,1,0:T(8,128)S(1)}, u32[]{:S(2)}, u32[]{:S(2)}) async-start(f32[4,96,768]{2,1,0:T(8,128)} %broadcast_in_dim.79), calls=%async_computation.2 | async-start | bytes 2359296 | tf_op jit(solution)/shard_map/all_to_all | solution.py:888
  124.8 33.4 %collective-permute-start.23 = (f32[3,96,768]{2,1,0:T(8,128)S(1)}, f32[3,96,768]{2,1,0:T(8,128)S(1)}, u32[]{:S(2)}, u32[]{:S(2)}) collective-permute-start(f32[3,96,768]{2,1,0:T(8,128)S(1)} %pad_maximum_fusion.2.refs_7_), channel_id=1, source_target_pairs={{0,16},{4,20},{8,24},{12,28},{16,0},{20,4},{24,8},{28,12},{1,17},{... | collective-permute-start | bytes 2654216 | tf_op jit(solution)/shard_map/ppermute | solution.py:881
  125.3 32.9 %collective-permute-start.22 = (f32[3,96,768]{2,1,0:T(8,128)S(1)}, f32[3,96,768]{2,1,0:T(8,128)}, u32[]{:S(2)}, u32[]{:S(2)}) collective-permute-start(f32[3,96,768]{2,1,0:T(8,128)S(1)} %pad_maximum_fusion.2.refs_7_), channel_id=1, source_target_pairs={{0,8},{4,12},{8,0},{12,4},{16,24},{20,28},{24,16},{28,20},{1,9},{5... | collective-permute-start | bytes 2654216 | tf_op jit(solution)/shard_map/ppermute | solution.py:881
  125.9 33.3 %collective-permute-start.21 = (f32[3,96,768]{2,1,0:T(8,128)S(1)}, f32[3,96,768]{2,1,0:T(8,128)}, u32[]{:S(2)}, u32[]{:S(2)}) collective-permute-start(f32[3,96,768]{2,1,0:T(8,128)S(1)} %pad_maximum_fusion.2.refs_7_), channel_id=1, source_target_pairs={{0,4},{4,0},{8,12},{12,8},{16,20},{20,16},{24,28},{28,24},{1,5},{5... | collective-permute-start | bytes 2654216 | tf_op jit(solution)/shard_map/ppermute | solution.py:881
  209.3 37.1 %collective-permute-start.30 = (f32[192,768]{1,0:T(8,128)}, f32[192,768]{1,0:T(8,128)S(1)}, u32[]{:S(2)}, u32[]{:S(2)}) collective-permute-start(f32[192,768]{1,0:T(8,128)} %get-tuple-element.166), channel_id=1, source_target_pairs={{0,24},{4,28},{8,16},{12,20},{16,8},{20,12},{24,0},{28,4},{1,25},{... | collective-permute-start | bytes 1769480 | tf_op jit(solution)/shard_map/ppermute | solution.py:881
  211.7 34.6 %collective-permute-start.29 = (f32[192,768]{1,0:T(8,128)S(1)}, f32[192,768]{1,0:T(8,128)S(1)}, u32[]{:S(2)}, u32[]{:S(2)}) collective-permute-start(f32[192,768]{1,0:T(8,128)S(1)} %get-tuple-element.167), channel_id=1, source_target_pairs={{0,16},{4,20},{8,24},{12,28},{16,0},{20,4},{24,8},{28,12},{1,17},{... | collective-permute-start | bytes 1769480 | tf_op jit(solution)/shard_map/ppermute | solution.py:881
  212.2 34.1 %collective-permute-start.28 = (f32[192,768]{1,0:T(8,128)S(1)}, f32[192,768]{1,0:T(8,128)S(1)}, u32[]{:S(2)}, u32[]{:S(2)}) collective-permute-start(f32[192,768]{1,0:T(8,128)S(1)} %get-tuple-element.168), channel_id=1, source_target_pairs={{0,8},{4,12},{8,0},{12,4},{16,24},{20,28},{24,16},{28,20},{1,9},{5... | collective-permute-start | bytes 1769480 | tf_op jit(solution)/shard_map/ppermute | solution.py:881
  263.1 17.3 %collective-permute-start.37 = (f32[1,192,768]{2,1,0:T(8,128)S(1)}, f32[1,192,768]{2,1,0:T(8,128)}, u32[]{:S(2)}, u32[]{:S(2)}) collective-permute-start(f32[1,192,768]{2,1,0:T(8,128)S(1)} %add_bitcast_fusion.refs_1_), channel_id=1, source_target_pairs={{0,24},{4,28},{8,16},{12,20},{16,8},{20,12},{24,0},{28,4},{1,25},{... | collective-permute-start | bytes 1769480 | tf_op jit(solution)/shard_map/ppermute | solution.py:881
  273.9 19.5 %collective-permute-start.36 = (f32[112,768]{1,0:T(8,128)}, f32[112,768]{1,0:T(8,128)S(1)}, u32[]{:S(2)}, u32[]{:S(2)}) collective-permute-start(f32[112,768]{1,0:T(8,128)} %get-tuple-element.171), channel_id=1, source_target_pairs={{0,24},{4,28},{8,16},{12,20},{16,8},{20,12},{24,0},{28,4},{1,25},{... | collective-permute-start | bytes 1032200 | tf_op jit(solution)/shard_map/ppermute | solution.py:881
  275.5 18.5 %collective-permute-start.35 = (f32[112,768]{1,0:T(8,128)}, f32[112,768]{1,0:T(8,128)S(1)}, u32[]{:S(2)}, u32[]{:S(2)}) collective-permute-start(f32[112,768]{1,0:T(8,128)} %get-tuple-element.172), channel_id=1, source_target_pairs={{0,16},{4,20},{8,24},{12,28},{16,0},{20,4},{24,8},{28,12},{1,17},{... | collective-permute-start | bytes 1032200 | tf_op jit(solution)/shard_map/ppermute | solution.py:881
  276.0 17.9 %collective-permute-start.34 = (f32[112,768]{1,0:T(8,128)S(1)}, f32[112,768]{1,0:T(8,128)S(1)}, u32[]{:S(2)}, u32[]{:S(2)}) collective-permute-start(f32[112,768]{1,0:T(8,128)S(1)} %get-tuple-element.173), channel_id=1, source_target_pairs={{0,8},{4,12},{8,0},{12,4},{16,24},{20,28},{24,16},{28,20},{1,9},{5... | collective-permute-start | bytes 1032200 | tf_op jit(solution)/shard_map/ppermute | solution.py:881
  280.4 17.2 %collective-permute-start.41 = (f32[1,192,768]{2,1,0:T(8,128)}, f32[1,192,768]{2,1,0:T(8,128)S(1)}, u32[]{:S(2)}, u32[]{:S(2)}) collective-permute-start(f32[1,192,768]{2,1,0:T(8,128)} %collective-permute-done.37.refs_7_), channel_id=1, source_target_pairs={{0,4},{4,0},{8,12},{12,8},{16,20},{20,16},{24,28},{28,24},{1,5},{5... | collective-permute-start | bytes 1769480 | tf_op jit(solution)/shard_map/ppermute | solution.py:881
  294.0 19.8 %collective-permute-start.44 = (f32[112,768]{1,0:T(8,128)S(1)}, f32[112,768]{1,0:T(8,128)S(1)}, u32[]{:S(2)}, u32[]{:S(2)}) collective-permute-start(f32[112,768]{1,0:T(8,128)S(1)} %add_add_fusion.refs_1_), channel_id=1, source_target_pairs={{0,24},{4,28},{8,16},{12,20},{16,8},{20,12},{24,0},{28,4},{1,25},{... | collective-permute-start | bytes 1032200 | tf_op jit(solution)/shard_map/ppermute | solution.py:881
  295.5 18.3 %collective-permute-start.43 = (f32[112,768]{1,0:T(8,128)S(1)}, f32[112,768]{1,0:T(8,128)S(1)}, u32[]{:S(2)}, u32[]{:S(2)}) collective-permute-start(f32[112,768]{1,0:T(8,128)S(1)} %add_add_fusion.refs_1_), channel_id=1, source_target_pairs={{0,16},{4,20},{8,24},{12,28},{16,0},{20,4},{24,8},{28,12},{1,17},{... | collective-permute-start | bytes 1032200 | tf_op jit(solution)/shard_map/ppermute | solution.py:881
  (59 other events, 598.5 us)

commit v3 on v2

--- a/solution.py
+++ b/solution.py
@@ -21,8 +21,8 @@
     )
 
 
-def params():
-    return pltpu.CompilerParams(vmem_limit_bytes=LIMIT)
+def params(limit=LIMIT):
+    return pltpu.CompilerParams(vmem_limit_bytes=limit)
 
 
 def cost(flops, moved):
@@ -793,7 +793,7 @@
             out_specs=[whole(s) for s in shapes],
         ),
         out_shape=[jax.ShapeDtypeStruct(s, F32) for s in shapes],
-        compiler_params=params(),
+        compiler_params=params(16 << 20),
         cost_estimate=cost(0, 10e6),
         name="spread",
     )(place, *parts)
@@ -832,7 +832,7 @@
             scratch_shapes=[pltpu.VMEM((3 * height, width), F32)],
         ),
         out_shape=[jax.ShapeDtypeStruct(s, F32) for s in shapes],
-        compiler_params=params(),
+        compiler_params=params(10 << 20),
         cost_estimate=cost(0, 8 * parts[0].size * 8),
         name="spread_late",
     )(place, *parts)

time: 331 us -> 328 us (level)
  transfers between devices with their start and end apart: 52 -> 52, of which waited for: 14 -> 15; matrix products, arithmetic and copies ran while one was open for 5% -> 6% of each run, Pallas kernels for 50% -> 50%
where the time goes in v3:
time: 328 us; the launch traced here: 326 us
  Pallas kernels  203 us (62%)
  starting transfers between devices  50.2 us (15%)
  waiting for transfers between devices  42.3 us (13%)
  local copies, waits for them, and re-layouts  15 us (5%)
  other arithmetic  14.8 us (5%)
    ppermute x46, waiting for transfers between devices, flip(): return lax.ppermute(values, 'dp', [(i, i ^ bits) for i in range(lanes)])  37.6 us
    pallas_call x1, Pallas kernels, reduce(): pl.pallas_call(lambda *refs: reduce_kernel(spots, *refs), grid_spec=pltpu...  35.4 us
    pallas_call x1, Pallas kernels, back_to_context(): pl.pallas_call(return_kernel, grid_spec=pltpu.PrefetchScalarGridSpec(num_...  33.6 us
    pallas_call x1, Pallas kernels, expand(): pl.pallas_call(lambda *refs: expand_kernel(spots, *refs), grid_spec=pltpu...  32 us
    ppermute x46, starting transfers between devices, flip(): return lax.ppermute(values, 'dp', [(i, i ^ bits) for i in range(lanes)])  31.7 us
    pallas_call x1, Pallas kernels, attend_peers(): pl.pallas_call(lambda *refs: attend_peers_kernel(spots, *refs), grid_spec...  22.3 us
    pallas_call x2, Pallas kernels, attend_back(): pl.pallas_call(attend_back_kernel, grid_spec=pltpu.PrefetchScalarGridSpec...  20.9 us
    pallas_call x1, Pallas kernels, input_grads(): pl.pallas_call(input_grads_kernel, grid_spec=pltpu.PrefetchScalarGridSpec...  16.4 us
  transfers between devices with their start and end apart: 52, of which 15 were waited for; matrix products, arithmetic and copies ran while one was open for 6% of the time, Pallas kernels for 50%

profile of v3, /device:TPU:0, one launch (start us, length us, event | category | flops | bytes accessed | tf_op | source)
XLA Modules:
  0.0 326.1 jit_solution(8454398813614125324)
XLA Ops:
  3.6 5.1 %collective-permute-start.2 = (f32[80,768]{1,0:T(8,128)S(1)}, f32[80,768]{1,0:T(8,128)S(1)}, u32[]{:S(2)}, u32[]{:S(2)}) collective-permute-start(f32[80,768]{1,0:T(8,128)S(1)} %pad_maximum_fusion.5), channel_id=1, source_target_pairs={{0,3},{1,0},{2,1},{3,2},{4,7},{5,4},{6,5},{7,6},{8,11},{9,8},{10,9... | collective-permute-start | bytes 737288 | tf_op jit(solution)/shard_map/ppermute | solution.py:884
  13.3 7.7 %shift.1 = (bf16[2048,768]{1,0:T(8,128)(2,1)}, bf16[2048,768]{1,0:T(8,128)(2,1)}) custom-call(s32[13]{0:T(128)} %concatenate.37.place_ref.refs_0_, bf16[2048,768]{1,0:T(8,128)(2,1)} %bitcast.61, bf16[2048,768]{1,0:T(8,128)(2,1)} %bitcast.62), custom_call_target="tpu_custom_call" | custom-call | flops 3221225472 | bytes 12000000 | tf_op jit(solution)/shard_map/shift/pallas_call | solution.py:93
  21.0 8.4 %attend_own.1 = (bf16[2304,768]{1,0:T(8,128)(2,1)}, bf16[12,192,2048]{2,1,0:T(8,128)(2,1)}, bf16[12,64,2048]{2,1,0:T(8,128)(2,1)}, bf16[12,16,2048]{2,1,0:T(8,128)(2,1)}) custom-call(s32[13]{0:T(128)} %concatenate.37.place_ref.refs_0_, bf16[2048,768]{1,0:T(8,128)(2,1)} %get-tuple-element.88.x_ref.refs_1_.refs_0_, f32[8,768]{1,0:T(8,128)} %copy-done.7, ...), custom_call_target="tpu_custom_call" | custom-call | flops 5033164800 | bytes 12000000 | tf_op jit(solution)/shard_map/attend_own/pallas_call | solution.py:188
  32.0 4.1 %all-to-all-start = ((f32[4,120,768]{2,1,0:T(8,128)}), f32[4,120,768]{2,1,0:T(8,128)S(1)}, u32[]{:S(2)}, u32[]{:S(2)}) async-start(f32[4,120,768]{2,1,0:T(8,128)} %broadcast_in_dim.77), calls=%async_computation | async-start | bytes 2949120 | tf_op jit(solution)/shard_map/all_to_all | solution.py:888
  39.1 12.9 %collective-permute-done.4.refs_7_ = f32[3,72,768]{2,1,0:T(8,128)} collective-permute-done((f32[3,72,768]{2,1,0:T(8,128)S(1)}, f32[3,72,768]{2,1,0:T(8,128)}, u32[]{:S(2)}, u32[]{:S(2)}) %collective-permute-start.4) | collective-permute-done | bytes 663584 | tf_op jit(solution)/shard_map/ppermute | solution.py:881
  57.8 4.0 %collective-permute-done.10.refs_13_ = f32[3,40,768]{2,1,0:T(8,128)} collective-permute-done((f32[3,40,768]{2,1,0:T(8,128)S(1)}, f32[3,40,768]{2,1,0:T(8,128)}, u32[]{:S(2)}, u32[]{:S(2)}) %collective-permute-start.10) | collective-permute-done | bytes 368672 | tf_op jit(solution)/shard_map/ppermute | solution.py:881
  61.8 3.9 %collective-permute-done.8.refs_11_ = f32[3,32,768]{2,1,0:T(8,128)} collective-permute-done((f32[3,32,768]{2,1,0:T(8,128)S(1)}, f32[3,32,768]{2,1,0:T(8,128)}, u32[]{:S(2)}, u32[]{:S(2)}) %collective-permute-start.8) | collective-permute-done | bytes 294944 | tf_op jit(solution)/shard_map/ppermute | solution.py:881
  65.7 4.7 %all-to-all-done = f32[4,120,768]{2,1,0:T(8,128)S(1)} async-done(((f32[4,120,768]{2,1,0:T(8,128)}), f32[4,120,768]{2,1,0:T(8,128)S(1)}, u32[]{:S(2)}, u32[]{:S(2)}) %all-to-all-start) | async-done | bytes 1474592 | tf_op jit(solution)/shard_map/all_to_all | solution.py:888
  72.8 3.5 %all-to-all-start.1 = ((f32[4,96,768]{2,1,0:T(8,128)}), f32[4,96,768]{2,1,0:T(8,128)S(1)}, u32[]{:S(2)}, u32[]{:S(2)}) async-start(f32[4,96,768]{2,1,0:T(8,128)} %broadcast_in_dim.78), calls=%async_computation.1 | async-start | bytes 2359296 | tf_op jit(solution)/shard_map/all_to_all | solution.py:888
  80.0 22.3 %attend_peers.1 = (bf16[2304,768]{1,0:T(8,128)(2,1)}, bf16[12,192,2048]{2,1,0:T(8,128)(2,1)}, bf16[12,64,2048]{2,1,0:T(8,128)(2,1)}, bf16[12,16,2048]{2,1,0:T(8,128)(2,1)}) custom-call(s32[13]{0:T(128)} %concatenate.37.place_ref.refs_0_, ...), custom_call_target="tpu_custom_call", output_to_operand_aliasing={{0}: (15, {}), {1}: (16, {}), {2}: (17, {}), {3}: (18, {})} | custom-call | flops 15099494400 | bytes 30000000 | tf_op jit(solution)/shard_map/attend_peers/pallas_call | solution.py:233
  110.7 4.8 %all-to-all-start.2 = ((f32[4,96,768]{2,1,0:T(8,128)}), f32[4,96,768]{2,1,0:T(8,128)S(1)}, u32[]{:S(2)}, u32[]{:S(2)}) async-start(f32[4,96,768]{2,1,0:T(8,128)} %broadcast_in_dim.79), calls=%async_computation.2 | async-start | bytes 2359296 | tf_op jit(solution)/shard_map/all_to_all | solution.py:888
  118.2 5.2 %collective-permute-done.19.refs_15_ = f32[3,56,768]{2,1,0:T(8,128)} collective-permute-done((f32[3,56,768]{2,1,0:T(8,128)}, f32[3,56,768]{2,1,0:T(8,128)}, u32[]{:S(2)}, u32[]{:S(2)}) %collective-permute-start.19) | collective-permute-done | bytes 516128 | tf_op jit(solution)/shard_map/ppermute | solution.py:881
  126.3 32.0 %expand.1 = (f32[2048,768]{1,0:T(8,128)}, bf16[4,2048,768]{2,1,0:T(8,128)(2,1)}, bf16[4,2048,768]{2,1,0:T(8,128)(2,1)}, bf16[4,768,768]{2,1,0:T(8,128)(2,1)}, bf16[768,768]{1,0:T(8,128)(2,1)}) custom-call(s32[13]{0:T(128)} %concatenate.37.place_ref.refs_0_, bf16[2048,768]{1,0:T(8,128)(2,1)} %get-tuple-element.88.x_ref.refs_1_.refs_0_, ...), custom_call_target="tpu_custom_call" | custom-call | flops 12079595520 | bytes 40000000 | tf_op jit(solution)/shard_map/expand/pallas_call | solution.py:513
  164.5 35.4 %reduce.15 = (bf16[2048,768]{1,0:T(8,128)(2,1)}, f32[2048,768]{1,0:T(8,128)}, bf16[4,768,768]{2,1,0:T(8,128)(2,1)}, f32[4,192,768]{2,1,0:T(8,128)}, f32[4,192,768]{2,1,0:T(8,128)}, /*index=5*/f32[8,768]{1,0:T(8,128)}) custom-call(s32[13]{0:T(128)} %concatenate.37.place_ref.refs_0_, f32[2048,768]{1,0:T(8,128)} %get-tuple-element.103.refs_1_.sum_ref, ...), custom_call_target="tpu_custom_call" | custom-call | flops 16911433728 | bytes 40000000 | tf_op jit(solution)/shard_map/reduce/pallas_call | solution.py:646
  200.2 6.4 %unshift.1 = bf16[2048,768]{1,0:T(8,128)(2,1)} custom-call(s32[13]{0:T(128)} %concatenate.37.place_ref.refs_0_, bf16[2048,768]{1,0:T(8,128)(2,1)} %get-tuple-element.111.in_ref), custom_call_target="tpu_custom_call" | custom-call | flops 1610612736 | bytes 6000000 | tf_op jit(solution)/shard_map/unshift/pallas_call | solution.py:117
  206.7 2.7 add_bitcast_fusion.1
  212.9 33.6 %back_to_context.1 = (f32[2048,768]{1,0:T(8,128)}, bf16[12,64,2048]{2,1,0:T(8,128)(2,1)}, f32[192,768]{1,0:T(8,128)}, f32[8,768]{1,0:T(8,128)}) custom-call(s32[13]{0:T(128)} %concatenate.37.place_ref.refs_0_, f32[2048,768]{1,0:T(8,128)} %get-tuple-element.103.refs_1_.sum_ref, f32[2048,768]{1,0:T(8,128)} %get-tuple-element.112.g2_ref, ...), custom_call_target="tpu_custom_call" | custom-call | flops 21743271936 | bytes 40000000 | tf_op jit(solution)/shard_map/back_to_context/pallas_call | solution.py:737
  249.7 11.8 %attend_back_own.1 = (bf16[12,192,2048]{2,1,0:T(8,128)(2,1)}, f32[4,112,768]{2,1,0:T(8,128)}, f32[4,112,768]{2,1,0:T(8,128)}) custom-call(s32[13]{0:T(128)} %concatenate.37.place_ref.refs_0_, bf16[12,192,2048]{2,1,0:T(8,128)(2,1)} %get-tuple-element.121.qkv_ref, bf16[12,64,2048]{2,1,0:T(8,128)(2,1)} %get-tuple-element.96.refs_2_.ctx_ref, ...), custom_call_target="tpu_custom_call" | custom-call | flops 5838471168 | bytes 12000000 | tf_op jit(solution)/shard_map/attend_back_own/pallas_call | solution.py:353
  264.9 7.8 %attend_back.2.old_ref = bf16[12,192,2048]{2,1,0:T(8,128)(2,1)} custom-call(s32[13]{0:T(128)} %concatenate.37.place_ref.refs_0_, bf16[12,192,2048]{2,1,0:T(8,128)(2,1)} %get-tuple-element.121.qkv_ref, bf16[12,64,2048]{2,1,0:T(8,128)(2,1)} %get-tuple-element.96.refs_2_.ctx_ref, ...), custom_call_target="tpu_custom_call", output_to_operand_aliasing={{}: (6, {})} | custom-call | flops 4026531840 | bytes 12000000 | tf_op jit(solution)/shard_map/attend_back/pallas_call | solution.py:392
  272.8 2.7 add_bitcast_fusion.8
  279.2 13.1 %attend_back.3.grad_ref = bf16[12,192,2048]{2,1,0:T(8,128)(2,1)} custom-call(s32[13]{0:T(128)} %concatenate.37.place_ref.refs_0_, bf16[12,192,2048]{2,1,0:T(8,128)(2,1)} %get-tuple-element.121.qkv_ref, bf16[12,64,2048]{2,1,0:T(8,128)(2,1)} %get-tuple-element.96.refs_2_.ctx_ref, ...), custom_call_target="tpu_custom_call", output_to_operand_aliasing={{}: (6, {})} | custom-call | flops 8053063680 | bytes 12000000 | tf_op jit(solution)/shard_map/attend_back/pallas_call | solution.py:392
  299.1 16.4 %input_grads.1 = bf16[2048,768]{1,0:T(8,128)(2,1)} custom-call(s32[13]{0:T(128)} %concatenate.37.place_ref.refs_0_, f32[2048,768]{1,0:T(8,128)} %get-tuple-element.146.g1_ref, bf16[12,192,2048]{2,1,0:T(8,128)(2,1)} %attend_back.3.grad_ref, bf16[2304,768]{1,0:T(8,128)(2,1)} %get-tuple-element.147.w_ref), custom_call_target="tpu_custom_call" | custom-call | flops 8858370048 | bytes 20000000 | tf_op jit(solution)/shard_map/input_grads/pallas_call | solution.py:852
  316.6 4.3 %spread.1 = (f32[768,768]{1,0:T(8,128)}, f32[768,768]{1,0:T(8,128)}) custom-call(s32[13]{0:T(128)S(1)} %copy-done, f32[1,192,768]{2,1,0:T(8,128)S(1)} %add_bitcast_fusion.refs_1_, f32[1,192,768]{2,1,0:T(8,128)S(1)} %collective-permute-done.38.refs_2_, f32[1,192,768]{2,1,0:T(8,128)S(1)} %collective-permute-done.31.refs_3_, ...), custom_call_target="tpu_custom_call" | custom-call | bytes 10000000 | tf_op jit(solution)/shard_map/spread/pallas_call | solution.py:787
  320.8 3.3 %spread_late.1 = (f32[192,768]{1,0:T(8,128)}, f32[192,768]{1,0:T(8,128)}, f32[192,768]{1,0:T(8,128)}, f32[192,768]{1,0:T(8,128)}, f32[16,768]{1,0:T(8,128)S(1)}) custom-call(s32[13]{0:T(128)S(1)} %copy-done, f32[112,768]{1,0:T(8,128)S(1)} %add_add_fusion.refs_1_, f32[112,768]{1,0:T(8,128)S(1)} %collective-permute-done.45.refs_2_, ...), custom_call_target="tpu_custom_call" | custom-call | bytes 5505024 | tf_op jit(solution)/shard_map/spread_late/pallas_call | solution.py:825
  (198 shorter events, 68.7 us)
Async XLA Ops:
  3.6 27.0 %collective-permute-start.2 = (f32[80,768]{1,0:T(8,128)S(1)}, f32[80,768]{1,0:T(8,128)S(1)}, u32[]{:S(2)}, u32[]{:S(2)}) collective-permute-start(f32[80,768]{1,0:T(8,128)S(1)} %pad_maximum_fusion.5), channel_id=1, source_target_pairs={{0,3},{1,0},{2,1},{3,2},{4,7},{5,4},{6,5},{7,6},{8,11},{9,8},{10,9... | collective-permute-start | bytes 737288 | tf_op jit(solution)/shard_map/ppermute | solution.py:884
  8.7 21.9 %collective-permute-start.1 = (f32[80,768]{1,0:T(8,128)S(1)}, f32[80,768]{1,0:T(8,128)S(1)}, u32[]{:S(2)}, u32[]{:S(2)}) collective-permute-start(f32[80,768]{1,0:T(8,128)S(1)} %pad_maximum_fusion.5), channel_id=1, source_target_pairs={{0,2},{1,3},{2,0},{3,1},{4,6},{5,7},{6,4},{7,5},{8,10},{9,11},{10,... | collective-permute-start | bytes 737288 | tf_op jit(solution)/shard_map/ppermute | solution.py:884
  8.7 21.9 %collective-permute-start = (f32[80,768]{1,0:T(8,128)S(1)}, f32[80,768]{1,0:T(8,128)S(1)}, u32[]{:S(2)}, u32[]{:S(2)}) collective-permute-start(f32[80,768]{1,0:T(8,128)S(1)} %pad_maximum_fusion.5), channel_id=1, source_target_pairs={{0,1},{1,2},{2,3},{3,0},{4,5},{5,6},{6,7},{7,4},{8,9},{9,10},{10,1... | collective-permute-start | bytes 737288 | tf_op jit(solution)/shard_map/ppermute | solution.py:884
  32.0 38.4 %all-to-all-start = ((f32[4,120,768]{2,1,0:T(8,128)}), f32[4,120,768]{2,1,0:T(8,128)S(1)}, u32[]{:S(2)}, u32[]{:S(2)}) async-start(f32[4,120,768]{2,1,0:T(8,128)} %broadcast_in_dim.77), calls=%async_computation | async-start | bytes 2949120 | tf_op jit(solution)/shard_map/all_to_all | solution.py:888
  37.6 17.0 %collective-permute-start.6 = (f32[3,72,768]{2,1,0:T(8,128)S(1)}, f32[3,72,768]{2,1,0:T(8,128)}, u32[]{:S(2)}, u32[]{:S(2)}) collective-permute-start(f32[3,72,768]{2,1,0:T(8,128)S(1)} %slice.94.refs_5_), channel_id=1, source_target_pairs={{0,16},{4,20},{8,24},{12,28},{16,0},{20,4},{24,8},{28,12},{1,17},{... | collective-permute-start | bytes 1990664 | tf_op jit(solution)/shard_map/ppermute | solution.py:881
  54.6 17.0 %collective-permute-start.3 = (f32[3,72,768]{2,1,0:T(8,128)S(1)}, f32[3,72,768]{2,1,0:T(8,128)}, u32[]{:S(2)}, u32[]{:S(2)}) collective-permute-start(f32[3,72,768]{2,1,0:T(8,128)S(1)} %slice.94.refs_5_), channel_id=1, source_target_pairs={{0,4},{4,0},{8,12},{12,8},{16,20},{20,16},{24,28},{28,24},{1,5},{5... | collective-permute-start | bytes 1990664 | tf_op jit(solution)/shard_map/ppermute | solution.py:881
  72.8 36.6 %all-to-all-start.1 = ((f32[4,96,768]{2,1,0:T(8,128)}), f32[4,96,768]{2,1,0:T(8,128)S(1)}, u32[]{:S(2)}, u32[]{:S(2)}) async-start(f32[4,96,768]{2,1,0:T(8,128)} %broadcast_in_dim.78), calls=%async_computation.1 | async-start | bytes 2359296 | tf_op jit(solution)/shard_map/all_to_all | solution.py:888
  76.9 25.7 %collective-permute-start.13 = (f32[3,120,768]{2,1,0:T(8,128)}, f32[3,120,768]{2,1,0:T(8,128)}, u32[]{:S(2)}, u32[]{:S(2)}) collective-permute-start(f32[3,120,768]{2,1,0:T(8,128)} %pad_maximum_fusion.refs_7_), channel_id=1, source_target_pairs={{0,16},{4,20},{8,24},{12,28},{16,0},{20,4},{24,8},{28,12},{1,17},{... | collective-permute-start | bytes 3317768 | tf_op jit(solution)/shard_map/ppermute | solution.py:881
  78.5 25.4 %collective-permute-start.12 = (f32[3,120,768]{2,1,0:T(8,128)}, f32[3,120,768]{2,1,0:T(8,128)}, u32[]{:S(2)}, u32[]{:S(2)}) collective-permute-start(f32[3,120,768]{2,1,0:T(8,128)} %pad_maximum_fusion.refs_7_), channel_id=1, source_target_pairs={{0,8},{4,12},{8,0},{12,4},{16,24},{20,28},{24,16},{28,20},{1,9},{5... | collective-permute-start | bytes 3317768 | tf_op jit(solution)/shard_map/ppermute | solution.py:881
  106.5 18.5 %collective-permute-start.14 = (f32[3,120,768]{2,1,0:T(8,128)}, f32[3,120,768]{2,1,0:T(8,128)}, u32[]{:S(2)}, u32[]{:S(2)}) collective-permute-start(f32[3,120,768]{2,1,0:T(8,128)} %pad_maximum_fusion.refs_7_), channel_id=1, source_target_pairs={{0,4},{4,0},{8,12},{12,8},{16,20},{20,16},{24,28},{28,24},{1,5},{5... | collective-permute-start | bytes 3317768 | tf_op jit(solution)/shard_map/ppermute | solution.py:881
  106.5 19.5 %collective-permute-start.15 = (f32[3,120,768]{2,1,0:T(8,128)}, f32[3,120,768]{2,1,0:T(8,128)}, u32[]{:S(2)}, u32[]{:S(2)}) collective-permute-start(f32[3,120,768]{2,1,0:T(8,128)} %collective-permute-done.12.refs_9_), channel_id=1, source_target_pairs={{0,4},{4,0},{8,12},{12,8},{16,20},{20,16},{24,28},{28,24},{1,5},{5... | collective-permute-start | bytes 3317768 | tf_op jit(solution)/shard_map/ppermute | solution.py:881
  107.0 19.0 %collective-permute-start.16 = (f32[3,120,768]{2,1,0:T(8,128)}, f32[3,120,768]{2,1,0:T(8,128)}, u32[]{:S(2)}, u32[]{:S(2)}) collective-permute-start(f32[3,120,768]{2,1,0:T(8,128)} %collective-permute-done.13.refs_11_), channel_id=1, source_target_pairs={{0,4},{4,0},{8,12},{12,8},{16,20},{20,16},{24,28},{28,24},{1,5},{5... | collective-permute-start | bytes 3317768 | tf_op jit(solution)/shard_map/ppermute | solution.py:881
  110.7 47.6 %all-to-all-start.2 = ((f32[4,96,768]{2,1,0:T(8,128)}), f32[4,96,768]{2,1,0:T(8,128)S(1)}, u32[]{:S(2)}, u32[]{:S(2)}) async-start(f32[4,96,768]{2,1,0:T(8,128)} %broadcast_in_dim.79), calls=%async_computation.2 | async-start | bytes 2359296 | tf_op jit(solution)/shard_map/all_to_all | solution.py:888
  125.0 33.5 %collective-permute-start.23 = (f32[3,96,768]{2,1,0:T(8,128)S(1)}, f32[3,96,768]{2,1,0:T(8,128)S(1)}, u32[]{:S(2)}, u32[]{:S(2)}) collective-permute-start(f32[3,96,768]{2,1,0:T(8,128)S(1)} %pad_maximum_fusion.2.refs_7_), channel_id=1, source_target_pairs={{0,16},{4,20},{8,24},{12,28},{16,0},{20,4},{24,8},{28,12},{1,17},{... | collective-permute-start | bytes 2654216 | tf_op jit(solution)/shard_map/ppermute | solution.py:881
  125.5 33.0 %collective-permute-start.22 = (f32[3,96,768]{2,1,0:T(8,128)S(1)}, f32[3,96,768]{2,1,0:T(8,128)}, u32[]{:S(2)}, u32[]{:S(2)}) collective-permute-start(f32[3,96,768]{2,1,0:T(8,128)S(1)} %pad_maximum_fusion.2.refs_7_), channel_id=1, source_target_pairs={{0,8},{4,12},{8,0},{12,4},{16,24},{20,28},{24,16},{28,20},{1,9},{5... | collective-permute-start | bytes 2654216 | tf_op jit(solution)/shard_map/ppermute | solution.py:881
  126.0 33.4 %collective-permute-start.21 = (f32[3,96,768]{2,1,0:T(8,128)S(1)}, f32[3,96,768]{2,1,0:T(8,128)}, u32[]{:S(2)}, u32[]{:S(2)}) collective-permute-start(f32[3,96,768]{2,1,0:T(8,128)S(1)} %pad_maximum_fusion.2.refs_7_), channel_id=1, source_target_pairs={{0,4},{4,0},{8,12},{12,8},{16,20},{20,16},{24,28},{28,24},{1,5},{5... | collective-permute-start | bytes 2654216 | tf_op jit(solution)/shard_map/ppermute | solution.py:881
  209.4 37.1 %collective-permute-start.30 = (f32[192,768]{1,0:T(8,128)}, f32[192,768]{1,0:T(8,128)S(1)}, u32[]{:S(2)}, u32[]{:S(2)}) collective-permute-start(f32[192,768]{1,0:T(8,128)} %get-tuple-element.166), channel_id=1, source_target_pairs={{0,24},{4,28},{8,16},{12,20},{16,8},{20,12},{24,0},{28,4},{1,25},{... | collective-permute-start | bytes 1769480 | tf_op jit(solution)/shard_map/ppermute | solution.py:881
  211.8 34.7 %collective-permute-start.29 = (f32[192,768]{1,0:T(8,128)S(1)}, f32[192,768]{1,0:T(8,128)S(1)}, u32[]{:S(2)}, u32[]{:S(2)}) collective-permute-start(f32[192,768]{1,0:T(8,128)S(1)} %get-tuple-element.167), channel_id=1, source_target_pairs={{0,16},{4,20},{8,24},{12,28},{16,0},{20,4},{24,8},{28,12},{1,17},{... | collective-permute-start | bytes 1769480 | tf_op jit(solution)/shard_map/ppermute | solution.py:881
  212.3 34.2 %collective-permute-start.28 = (f32[192,768]{1,0:T(8,128)S(1)}, f32[192,768]{1,0:T(8,128)S(1)}, u32[]{:S(2)}, u32[]{:S(2)}) collective-permute-start(f32[192,768]{1,0:T(8,128)S(1)} %get-tuple-element.168), channel_id=1, source_target_pairs={{0,8},{4,12},{8,0},{12,4},{16,24},{20,28},{24,16},{28,20},{1,9},{5... | collective-permute-start | bytes 1769480 | tf_op jit(solution)/shard_map/ppermute | solution.py:881
  277.1 17.0 %collective-permute-start.35 = (f32[112,768]{1,0:T(8,128)}, f32[112,768]{1,0:T(8,128)}, u32[]{:S(2)}, u32[]{:S(2)}) collective-permute-start(f32[112,768]{1,0:T(8,128)} %get-tuple-element.172), channel_id=1, source_target_pairs={{0,16},{4,20},{8,24},{12,28},{16,0},{20,4},{24,8},{28,12},{1,17},{... | collective-permute-start | bytes 1032200 | tf_op jit(solution)/shard_map/ppermute | solution.py:881
  279.2 19.8 %collective-permute-start.41 = (f32[1,192,768]{2,1,0:T(8,128)S(1)}, f32[1,192,768]{2,1,0:T(8,128)}, u32[]{:S(2)}, u32[]{:S(2)}) collective-permute-start(f32[1,192,768]{2,1,0:T(8,128)S(1)} %collective-permute-done.37.refs_7_), channel_id=1, source_target_pairs={{0,4},{4,0},{8,12},{12,8},{16,20},{20,16},{24,28},{28,24},{1,5},{5... | collective-permute-start | bytes 1769480 | tf_op jit(solution)/shard_map/ppermute | solution.py:881
  295.5 19.9 %collective-permute-start.44 = (f32[112,768]{1,0:T(8,128)S(1)}, f32[112,768]{1,0:T(8,128)}, u32[]{:S(2)}, u32[]{:S(2)}) collective-permute-start(f32[112,768]{1,0:T(8,128)S(1)} %add_add_fusion.refs_1_), channel_id=1, source_target_pairs={{0,24},{4,28},{8,16},{12,20},{16,8},{20,12},{24,0},{28,4},{1,25},{... | collective-permute-start | bytes 1032200 | tf_op jit(solution)/shard_map/ppermute | solution.py:881
  297.0 18.4 %collective-permute-start.43 = (f32[112,768]{1,0:T(8,128)S(1)}, f32[112,768]{1,0:T(8,128)}, u32[]{:S(2)}, u32[]{:S(2)}) collective-permute-start(f32[112,768]{1,0:T(8,128)S(1)} %add_add_fusion.refs_1_), channel_id=1, source_target_pairs={{0,16},{4,20},{8,24},{12,28},{16,0},{20,4},{24,8},{28,12},{1,17},{... | collective-permute-start | bytes 1032200 | tf_op jit(solution)/shard_map/ppermute | solution.py:881
  298.4 17.1 %collective-permute-start.42 = (f32[112,768]{1,0:T(8,128)S(1)}, f32[112,768]{1,0:T(8,128)}, u32[]{:S(2)}, u32[]{:S(2)}) collective-permute-start(f32[112,768]{1,0:T(8,128)S(1)} %add_add_fusion.refs_1_), channel_id=1, source_target_pairs={{0,8},{4,12},{8,0},{12,4},{16,24},{20,28},{24,16},{28,20},{1,9},{5... | collective-permute-start | bytes 1032200 | tf_op jit(solution)/shard_map/ppermute | solution.py:881
  (49 other events, 527.8 us)

commit v4 on v3

--- a/solution.py
+++ b/solution.py
@@ -862,7 +862,7 @@
             out_specs=by_row(),
         ),
         out_shape=jax.ShapeDtypeStruct((tokens, width), BF16),
-        compiler_params=params(),
+        compiler_params=params(56 << 20),
         cost_estimate=cost(2 * tokens * width * (every * 3 * HD + length), 20e6),
         name="input_grads",
     )(place, grad_one, grads, weights)

time: 328 us -> 326 us (level)
  no operation moved by 1% of the time
where the time goes in v4:
time: 326 us; the launch traced here: 325 us
  Pallas kernels  201 us (62%)
  starting transfers between devices  50.2 us (15%)
  waiting for transfers between devices  42.3 us (13%)
  local copies, waits for them, and re-layouts  14.9 us (5%)
  other arithmetic  14.9 us (5%)
    ppermute x46, waiting for transfers between devices, flip(): return lax.ppermute(values, 'dp', [(i, i ^ bits) for i in range(lanes)])  37.6 us
    pallas_call x1, Pallas kernels, reduce(): pl.pallas_call(lambda *refs: reduce_kernel(spots, *refs), grid_spec=pltpu...  35.3 us
    pallas_call x1, Pallas kernels, back_to_context(): pl.pallas_call(return_kernel, grid_spec=pltpu.PrefetchScalarGridSpec(num_...  33.6 us
    pallas_call x1, Pallas kernels, expand(): pl.pallas_call(lambda *refs: expand_kernel(spots, *refs), grid_spec=pltpu...  32 us
    ppermute x46, starting transfers between devices, flip(): return lax.ppermute(values, 'dp', [(i, i ^ bits) for i in range(lanes)])  31.7 us
    pallas_call x1, Pallas kernels, attend_peers(): pl.pallas_call(lambda *refs: attend_peers_kernel(spots, *refs), grid_spec...  22.3 us
    pallas_call x2, Pallas kernels, attend_back(): pl.pallas_call(attend_back_kernel, grid_spec=pltpu.PrefetchScalarGridSpec...  20.9 us
    pallas_call x1, Pallas kernels, input_grads(): pl.pallas_call(input_grads_kernel, grid_spec=pltpu.PrefetchScalarGridSpec...  16.4 us
  transfers between devices with their start and end apart: 52, of which 15 were waited for; matrix products, arithmetic and copies ran while one was open for 6% of the time, Pallas kernels for 50%

profile of v4, /device:TPU:0, one launch (start us, length us, event | category | flops | bytes accessed | tf_op | source)
XLA Modules:
  0.0 324.8 jit_solution(10415711735968980544)
XLA Ops:
  3.6 5.1 %collective-permute-start.2 = (f32[80,768]{1,0:T(8,128)S(1)}, f32[80,768]{1,0:T(8,128)S(1)}, u32[]{:S(2)}, u32[]{:S(2)}) collective-permute-start(f32[80,768]{1,0:T(8,128)S(1)} %pad_maximum_fusion.5), channel_id=1, source_target_pairs={{0,3},{1,0},{2,1},{3,2},{4,7},{5,4},{6,5},{7,6},{8,11},{9,8},{10,9... | collective-permute-start | bytes 737288 | tf_op jit(solution)/shard_map/ppermute | solution.py:884
  13.2 7.7 %shift.1 = (bf16[2048,768]{1,0:T(8,128)(2,1)}, bf16[2048,768]{1,0:T(8,128)(2,1)}) custom-call(s32[13]{0:T(128)} %concatenate.37.place_ref.refs_0_, bf16[2048,768]{1,0:T(8,128)(2,1)} %bitcast.61, bf16[2048,768]{1,0:T(8,128)(2,1)} %bitcast.62), custom_call_target="tpu_custom_call" | custom-call | flops 3221225472 | bytes 12000000 | tf_op jit(solution)/shard_map/shift/pallas_call | solution.py:93
  20.9 8.4 %attend_own.1 = (bf16[2304,768]{1,0:T(8,128)(2,1)}, bf16[12,192,2048]{2,1,0:T(8,128)(2,1)}, bf16[12,64,2048]{2,1,0:T(8,128)(2,1)}, bf16[12,16,2048]{2,1,0:T(8,128)(2,1)}) custom-call(s32[13]{0:T(128)} %concatenate.37.place_ref.refs_0_, bf16[2048,768]{1,0:T(8,128)(2,1)} %get-tuple-element.88.x_ref.refs_1_.refs_0_, f32[8,768]{1,0:T(8,128)} %copy-done.7, ...), custom_call_target="tpu_custom_call" | custom-call | flops 5033164800 | bytes 12000000 | tf_op jit(solution)/shard_map/attend_own/pallas_call | solution.py:188
  31.9 4.1 %all-to-all-start = ((f32[4,120,768]{2,1,0:T(8,128)}), f32[4,120,768]{2,1,0:T(8,128)S(1)}, u32[]{:S(2)}, u32[]{:S(2)}) async-start(f32[4,120,768]{2,1,0:T(8,128)} %broadcast_in_dim.77), calls=%async_computation | async-start | bytes 2949120 | tf_op jit(solution)/shard_map/all_to_all | solution.py:888
  39.1 12.9 %collective-permute-done.4.refs_7_ = f32[3,72,768]{2,1,0:T(8,128)} collective-permute-done((f32[3,72,768]{2,1,0:T(8,128)S(1)}, f32[3,72,768]{2,1,0:T(8,128)}, u32[]{:S(2)}, u32[]{:S(2)}) %collective-permute-start.4) | collective-permute-done | bytes 663584 | tf_op jit(solution)/shard_map/ppermute | solution.py:881
  57.7 4.0 %collective-permute-done.10.refs_13_ = f32[3,40,768]{2,1,0:T(8,128)} collective-permute-done((f32[3,40,768]{2,1,0:T(8,128)S(1)}, f32[3,40,768]{2,1,0:T(8,128)}, u32[]{:S(2)}, u32[]{:S(2)}) %collective-permute-start.10) | collective-permute-done | bytes 368672 | tf_op jit(solution)/shard_map/ppermute | solution.py:881
  61.7 3.9 %collective-permute-done.8.refs_11_ = f32[3,32,768]{2,1,0:T(8,128)} collective-permute-done((f32[3,32,768]{2,1,0:T(8,128)S(1)}, f32[3,32,768]{2,1,0:T(8,128)}, u32[]{:S(2)}, u32[]{:S(2)}) %collective-permute-start.8) | collective-permute-done | bytes 294944 | tf_op jit(solution)/shard_map/ppermute | solution.py:881
  65.7 4.7 %all-to-all-done = f32[4,120,768]{2,1,0:T(8,128)S(1)} async-done(((f32[4,120,768]{2,1,0:T(8,128)}), f32[4,120,768]{2,1,0:T(8,128)S(1)}, u32[]{:S(2)}, u32[]{:S(2)}) %all-to-all-start) | async-done | bytes 1474592 | tf_op jit(solution)/shard_map/all_to_all | solution.py:888
  72.7 3.5 %all-to-all-start.1 = ((f32[4,96,768]{2,1,0:T(8,128)}), f32[4,96,768]{2,1,0:T(8,128)S(1)}, u32[]{:S(2)}, u32[]{:S(2)}) async-start(f32[4,96,768]{2,1,0:T(8,128)} %broadcast_in_dim.78), calls=%async_computation.1 | async-start | bytes 2359296 | tf_op jit(solution)/shard_map/all_to_all | solution.py:888
  79.9 22.3 %attend_peers.1 = (bf16[2304,768]{1,0:T(8,128)(2,1)}, bf16[12,192,2048]{2,1,0:T(8,128)(2,1)}, bf16[12,64,2048]{2,1,0:T(8,128)(2,1)}, bf16[12,16,2048]{2,1,0:T(8,128)(2,1)}) custom-call(s32[13]{0:T(128)} %concatenate.37.place_ref.refs_0_, ...), custom_call_target="tpu_custom_call", output_to_operand_aliasing={{0}: (15, {}), {1}: (16, {}), {2}: (17, {}), {3}: (18, {})} | custom-call | flops 15099494400 | bytes 30000000 | tf_op jit(solution)/shard_map/attend_peers/pallas_call | solution.py:233
  110.7 4.8 %all-to-all-start.2 = ((f32[4,96,768]{2,1,0:T(8,128)}), f32[4,96,768]{2,1,0:T(8,128)S(1)}, u32[]{:S(2)}, u32[]{:S(2)}) async-start(f32[4,96,768]{2,1,0:T(8,128)} %broadcast_in_dim.79), calls=%async_computation.2 | async-start | bytes 2359296 | tf_op jit(solution)/shard_map/all_to_all | solution.py:888
  115.5 2.7 collective-permute-done.17.refs_13_
  118.1 5.1 %collective-permute-done.19.refs_15_ = f32[3,56,768]{2,1,0:T(8,128)} collective-permute-done((f32[3,56,768]{2,1,0:T(8,128)}, f32[3,56,768]{2,1,0:T(8,128)}, u32[]{:S(2)}, u32[]{:S(2)}) %collective-permute-start.19) | collective-permute-done | bytes 516128 | tf_op jit(solution)/shard_map/ppermute | solution.py:881
  126.2 32.0 %expand.1 = (f32[2048,768]{1,0:T(8,128)}, bf16[4,2048,768]{2,1,0:T(8,128)(2,1)}, bf16[4,2048,768]{2,1,0:T(8,128)(2,1)}, bf16[4,768,768]{2,1,0:T(8,128)(2,1)}, bf16[768,768]{1,0:T(8,128)(2,1)}) custom-call(s32[13]{0:T(128)} %concatenate.37.place_ref.refs_0_, bf16[2048,768]{1,0:T(8,128)(2,1)} %get-tuple-element.88.x_ref.refs_1_.refs_0_, ...), custom_call_target="tpu_custom_call" | custom-call | flops 12079595520 | bytes 40000000 | tf_op jit(solution)/shard_map/expand/pallas_call | solution.py:513
  164.4 35.3 %reduce.15 = (bf16[2048,768]{1,0:T(8,128)(2,1)}, f32[2048,768]{1,0:T(8,128)}, bf16[4,768,768]{2,1,0:T(8,128)(2,1)}, f32[4,192,768]{2,1,0:T(8,128)}, f32[4,192,768]{2,1,0:T(8,128)}, /*index=5*/f32[8,768]{1,0:T(8,128)}) custom-call(s32[13]{0:T(128)} %concatenate.37.place_ref.refs_0_, f32[2048,768]{1,0:T(8,128)} %get-tuple-element.103.refs_1_.sum_ref, ...), custom_call_target="tpu_custom_call" | custom-call | flops 16911433728 | bytes 40000000 | tf_op jit(solution)/shard_map/reduce/pallas_call | solution.py:646
  200.2 6.4 %unshift.1 = bf16[2048,768]{1,0:T(8,128)(2,1)} custom-call(s32[13]{0:T(128)} %concatenate.37.place_ref.refs_0_, bf16[2048,768]{1,0:T(8,128)(2,1)} %get-tuple-element.111.in_ref), custom_call_target="tpu_custom_call" | custom-call | flops 1610612736 | bytes 6000000 | tf_op jit(solution)/shard_map/unshift/pallas_call | solution.py:117
  206.6 2.7 add_bitcast_fusion.1
  212.8 33.6 %back_to_context.1 = (f32[2048,768]{1,0:T(8,128)}, bf16[12,64,2048]{2,1,0:T(8,128)(2,1)}, f32[192,768]{1,0:T(8,128)}, f32[8,768]{1,0:T(8,128)}) custom-call(s32[13]{0:T(128)} %concatenate.37.place_ref.refs_0_, f32[2048,768]{1,0:T(8,128)} %get-tuple-element.103.refs_1_.sum_ref, f32[2048,768]{1,0:T(8,128)} %get-tuple-element.112.g2_ref, ...), custom_call_target="tpu_custom_call" | custom-call | flops 21743271936 | bytes 40000000 | tf_op jit(solution)/shard_map/back_to_context/pallas_call | solution.py:737
  249.7 11.8 %attend_back_own.1 = (bf16[12,192,2048]{2,1,0:T(8,128)(2,1)}, f32[4,112,768]{2,1,0:T(8,128)}, f32[4,112,768]{2,1,0:T(8,128)}) custom-call(s32[13]{0:T(128)} %concatenate.37.place_ref.refs_0_, bf16[12,192,2048]{2,1,0:T(8,128)(2,1)} %get-tuple-element.121.qkv_ref, bf16[12,64,2048]{2,1,0:T(8,128)(2,1)} %get-tuple-element.96.refs_2_.ctx_ref, ...), custom_call_target="tpu_custom_call" | custom-call | flops 5838471168 | bytes 12000000 | tf_op jit(solution)/shard_map/attend_back_own/pallas_call | solution.py:353
  264.9 7.8 %attend_back.2.old_ref = bf16[12,192,2048]{2,1,0:T(8,128)(2,1)} custom-call(s32[13]{0:T(128)} %concatenate.37.place_ref.refs_0_, bf16[12,192,2048]{2,1,0:T(8,128)(2,1)} %get-tuple-element.121.qkv_ref, bf16[12,64,2048]{2,1,0:T(8,128)(2,1)} %get-tuple-element.96.refs_2_.ctx_ref, ...), custom_call_target="tpu_custom_call", output_to_operand_aliasing={{}: (6, {})} | custom-call | flops 4026531840 | bytes 12000000 | tf_op jit(solution)/shard_map/attend_back/pallas_call | solution.py:392
  272.7 2.8 add_bitcast_fusion.8
  279.1 13.1 %attend_back.3.grad_ref = bf16[12,192,2048]{2,1,0:T(8,128)(2,1)} custom-call(s32[13]{0:T(128)} %concatenate.37.place_ref.refs_0_, bf16[12,192,2048]{2,1,0:T(8,128)(2,1)} %get-tuple-element.121.qkv_ref, bf16[12,64,2048]{2,1,0:T(8,128)(2,1)} %get-tuple-element.96.refs_2_.ctx_ref, ...), custom_call_target="tpu_custom_call", output_to_operand_aliasing={{}: (6, {})} | custom-call | flops 8053063680 | bytes 12000000 | tf_op jit(solution)/shard_map/attend_back/pallas_call | solution.py:392
  299.1 16.4 %input_grads.1 = bf16[2048,768]{1,0:T(8,128)(2,1)} custom-call(s32[13]{0:T(128)} %concatenate.37.place_ref.refs_0_, f32[2048,768]{1,0:T(8,128)} %get-tuple-element.146.g1_ref, bf16[12,192,2048]{2,1,0:T(8,128)(2,1)} %attend_back.3.grad_ref, bf16[2304,768]{1,0:T(8,128)(2,1)} %get-tuple-element.147.w_ref), custom_call_target="tpu_custom_call" | custom-call | flops 8858370048 | bytes 20000000 | tf_op jit(solution)/shard_map/input_grads/pallas_call | solution.py:852
  316.6 4.1 %spread.1 = (f32[768,768]{1,0:T(8,128)}, f32[768,768]{1,0:T(8,128)}) custom-call(s32[13]{0:T(128)S(1)} %copy-done, f32[1,192,768]{2,1,0:T(8,128)S(1)} %add_bitcast_fusion.refs_1_, f32[1,192,768]{2,1,0:T(8,128)S(1)} %collective-permute-done.38.refs_2_, f32[1,192,768]{2,1,0:T(8,128)S(1)} %collective-permute-done.31.refs_3_, ...), custom_call_target="tpu_custom_call" | custom-call | bytes 10000000 | tf_op jit(solution)/shard_map/spread/pallas_call | solution.py:787
  (198 shorter events, 68.1 us)
Async XLA Ops:
  3.6 26.9 %collective-permute-start.2 = (f32[80,768]{1,0:T(8,128)S(1)}, f32[80,768]{1,0:T(8,128)S(1)}, u32[]{:S(2)}, u32[]{:S(2)}) collective-permute-start(f32[80,768]{1,0:T(8,128)S(1)} %pad_maximum_fusion.5), channel_id=1, source_target_pairs={{0,3},{1,0},{2,1},{3,2},{4,7},{5,4},{6,5},{7,6},{8,11},{9,8},{10,9... | collective-permute-start | bytes 737288 | tf_op jit(solution)/shard_map/ppermute | solution.py:884
  8.7 21.8 %collective-permute-start.1 = (f32[80,768]{1,0:T(8,128)S(1)}, f32[80,768]{1,0:T(8,128)S(1)}, u32[]{:S(2)}, u32[]{:S(2)}) collective-permute-start(f32[80,768]{1,0:T(8,128)S(1)} %pad_maximum_fusion.5), channel_id=1, source_target_pairs={{0,2},{1,3},{2,0},{3,1},{4,6},{5,7},{6,4},{7,5},{8,10},{9,11},{10,... | collective-permute-start | bytes 737288 | tf_op jit(solution)/shard_map/ppermute | solution.py:884
  8.7 21.8 %collective-permute-start = (f32[80,768]{1,0:T(8,128)S(1)}, f32[80,768]{1,0:T(8,128)S(1)}, u32[]{:S(2)}, u32[]{:S(2)}) collective-permute-start(f32[80,768]{1,0:T(8,128)S(1)} %pad_maximum_fusion.5), channel_id=1, source_target_pairs={{0,1},{1,2},{2,3},{3,0},{4,5},{5,6},{6,7},{7,4},{8,9},{9,10},{10,1... | collective-permute-start | bytes 737288 | tf_op jit(solution)/shard_map/ppermute | solution.py:884
  31.9 38.4 %all-to-all-start = ((f32[4,120,768]{2,1,0:T(8,128)}), f32[4,120,768]{2,1,0:T(8,128)S(1)}, u32[]{:S(2)}, u32[]{:S(2)}) async-start(f32[4,120,768]{2,1,0:T(8,128)} %broadcast_in_dim.77), calls=%async_computation | async-start | bytes 2949120 | tf_op jit(solution)/shard_map/all_to_all | solution.py:888
  37.6 17.0 %collective-permute-start.6 = (f32[3,72,768]{2,1,0:T(8,128)S(1)}, f32[3,72,768]{2,1,0:T(8,128)}, u32[]{:S(2)}, u32[]{:S(2)}) collective-permute-start(f32[3,72,768]{2,1,0:T(8,128)S(1)} %slice.94.refs_5_), channel_id=1, source_target_pairs={{0,16},{4,20},{8,24},{12,28},{16,0},{20,4},{24,8},{28,12},{1,17},{... | collective-permute-start | bytes 1990664 | tf_op jit(solution)/shard_map/ppermute | solution.py:881
  54.6 17.0 %collective-permute-start.3 = (f32[3,72,768]{2,1,0:T(8,128)S(1)}, f32[3,72,768]{2,1,0:T(8,128)}, u32[]{:S(2)}, u32[]{:S(2)}) collective-permute-start(f32[3,72,768]{2,1,0:T(8,128)S(1)} %slice.94.refs_5_), channel_id=1, source_target_pairs={{0,4},{4,0},{8,12},{12,8},{16,20},{20,16},{24,28},{28,24},{1,5},{5... | collective-permute-start | bytes 1990664 | tf_op jit(solution)/shard_map/ppermute | solution.py:881
  54.6 17.0 %collective-permute-start.7 = (f32[3,72,768]{2,1,0:T(8,128)}, f32[3,72,768]{2,1,0:T(8,128)}, u32[]{:S(2)}, u32[]{:S(2)}) collective-permute-start(f32[3,72,768]{2,1,0:T(8,128)} %collective-permute-done.6.refs_9_), channel_id=1, source_target_pairs={{0,4},{4,0},{8,12},{12,8},{16,20},{20,16},{24,28},{28,24},{1,5},{5... | collective-permute-start | bytes 1990664 | tf_op jit(solution)/shard_map/ppermute | solution.py:881
  72.7 36.6 %all-to-all-start.1 = ((f32[4,96,768]{2,1,0:T(8,128)}), f32[4,96,768]{2,1,0:T(8,128)S(1)}, u32[]{:S(2)}, u32[]{:S(2)}) async-start(f32[4,96,768]{2,1,0:T(8,128)} %broadcast_in_dim.78), calls=%async_computation.1 | async-start | bytes 2359296 | tf_op jit(solution)/shard_map/all_to_all | solution.py:888
  76.9 25.7 %collective-permute-start.13 = (f32[3,120,768]{2,1,0:T(8,128)}, f32[3,120,768]{2,1,0:T(8,128)}, u32[]{:S(2)}, u32[]{:S(2)}) collective-permute-start(f32[3,120,768]{2,1,0:T(8,128)} %pad_maximum_fusion.refs_7_), channel_id=1, source_target_pairs={{0,16},{4,20},{8,24},{12,28},{16,0},{20,4},{24,8},{28,12},{1,17},{... | collective-permute-start | bytes 3317768 | tf_op jit(solution)/shard_map/ppermute | solution.py:881
  78.4 25.4 %collective-permute-start.12 = (f32[3,120,768]{2,1,0:T(8,128)}, f32[3,120,768]{2,1,0:T(8,128)}, u32[]{:S(2)}, u32[]{:S(2)}) collective-permute-start(f32[3,120,768]{2,1,0:T(8,128)} %pad_maximum_fusion.refs_7_), channel_id=1, source_target_pairs={{0,8},{4,12},{8,0},{12,4},{16,24},{20,28},{24,16},{28,20},{1,9},{5... | collective-permute-start | bytes 3317768 | tf_op jit(solution)/shard_map/ppermute | solution.py:881
  106.4 18.5 %collective-permute-start.14 = (f32[3,120,768]{2,1,0:T(8,128)}, f32[3,120,768]{2,1,0:T(8,128)}, u32[]{:S(2)}, u32[]{:S(2)}) collective-permute-start(f32[3,120,768]{2,1,0:T(8,128)} %pad_maximum_fusion.refs_7_), channel_id=1, source_target_pairs={{0,4},{4,0},{8,12},{12,8},{16,20},{20,16},{24,28},{28,24},{1,5},{5... | collective-permute-start | bytes 3317768 | tf_op jit(solution)/shard_map/ppermute | solution.py:881
  106.4 19.5 %collective-permute-start.15 = (f32[3,120,768]{2,1,0:T(8,128)}, f32[3,120,768]{2,1,0:T(8,128)}, u32[]{:S(2)}, u32[]{:S(2)}) collective-permute-start(f32[3,120,768]{2,1,0:T(8,128)} %collective-permute-done.12.refs_9_), channel_id=1, source_target_pairs={{0,4},{4,0},{8,12},{12,8},{16,20},{20,16},{24,28},{28,24},{1,5},{5... | collective-permute-start | bytes 3317768 | tf_op jit(solution)/shard_map/ppermute | solution.py:881
  107.0 19.0 %collective-permute-start.16 = (f32[3,120,768]{2,1,0:T(8,128)}, f32[3,120,768]{2,1,0:T(8,128)}, u32[]{:S(2)}, u32[]{:S(2)}) collective-permute-start(f32[3,120,768]{2,1,0:T(8,128)} %collective-permute-done.13.refs_11_), channel_id=1, source_target_pairs={{0,4},{4,0},{8,12},{12,8},{16,20},{20,16},{24,28},{28,24},{1,5},{5... | collective-permute-start | bytes 3317768 | tf_op jit(solution)/shard_map/ppermute | solution.py:881
  110.7 47.6 %all-to-all-start.2 = ((f32[4,96,768]{2,1,0:T(8,128)}), f32[4,96,768]{2,1,0:T(8,128)S(1)}, u32[]{:S(2)}, u32[]{:S(2)}) async-start(f32[4,96,768]{2,1,0:T(8,128)} %broadcast_in_dim.79), calls=%async_computation.2 | async-start | bytes 2359296 | tf_op jit(solution)/shard_map/all_to_all | solution.py:888
  124.9 33.5 %collective-permute-start.23 = (f32[3,96,768]{2,1,0:T(8,128)S(1)}, f32[3,96,768]{2,1,0:T(8,128)S(1)}, u32[]{:S(2)}, u32[]{:S(2)}) collective-permute-start(f32[3,96,768]{2,1,0:T(8,128)S(1)} %pad_maximum_fusion.2.refs_7_), channel_id=1, source_target_pairs={{0,16},{4,20},{8,24},{12,28},{16,0},{20,4},{24,8},{28,12},{1,17},{... | collective-permute-start | bytes 2654216 | tf_op jit(solution)/shard_map/ppermute | solution.py:881
  125.4 33.0 %collective-permute-start.22 = (f32[3,96,768]{2,1,0:T(8,128)S(1)}, f32[3,96,768]{2,1,0:T(8,128)}, u32[]{:S(2)}, u32[]{:S(2)}) collective-permute-start(f32[3,96,768]{2,1,0:T(8,128)S(1)} %pad_maximum_fusion.2.refs_7_), channel_id=1, source_target_pairs={{0,8},{4,12},{8,0},{12,4},{16,24},{20,28},{24,16},{28,20},{1,9},{5... | collective-permute-start | bytes 2654216 | tf_op jit(solution)/shard_map/ppermute | solution.py:881
  126.0 33.4 %collective-permute-start.21 = (f32[3,96,768]{2,1,0:T(8,128)S(1)}, f32[3,96,768]{2,1,0:T(8,128)}, u32[]{:S(2)}, u32[]{:S(2)}) collective-permute-start(f32[3,96,768]{2,1,0:T(8,128)S(1)} %pad_maximum_fusion.2.refs_7_), channel_id=1, source_target_pairs={{0,4},{4,0},{8,12},{12,8},{16,20},{20,16},{24,28},{28,24},{1,5},{5... | collective-permute-start | bytes 2654216 | tf_op jit(solution)/shard_map/ppermute | solution.py:881
  209.3 37.1 %collective-permute-start.30 = (f32[192,768]{1,0:T(8,128)}, f32[192,768]{1,0:T(8,128)S(1)}, u32[]{:S(2)}, u32[]{:S(2)}) collective-permute-start(f32[192,768]{1,0:T(8,128)} %get-tuple-element.166), channel_id=1, source_target_pairs={{0,24},{4,28},{8,16},{12,20},{16,8},{20,12},{24,0},{28,4},{1,25},{... | collective-permute-start | bytes 1769480 | tf_op jit(solution)/shard_map/ppermute | solution.py:881
  211.7 34.7 %collective-permute-start.29 = (f32[192,768]{1,0:T(8,128)S(1)}, f32[192,768]{1,0:T(8,128)S(1)}, u32[]{:S(2)}, u32[]{:S(2)}) collective-permute-start(f32[192,768]{1,0:T(8,128)S(1)} %get-tuple-element.167), channel_id=1, source_target_pairs={{0,16},{4,20},{8,24},{12,28},{16,0},{20,4},{24,8},{28,12},{1,17},{... | collective-permute-start | bytes 1769480 | tf_op jit(solution)/shard_map/ppermute | solution.py:881
  212.2 34.2 %collective-permute-start.28 = (f32[192,768]{1,0:T(8,128)S(1)}, f32[192,768]{1,0:T(8,128)S(1)}, u32[]{:S(2)}, u32[]{:S(2)}) collective-permute-start(f32[192,768]{1,0:T(8,128)S(1)} %get-tuple-element.168), channel_id=1, source_target_pairs={{0,8},{4,12},{8,0},{12,4},{16,24},{20,28},{24,16},{28,20},{1,9},{5... | collective-permute-start | bytes 1769480 | tf_op jit(solution)/shard_map/ppermute | solution.py:881
  279.1 20.0 %collective-permute-start.41 = (f32[1,192,768]{2,1,0:T(8,128)S(1)}, f32[1,192,768]{2,1,0:T(8,128)}, u32[]{:S(2)}, u32[]{:S(2)}) collective-permute-start(f32[1,192,768]{2,1,0:T(8,128)S(1)} %collective-permute-done.37.refs_7_), channel_id=1, source_target_pairs={{0,4},{4,0},{8,12},{12,8},{16,20},{20,16},{24,28},{28,24},{1,5},{5... | collective-permute-start | bytes 1769480 | tf_op jit(solution)/shard_map/ppermute | solution.py:881
  295.5 19.9 %collective-permute-start.44 = (f32[112,768]{1,0:T(8,128)S(1)}, f32[112,768]{1,0:T(8,128)S(1)}, u32[]{:S(2)}, u32[]{:S(2)}) collective-permute-start(f32[112,768]{1,0:T(8,128)S(1)} %add_add_fusion.refs_1_), channel_id=1, source_target_pairs={{0,24},{4,28},{8,16},{12,20},{16,8},{20,12},{24,0},{28,4},{1,25},{... | collective-permute-start | bytes 1032200 | tf_op jit(solution)/shard_map/ppermute | solution.py:881
  297.1 18.4 %collective-permute-start.43 = (f32[112,768]{1,0:T(8,128)S(1)}, f32[112,768]{1,0:T(8,128)S(1)}, u32[]{:S(2)}, u32[]{:S(2)}) collective-permute-start(f32[112,768]{1,0:T(8,128)S(1)} %add_add_fusion.refs_1_), channel_id=1, source_target_pairs={{0,16},{4,20},{8,24},{12,28},{16,0},{20,4},{24,8},{28,12},{1,17},{... | collective-permute-start | bytes 1032200 | tf_op jit(solution)/shard_map/ppermute | solution.py:881
  298.3 17.2 %collective-permute-start.42 = (f32[112,768]{1,0:T(8,128)S(1)}, f32[112,768]{1,0:T(8,128)S(1)}, u32[]{:S(2)}, u32[]{:S(2)}) collective-permute-start(f32[112,768]{1,0:T(8,128)S(1)} %add_add_fusion.refs_1_), channel_id=1, source_target_pairs={{0,8},{4,12},{8,0},{12,4},{16,24},{20,28},{24,16},{28,20},{1,9},{5... | collective-permute-start | bytes 1032200 | tf_op jit(solution)/shard_map/ppermute | solution.py:881
  (49 other events, 527.0 us)
